TPU v7x, 128 devices: a whole 4x4x4 slice. The times are simulated.
128 devices in a mesh: loop: 8 (over z_lo, y), wide: 16 (over z_hi, x, core).
Axes of the slice: x: 4, y: 4, z: 4 (z_hi: 2, z_lo: 2; z = z_hi * 2 + z_lo), core: 2. Of those that a mesh axis runs over, the one named last changes fastest.
Arguments:
- feats: bfloat16 [16, 2048, 256], P('wide', 'loop'), may hold values from -6 to 6
- w_first: bfloat16 [256, 1024], replicated, may hold values from -0.375 to 0.375
- w_second: bfloat16 [1024, 256], replicated, may hold values from -0.1875 to 0.1875
- cotangent: bfloat16 [16, 2048, 256], P('wide', 'loop'), may hold values from -0.078125 to 0.078125
- block_values: bfloat16 [8, 16, 80, 64, 64], P('loop', 'wide'), may hold values from -0.25 to 0.25
- row_ptr: int32 [8, 16, 33], P('loop', 'wide'), may hold values from 0 to 80, as said below
- col_idx: int32 [8, 16, 80], P('loop', 'wide'), may hold values from 0 to 63
Outputs:
- propagated: bfloat16 [16, 2048, 256], P('wide', 'loop')
- grad_first: float32 [256, 1024], P('wide')
- grad_second: float32 [1024, 256], P('wide')
Inputs may be any that keep to these rules, and one draw needn't show every extreme that they name: In each tile row_ptr starts at 0, never falls, and its last entry (the tile's live blocks) is at most 80; in every draw some tile has exactly 80 live blocks. `col_idx`: entries of empty slots are ignored.
All inputs are finite; a program needn't handle non-finite values.
Results may differ from a plain program's by a relative error of at most 0.02.
Values may be sent and summed in bfloat16 or wider, within the bound.
No kernel may reach another device: no remote copies, remote signals or barrier semaphores. Data moves between devices by JAX's collectives and lax.ppermute only.
A program may use at most 128 MiB of HBM per device.

v0:
```python
import jax
import jax.numpy as jnp
from jax import lax
from jax.sharding import PartitionSpec as P

STEPS = 3


ALPHA = 0.1


def slot_layout(pointers, slot_total):
    slot_ids = jnp.arange(slot_total, dtype=jnp.int32)
    slot_row = jnp.sum((pointers[1:, None] <= slot_ids).astype(jnp.int32), axis=0)
    slot_live = (slot_ids < pointers[-1:]).astype(jnp.float32)
    return (jnp.minimum(slot_row, pointers.shape[0] - 2), slot_live)


def silu_slope(value):
    sigma = jax.nn.sigmoid(value)
    return sigma * (1.0 + value * (1.0 - sigma))


def block_sums(slot_target, products, first_row, row_count, block_size):
    targets = first_row // block_size + jnp.arange(row_count // block_size)
    one_hot = (slot_target[:, None] == targets[None, :]).astype(jnp.float32)
    landed = jnp.einsum("sr,sid->rid", one_hot, products, precision=lax.Precision.HIGHEST)
    return landed.reshape(row_count, products.shape[-1])


def propagate(current, teleport, tile_values, slot_row, slot_live, slot_col):
    block_size = tile_values.shape[-1]
    features = current.shape[-1]
    columns = lax.all_gather(current, "wide", axis=0, tiled=True)
    picked = columns.reshape(-1, block_size, features)[slot_col]
    products = (
        jnp.einsum("sij,sjd->sid", tile_values, picked, preferred_element_type=jnp.float32)
        * slot_live[:, None, None]
    )
    summed = lax.psum_scatter(
        block_sums(
            slot_row, products, jnp.int32(0), current.shape[0] * lax.axis_size("loop"), block_size
        ),
        "loop",
        scatter_dimension=0,
        tiled=True,
    )
    return ((1.0 - ALPHA) * summed + ALPHA * teleport.astype(jnp.float32)).astype(jnp.bfloat16)


def pull_back(adjoint_now, tile_values, slot_row, slot_live, slot_col):
    block_size = tile_values.shape[-1]
    features = adjoint_now.shape[-1]
    own_rows = adjoint_now.shape[0]
    whole_rows = lax.all_gather(adjoint_now, "loop", axis=0, tiled=True)
    picked = whole_rows.reshape(-1, block_size, features)[slot_row]
    products = (
        jnp.einsum("sij,sid->sjd", tile_values, picked, preferred_element_type=jnp.float32)
        * slot_live[:, None, None]
    )
    summed_all = lax.psum(
        block_sums(slot_col, products, 0, lax.axis_size("wide") * own_rows, block_size), "wide"
    )
    summed = lax.dynamic_slice_in_dim(summed_all, lax.axis_index("wide") * own_rows, own_rows, 0)
    return ((1.0 - ALPHA) * summed).astype(jnp.bfloat16)


def body(feats, w_first, w_second, cotangent, block_values, row_ptr, col_idx):
    tile_values = block_values[0, 0]
    slot_row, slot_live = slot_layout(row_ptr[0, 0], tile_values.shape[0])
    slot_col = col_idx[0, 0]
    flat_feats = feats[0]
    pre_act = jnp.dot(flat_feats, w_first, preferred_element_type=jnp.float32)
    hidden = jax.nn.silu(pre_act).astype(jnp.bfloat16)
    teleport = jnp.dot(hidden, w_second, preferred_element_type=jnp.float32).astype(jnp.bfloat16)
    current = teleport
    for _ in range(STEPS):
        current = propagate(current, teleport, tile_values, slot_row, slot_live, slot_col)
    adjoint_now = cotangent[0]
    collected = adjoint_now.astype(jnp.float32)
    for repeat in range(STEPS):
        adjoint_now = pull_back(adjoint_now, tile_values, slot_row, slot_live, slot_col)
        if repeat < STEPS - 1:
            collected = collected + adjoint_now.astype(jnp.float32)
    grad_teleport = (ALPHA * collected + adjoint_now.astype(jnp.float32)).astype(jnp.bfloat16)
    grad_hidden = lax.dot_general(
        grad_teleport, w_second, (((1,), (1,)), ((), ())), preferred_element_type=jnp.float32
    )
    grad_pre = (grad_hidden * silu_slope(pre_act)).astype(jnp.bfloat16)
    contract_items = (((0,), (0,)), ((), ()))
    piece = flat_feats
    first_part = lax.psum_scatter(
        lax.dot_general(piece, grad_pre, contract_items, preferred_element_type=jnp.float32).astype(
            jnp.bfloat16
        ),
        "wide",
        scatter_dimension=0,
        tiled=True,
    )
    piece = hidden
    second_part = lax.psum_scatter(
        lax.dot_general(
            piece, grad_teleport, contract_items, preferred_element_type=jnp.float32
        ).astype(jnp.bfloat16),
        "wide",
        scatter_dimension=0,
        tiled=True,
    )
    grad_first, grad_second = (
        lax.psum(first_part, "loop").astype(jnp.float32),
        lax.psum(second_part, "loop").astype(jnp.float32),
    )
    return (current[None], grad_first, grad_second)


def solution(mesh):
    return jax.shard_map(
        body,
        mesh=mesh,
        in_specs=(
            P("wide", "loop", None),
            P(),
            P(),
            P("wide", "loop", None),
            P("loop", "wide", None, None, None),
            P("loop", "wide", None),
            P("loop", "wide", None),
        ),
        out_specs=(P("wide", "loop", None), P("wide", None), P("wide", None)),
        check_vma=False,
    )
```

profile of v0, /device:TPU:0, one launch (start us, length us, event | category | flops | bytes accessed | tf_op | source)
XLA Modules:
  0.0 1107.6 jit_solution(12611769224708004962)
XLA Ops:
  8.0 3.6 copy.33
  14.3 36.8 %all-gather.18.cloned.1.call-done = bf16[1,2048,256]{2,1,0:T(8,128)(2,1)} async-done(((bf16[1,256,256]{2,1,0:T(8,128)(2,1)}), bf16[1,2048,256]{2,1,0:T(8,128)(2,1)}) %all-gather.18.cloned.1.call-update) | async-done | bytes 1048592 | tf_op jit(solution)/shard_map/all_gather | solution.py:55
  51.2 3.6 gather_fusion.3
  54.8 2.6 multiply_bitcast_fusion.2
  57.4 5.8 fusion.4
  63.2 4.4 copy.35
  67.7 149.5 %all-reduce.6.cloned.1.call-done = f32[4096,256]{1,0:T(8,128)} async-done(((f32[4096,256]{1,0:T(8,128)}), f32[4096,256]{1,0:T(8,128)}) %all-reduce.6.cloned.1.call-update) | async-done | bytes 4194320 | tf_op jit(solution)/shard_map/psum | solution.py:61
  217.2 1.6 multiply_convert_fusion.3
  221.5 37.1 %all-gather.14.cloned.1.call-done = bf16[2048,256]{1,0:T(8,128)(2,1)} async-done(((bf16[256,256]{1,0:T(8,128)(2,1)}), bf16[2048,256]{1,0:T(8,128)(2,1)}) %all-gather.14.cloned.1.call-update) | async-done | bytes 1048592 | tf_op jit(solution)/shard_map/all_gather | solution.py:55
  258.6 3.6 gather_fusion.4
  262.2 2.6 multiply_bitcast_fusion.1
  264.8 5.8 fusion.2
  270.6 4.4 copy.38
  275.5 33.4 %all-gather.8.cloned.1.call-done = bf16[4096,256]{1,0:T(8,128)(2,1)} async-done(((bf16[256,256]{1,0:T(8,128)(2,1)}), bf16[4096,256]{1,0:T(8,128)(2,1)}) %all-gather.8.cloned.1.call-update) | async-done | bytes 2097168 | tf_op jit(solution)/shard_map/all_gather | solution.py:34
  308.9 4.0 gather_fusion
  312.8 2.7 multiply_bitcast_fusion.5
  315.6 5.0 fusion.10
  320.6 2.5 copy.26
  323.2 137.1 %all-reduce.8.cloned.1.call-done = f32[4096,256]{1,0:T(8,128)} async-done(((f32[4096,256]{1,0:T(8,128)}), f32[4096,256]{1,0:T(8,128)}) %all-reduce.8.cloned.1.call-update) | async-done | bytes 4194320 | tf_op jit(solution)/shard_map/psum | solution.py:61
  460.3 1.6 multiply_convert_fusion.2
  462.0 44.1 %reduce-scatter.8.cloned.1.call-done = f32[256,256]{1,0:T(8,128)} async-done(((f32[2048,256]{1,0:T(8,128)}), f32[256,256]{1,0:T(8,128)}) %reduce-scatter.8.cloned.1.call-update) | async-done | bytes 262160 | tf_op jit(solution)/shard_map/reduce_scatter | solution.py:40
  506.2 1.6 add_convert_fusion.2
  508.1 37.2 %all-gather.16.cloned.1.call-done = bf16[2048,256]{1,0:T(8,128)(2,1)} async-done(((bf16[256,256]{1,0:T(8,128)(2,1)}), bf16[2048,256]{1,0:T(8,128)(2,1)}) %all-gather.16.cloned.1.call-update) | async-done | bytes 1048592 | tf_op jit(solution)/shard_map/all_gather | solution.py:55
  545.2 3.7 gather_fusion.5
  548.9 2.6 multiply_bitcast_fusion
  551.5 5.8 fusion
  557.3 4.4 copy.41
  561.9 33.7 %all-gather.10.cloned.1.call-done = bf16[4096,256]{1,0:T(8,128)(2,1)} async-done(((bf16[256,256]{1,0:T(8,128)(2,1)}), bf16[4096,256]{1,0:T(8,128)(2,1)}) %all-gather.10.cloned.1.call-update) | async-done | bytes 2097168 | tf_op jit(solution)/shard_map/all_gather | solution.py:34
  595.7 4.0 gather_fusion.1
  599.6 2.7 multiply_bitcast_fusion.4
  602.4 5.0 fusion.8
  607.5 2.5 copy.29
  610.1 137.2 %all-reduce.10.cloned.1.call-done = f32[4096,256]{1,0:T(8,128)} async-done(((f32[4096,256]{1,0:T(8,128)}), f32[4096,256]{1,0:T(8,128)}) %all-reduce.10.cloned.1.call-update) | async-done | bytes 4194320 | tf_op jit(solution)/shard_map/psum | solution.py:61
  748.5 2.0 fusion.13
  752.8 40.3 %reduce-scatter.10.cloned.1.call-done = f32[256,256]{1,0:T(8,128)} async-done(((f32[2048,256]{1,0:T(8,128)}), f32[256,256]{1,0:T(8,128)}) %reduce-scatter.10.cloned.1.call-update) | async-done | bytes 262160 | tf_op jit(solution)/shard_map/reduce_scatter | solution.py:40
  793.1 1.6 add_convert_fusion.1
  794.8 65.8 %reduce-scatter.16.cloned.1.call-done = bf16[16,1024]{1,0:T(8,128)(2,1)} async-done(((bf16[256,1024]{1,0:T(8,128)(2,1)}), bf16[16,1024]{1,0:T(8,128)(2,1)}) %reduce-scatter.16.cloned.1.call-update) | async-done | bytes 32784
  860.7 1.6 copy.44
  862.3 66.9 %reduce-scatter.14.cloned.1.call-done = bf16[64,256]{1,0:T(8,128)(2,1)} async-done(((bf16[1024,256]{1,0:T(8,128)(2,1)}), bf16[64,256]{1,0:T(8,128)(2,1)}) %reduce-scatter.14.cloned.1.call-update) | async-done | bytes 32784 | tf_op jit(solution)/shard_map/reduce_scatter | solution.py:101
  929.5 50.1 %all-gather.12.cloned.1.call-done = bf16[4096,256]{1,0:T(8,128)(2,1)} async-done(((bf16[256,256]{1,0:T(8,128)(2,1)}), bf16[4096,256]{1,0:T(8,128)(2,1)}) %all-gather.12.cloned.1.call-update) | async-done | bytes 2097168 | tf_op jit(solution)/shard_map/all_gather | solution.py:34
  979.6 4.0 gather_fusion.2
  983.6 2.7 multiply_bitcast_fusion.3
  986.3 5.0 fusion.6
  991.4 2.6 copy.32
  993.9 61.1 %all-reduce.12.cloned.1.call-done = (bf16[16,1024]{0,1:T(8,128)(2,1)}, bf16[64,256]{1,0:T(8,128)(2,1)}) async-done(((bf16[16,1024]{0,1:T(8,128)(2,1)}, bf16[64,256]{1,0:T(8,128)(2,1)}), (bf16[16,1024]{0,1:T(8,128)(2,1)}, bf16[64,256]{1,0:T(8,128)(2,1)})) %all-reduce.12.cloned.1.call-update) | async-done | bytes 65552 | tf_op jit(solution)/shard_map/psum | solution.py:110
  1056.5 1.7 copy.42
  1058.2 40.8 %reduce-scatter.12.cloned.1.call-done = f32[256,256]{1,0:T(8,128)} async-done(((f32[2048,256]{1,0:T(8,128)}), f32[256,256]{1,0:T(8,128)}) %reduce-scatter.12.cloned.1.call-update) | async-done | bytes 262160 | tf_op jit(solution)/shard_map/reduce_scatter | solution.py:40
  1099.0 1.6 fusion.23
  (59 shorter events, 12.6 us)
Async XLA Ops:
  7.2 211.7 %copy-start = (bf16[256,1024]{1,0:T(8,128)(2,1)S(1)}, bf16[256,1024]{1,0:T(8,128)(2,1)}, u32[]{:S(2)}) copy-start(bf16[256,1024]{1,0:T(8,128)(2,1)} %param.8) | copy-start | bytes 1572868
  7.2 44.0 %all-gather.18.cloned.1.call-start = ((), (), s32[]{:S(2)}) async-start(), calls=%async_computation.17 | async-start | bytes 1179648 | tf_op jit(solution)/shard_map/all_gather | solution.py:55
  7.9 209.2 %all-reduce.6.cloned.1.call-start = ((), (), s32[]{:S(2)}) async-start(), calls=%async_computation.11 | async-start | bytes 8388608 | tf_op jit(solution)/shard_map/psum | solution.py:61
  54.8 2.6 copy-start.5
  67.6 151.3 %copy-start.6 = (bf16[1,256,256]{2,1,0:T(8,128)(2,1)S(1)}, bf16[1,256,256]{2,1,0:T(8,128)(2,1)}, u32[]{:S(2)}) copy-start(bf16[1,256,256]{2,1,0:T(8,128)(2,1)} %param.7) | copy-start | bytes 393220
  67.6 190.9 %all-gather.14.cloned.1.call-start = ((), (), s32[]{:S(2)}) async-start(), calls=%async_computation.12 | async-start | bytes 1179648 | tf_op jit(solution)/shard_map/all_gather | solution.py:55
  218.8 1.4 copy-start.3
  218.8 90.1 %all-gather.8.cloned.1.call-start = ((), (), s32[]{:S(2)}) async-start(), calls=%async_computation.5 | async-start | bytes 2228224 | tf_op jit(solution)/shard_map/all_gather | solution.py:34
  221.2 239.1 %all-reduce.8.cloned.1.call-start = ((), (), s32[]{:S(2)}) async-start(), calls=%async_computation.13 | async-start | bytes 8388608 | tf_op jit(solution)/shard_map/psum | solution.py:61
  275.0 231.2 %reduce-scatter.8.cloned.1.call-start = ((), (), s32[]{:S(2)}) async-start(), calls=%async_computation.6 | async-start | bytes 2359296 | tf_op jit(solution)/shard_map/reduce_scatter | solution.py:40
  320.6 185.6 %copy-start.2 = (bf16[256,256]{1,0:T(8,128)(2,1)S(1)}, bf16[256,256]{1,0:T(8,128)(2,1)}, u32[]{:S(2)}) copy-start(bf16[256,256]{1,0:T(8,128)(2,1)} %convolution_convert_fusion.2) | copy-start | bytes 393220
  323.2 222.1 %all-gather.16.cloned.1.call-start = ((), (), s32[]{:S(2)}) async-start(), calls=%async_computation.14 | async-start | bytes 1179648 | tf_op jit(solution)/shard_map/all_gather | solution.py:55
  462.0 133.7 %all-gather.10.cloned.1.call-start = ((), (), s32[]{:S(2)}) async-start(), calls=%async_computation.7 | async-start | bytes 2228224 | tf_op jit(solution)/shard_map/all_gather | solution.py:34
  507.8 239.5 %all-reduce.10.cloned.1.call-start = ((), (), s32[]{:S(2)}) async-start(), calls=%async_computation.15 | async-start | bytes 8388608 | tf_op jit(solution)/shard_map/psum | solution.py:61
  561.7 231.4 %reduce-scatter.10.cloned.1.call-start = ((), (), s32[]{:S(2)}) async-start(), calls=%async_computation.8 | async-start | bytes 2359296 | tf_op jit(solution)/shard_map/reduce_scatter | solution.py:40
  607.4 139.9 %copy-start.4 = (bf16[1,256,256]{2,1,0:T(8,128)(2,1)S(1)}, bf16[1,256,256]{2,1,0:T(8,128)(2,1)}, u32[]{:S(2)}) copy-start(bf16[1,256,256]{2,1,0:T(8,128)(2,1)} %param.10) | copy-start | bytes 393220
  610.0 250.6 %reduce-scatter.16.cloned.1.call-start = ((), (), s32[]{:S(2)}) async-start(), calls=%async_computation.18 | async-start | bytes 557056
  751.5 177.6 %reduce-scatter.14.cloned.1.call-start = ((), (), s32[]{:S(2)}) async-start(), calls=%async_computation.16 | async-start | bytes 557056 | tf_op jit(solution)/shard_map/reduce_scatter | solution.py:101
  752.7 226.8 %all-gather.12.cloned.1.call-start = ((), (), s32[]{:S(2)}) async-start(), calls=%async_computation.9 | async-start | bytes 2228224 | tf_op jit(solution)/shard_map/all_gather | solution.py:34
  794.8 260.3 %all-reduce.12.cloned.1.call-start = ((), (), s32[]{:S(2)}) async-start(), calls=%async_computation.19 | async-start | bytes 589824 | tf_op jit(solution)/shard_map/psum | solution.py:110
  929.2 169.8 %reduce-scatter.12.cloned.1.call-start = ((), (), s32[]{:S(2)}) async-start(), calls=%async_computation.10 | async-start | bytes 2359296 | tf_op jit(solution)/shard_map/reduce_scatter | solution.py:40
  986.3 114.3 %copy-start.1 = (bf16[256,1024]{1,0:T(8,128)(2,1)S(1)}, bf16[256,1024]{1,0:T(8,128)(2,1)}, u32[]{:S(2)}) copy-start(bf16[256,1024]{1,0:T(8,128)(2,1)} %param.8) | copy-start | bytes 1572868
Sparse Core Ops, SparseCore 0:
  9.7 41.4 all-gather.17
  67.8 149.3 all-reduce.5
  218.9 39.6 all-gather.13
  261.4 47.3 all-gather.7
  311.2 149.0 all-reduce.7
  462.6 43.5 reduce-scatter.7
  507.8 37.3 all-gather.15
  548.2 47.3 all-gather.9
  598.2 149.0 all-reduce.9
  749.6 43.5 reduce-scatter.9
  796.9 63.7 reduce-scatter.15
  864.7 64.3 reduce-scatter.13
  932.1 47.3 all-gather.11
  982.0 73.0 all-reduce.11
  1057.5 41.4 reduce-scatter.11
where the time goes:
time: 1120 us; the launch traced here: 1110 us
  waiting for transfers between devices  972 us (87%)
  matrix products  53.8 us (5%)
  local copies, waits for them, and re-layouts  53.6 us (5%)
  between operations  14.6 us (1%)
  other arithmetic  11.5 us (1%)
    psum x3, waiting for transfers between devices, pull_back(): lax.psum(block_sums(slot_col, products, 0, lax.axis_size('wide') * own_ro...  424 us
    reduce_scatter x3, waiting for transfers between devices, propagate(): lax.psum_scatter(block_sums(slot_row, products, jnp.int32(0), current.sha...  125 us
    all_gather x3, waiting for transfers between devices, propagate(): columns = lax.all_gather(current, 'wide', axis=0, tiled=True)  117 us
    all_gather x3, waiting for transfers between devices, pull_back(): whole_rows = lax.all_gather(adjoint_now, 'loop', axis=0, tiled=True)  111 us
    reduce_scatter x1, waiting for transfers between devices, body(): lax.psum_scatter(lax.dot_general(piece, grad_teleport, contract_items, pr...  66.9 us
    unnamed x16, waiting for transfers between devices  66.7 us
    psum x1, waiting for transfers between devices, body(): lax.psum(first_part, 'loop').astype(jnp.float32)  61.1 us
    dot_general x6, matrix products, block_sums(): jnp.einsum('sr,sid->rid', one_hot, products, precision=lax.Precision.HIGH...  32.4 us
  transfers between devices with their start and end apart: 15, of which 15 were waited for; matrix products, arithmetic and copies ran while one was open for 9% of the time, Pallas kernels for 0%

commit v1 on v0

v1 whole, which is shorter than its diff:
```python
import functools

import jax
import jax.numpy as jnp
import numpy as np
from jax import lax
from jax.experimental import pallas as pl
from jax.experimental.pallas import tpu as pltpu
from jax.sharding import Mesh
from jax.sharding import PartitionSpec as P

STEPS = 3
ALPHA = 0.1
AXES = ("zl", "y", "zh", "x", "c")
SIZES = (2, 4, 2, 4, 2)
LOOP = ("zl", "y")
WIDE = ("zh", "x", "c")
BLK = 64
DIM = 256
ITEMS = 256
PIECE = 2 * ITEMS
PAIR = 2 * PIECE
GRAPH = 4 * PAIR
SLOTS = 80
HALF = SLOTS // 2


def permutation(move):
    pairs = []
    for source in range(int(np.prod(SIZES))):
        place = dict(zip(AXES, np.unravel_index(source, SIZES)))
        place = {name: int(value) for name, value in place.items()}
        place.update(move(place))
        pairs.append((source, int(np.ravel_multi_index([place[name] for name in AXES], SIZES))))
    return pairs


def send(value, move):
    return lax.ppermute(value, AXES, permutation(move))


def core_move(place):
    return {"c": 1 - place["c"]}


def gather_z(place):
    return {"zl": 1 - place["zl"]} if place["c"] else {"zh": 1 - place["zh"]}


def scatter_z(place):
    return {"zh": 1 - place["zh"]} if place["c"] else {"zl": 1 - place["zl"]}


def gather_ring(step, place):
    return {"y": (place["y"] + step) % 4} if place["c"] else {"x": (place["x"] + step) % 4}


def scatter_ring(step, place):
    return {"x": (place["x"] + step) % 4} if place["c"] else {"y": (place["y"] + step) % 4}


def product_kernel(meta, values, part0, part1, part2, part3, out0, out1, out2, out3, gathered, sums, sems):
    copies = [
        pltpu.make_async_copy(part, gathered.at[pl.ds(index * PAIR, PAIR)], sems.at[index])
        for index, part in enumerate((part0, part1, part2, part3))
    ]
    for copy in copies:
        copy.start()
    sums[...] = jnp.zeros_like(sums)
    for copy in copies:
        copy.wait()

    def run(tile, half):
        live = meta[2, tile * SLOTS]
        count = jnp.clip(live - half * HALF, 0, HALF)

        def four(group, carry):
            products = []
            for lane in range(4):
                slot = group * 4 + lane
                source = pl.multiple_of(meta[0, tile * SLOTS + half * HALF + slot], BLK)
                block = values[tile * HALF + slot][:, half * BLK : (half + 1) * BLK]
                products.append(
                    jnp.dot(block, gathered[pl.ds(source, BLK), :], preferred_element_type=jnp.float32)
                )
            for lane in range(4):
                target = pl.multiple_of(meta[1, tile * SLOTS + half * HALF + group * 4 + lane], BLK)
                sums[pl.ds(target, BLK), :] += products[lane]
            return carry

        lax.fori_loop(0, (count + 3) // 4, four, 0)

    for tile in range(2):
        for half in range(2):
            run(tile, half)
    for index, out in enumerate((out0, out1, out2, out3)):
        out[...] = sums[index * PAIR : (index + 1) * PAIR, :].astype(out.dtype)


def block_product(meta, values, parts):
    piece = jax.ShapeDtypeStruct((PAIR, DIM), jnp.bfloat16)
    return pl.pallas_call(
        product_kernel,
        out_shape=(piece,) * 4,
        in_specs=[
            pl.BlockSpec(memory_space=pltpu.SMEM),
            pl.BlockSpec(memory_space=pltpu.VMEM),
        ]
        + [pl.BlockSpec(memory_space=pl.ANY)] * 4,
        out_specs=(pl.BlockSpec(memory_space=pltpu.VMEM),) * 4,
        scratch_shapes=[
            pltpu.VMEM((GRAPH, DIM), jnp.bfloat16),
            pltpu.VMEM((GRAPH + BLK, DIM), jnp.float32),
            pltpu.SemaphoreType.DMA((4,)),
        ],
        compiler_params=pltpu.CompilerParams(vmem_limit_bytes=40 * 2**20),
        name="block_product",
    )(meta, values, *parts)


def slot_tables(pointers, columns, zl, y, zh, x, core):
    slot_ids = jnp.arange(SLOTS, dtype=jnp.int32)
    rows = jnp.sum((pointers[:, 1:, None] <= slot_ids).astype(jnp.int32), axis=1)
    rows = jnp.minimum(rows, pointers.shape[1] - 2)
    live_count = pointers[:, -1:]
    live = slot_ids[None, :] < live_count
    tile = jnp.arange(2, dtype=jnp.int32)[:, None]
    row_l = rows // 4
    row_zl, row_y = row_l // 4, row_l % 4
    row_base = (row_zl ^ zl) * PIECE + tile * ITEMS + (rows % 4) * BLK
    col_w = columns // 4
    col_zh, col_x, col_c = col_w // 8, (col_w // 2) % 4, col_w % 2
    col_base = (col_zh ^ zh) * PIECE + col_c * ITEMS + (columns % 4) * BLK
    forward_source = ((x - col_x) % 4) * PAIR + col_base
    forward_target = ((row_y - y) % 4) * PAIR + row_base
    adjoint_source = ((y - row_y) % 4) * PAIR + row_base
    adjoint_target = ((col_x - x) % 4) * PAIR + col_base
    source = jnp.where(core == 0, forward_source, adjoint_source)
    target = jnp.where(core == 0, forward_target, adjoint_target)
    source = jnp.where(live, source, 0)
    target = jnp.where(live, target, GRAPH)
    counts = jnp.broadcast_to(live_count, source.shape)
    return jnp.stack([source, target, counts]).reshape(3, 2 * SLOTS)


def silu_slope(value):
    sigma = jax.nn.sigmoid(value)
    return sigma * (1.0 + value * (1.0 - sigma))


def by_tile(own, other, core):
    return jnp.where(core == 0, jnp.stack([own, other]), jnp.stack([other, own]))


def body(feats, w_first, w_second, cotangent, block_values, row_ptr, col_idx):
    f32, bf16 = jnp.float32, jnp.bfloat16
    zl, y, zh, x, core = (lax.axis_index(name) for name in AXES)
    own_feats, own_cot = feats[0], cotangent[0]
    other = send(jnp.concatenate([own_feats, own_cot]), core_move)
    tile = block_values[0, 0]
    packed = jnp.concatenate([tile[:HALF], tile[HALF:]], axis=-1)
    other_packed = send(packed, core_move)
    table = jnp.concatenate([row_ptr[0, 0], col_idx[0, 0]])
    other_table = send(table, core_move)

    chip_feats = by_tile(own_feats, other[:ITEMS], core).reshape(PIECE, DIM)
    chip_cot = by_tile(own_cot, other[ITEMS:], core).reshape(PIECE, DIM)
    pre_act = jnp.dot(chip_feats, w_first, preferred_element_type=f32)
    hidden = jax.nn.silu(pre_act).astype(bf16)
    teleport = jnp.dot(hidden, w_second, preferred_element_type=f32).astype(bf16)

    tables = by_tile(table, other_table, core)
    meta = slot_tables(tables[:, :33], tables[:, 33:], zl, y, zh, x, core)
    values = by_tile(packed, other_packed, core)
    flipped = jnp.concatenate(
        [jnp.swapaxes(values[..., :BLK], -1, -2), jnp.swapaxes(values[..., BLK:], -1, -2)], axis=-1
    )
    values = jnp.where(core == 0, values, flipped).reshape(2 * HALF, BLK, 2 * BLK)

    state = jnp.where(core == 0, teleport, chip_cot)
    restart = jnp.where(core == 0, ALPHA, 0.0).astype(f32)
    collected = state.astype(f32)
    for step in range(STEPS):
        z_piece = send(state, gather_z)
        pair = jnp.concatenate([state, z_piece])
        parts = [pair] + [send(pair, functools.partial(gather_ring, hop)) for hop in (1, 2, 3)]
        outs = block_product(meta, values, parts)
        got = [outs[0]] + [send(outs[hop], functools.partial(scatter_ring, hop)) for hop in (1, 2, 3)]
        far = sum(piece[PIECE:].astype(f32) for piece in got).astype(bf16)
        back = send(far, scatter_z)
        summed = sum(piece[:PIECE].astype(f32) for piece in got) + back.astype(f32)
        state = ((1.0 - ALPHA) * summed + restart * teleport.astype(f32)).astype(bf16)
        if step < STEPS - 1:
            collected = collected + state.astype(f32)
    grad_own = (ALPHA * collected + state.astype(f32)).astype(bf16)
    ending = send(jnp.where(core == 0, state, grad_own), core_move)
    propagated = jnp.where(core == 0, state[:ITEMS], ending[ITEMS:])
    grad_teleport = jnp.where(core == 0, ending, grad_own)

    grad_hidden = lax.dot_general(
        grad_teleport, w_second, (((1,), (1,)), ((), ())), preferred_element_type=f32
    )
    grad_pre = (grad_hidden * silu_slope(pre_act)).astype(bf16)
    contract_items = (((0,), (0,)), ((), ()))
    feats_part = lax.dynamic_index_in_dim(chip_feats.reshape(PIECE, 8, 2, 16), core, 2, False).reshape(PIECE, 128)
    hidden_part = lax.dynamic_index_in_dim(hidden.reshape(PIECE, 8, 2, 64), core, 2, False).reshape(PIECE, 512)
    first = lax.dot_general(feats_part, grad_pre, contract_items, preferred_element_type=f32).astype(bf16)
    second = lax.dot_general(hidden_part, grad_teleport, contract_items, preferred_element_type=f32).astype(bf16)
    first = first.reshape(8, 16, 8, 128).transpose(2, 0, 1, 3)
    second = second.reshape(8, 4, 16, 2, 128).transpose(3, 1, 0, 2, 4).reshape(8, 8, 16, 128)
    spread = jnp.concatenate([first, second], axis=2).reshape(64, 32, 128)
    landed = lax.all_to_all(spread, ("zl", "y", "zh", "x"), 0, 0)
    mine = jnp.sum(landed.astype(f32), axis=0)
    z_mine = send(mine, lambda place: {"zl": 1 - place["zl"]})
    both = jnp.where(zl == 0, jnp.stack([mine, z_mine]), jnp.stack([z_mine, mine]))
    ring = [both] + [
        send(both, functools.partial(lambda hop, place: {"y": (place["y"] + hop) % 4}, hop)) for hop in (1, 2, 3)
    ]
    ring = jnp.stack(ring)
    order = (y - jnp.arange(4)) % 4
    ring = ring[order].transpose(1, 0, 2, 3).reshape(8, 32, 128)
    grad_first = ring[:, :16].transpose(1, 0, 2).reshape(16, 1024)
    grad_second = ring[:, 16:].reshape(2, 4, 16, 128).transpose(1, 2, 0, 3).reshape(64, 256)
    return (propagated[None], grad_first, grad_second)


def solution(mesh):
    fine = Mesh(mesh.devices.reshape(SIZES), AXES)
    return jax.shard_map(
        body,
        mesh=fine,
        in_specs=(
            P(WIDE, LOOP, None),
            P(),
            P(),
            P(WIDE, LOOP, None),
            P(LOOP, WIDE, None, None, None),
            P(LOOP, WIDE, None),
            P(LOOP, WIDE, None),
        ),
        out_specs=(P(WIDE, LOOP, None), P(WIDE, None), P(WIDE, None)),
        check_vma=False,
    )
```

time: 1120 us -> 238 us (0.21)
  waiting for transfers between devices: 972 us -> 122 us
  starting transfers between devices: 1.87 us -> 56.8 us
  matrix products: 53.8 us -> 7.17 us
  local copies, waits for them, and re-layouts: 53.6 us -> 19.8 us
  Pallas kernels: 0 us -> 13.6 us
  between operations: 14.6 us -> 1.11 us
    psum x4 -> x0, waiting for transfers between devices: 485 us -> none  [the longest x3 424 us: pull_back(): lax.psum(block_sums(slot_col, products, 0, lax.axis_size('wide') * own_ro...]
    all_gather x6 -> x0, waiting for transfers between devices: 228 us -> none  [the longest x3 117 us: propagate(): columns = lax.all_gather(current, 'wide', axis=0, tiled=True)]
    reduce_scatter x4 -> x0, waiting for transfers between devices: 192 us -> none  [the longest x3 125 us: propagate(): lax.psum_scatter(block_sums(slot_row, products, jnp.int32(0), current.sha...]
    ppermute x0 -> x32, waiting for transfers between devices: none -> 109 us  [send(): return lax.ppermute(value, AXES, permutation(move))]
    unnamed x16 -> x0, waiting for transfers between devices: 66.7 us -> none
    ppermute x0 -> x32, starting transfers between devices: none -> 49.3 us  [send(): return lax.ppermute(value, AXES, permutation(move))]
    dot_general x16 -> x4, matrix products: 53.8 us -> 7.17 us  [the longest x1 2.77 us: body(): lax.dot_general(feats_part, grad_pre, contract_items, preferred_element_t...]
    gather x6 -> x1, local copies, waits for them, and re-layouts: 22.9 us -> 0.56 us  [body(): ring = ring[order].transpose(1, 0, 2, 3).reshape(8, 32, 128)]
  transfers between devices with their start and end apart: 15 -> 33, of which waited for: 15 -> 24; matrix products, arithmetic and copies ran while one was open for 9% -> 12% of each run, Pallas kernels for 0% -> 0%
where the time goes in v1:
time: 238 us; the launch traced here: 235 us
  waiting for transfers between devices  122 us (51%)
  starting transfers between devices  56.8 us (24%)
  local copies, waits for them, and re-layouts  19.8 us (8%)
  other arithmetic  15.5 us (7%)
  Pallas kernels  13.6 us (6%)
  matrix products  7.17 us (3%)
    ppermute x32, waiting for transfers between devices, send(): return lax.ppermute(value, AXES, permutation(move))  109 us
    ppermute x32, starting transfers between devices, send(): return lax.ppermute(value, AXES, permutation(move))  49.3 us
    pallas_call x3, Pallas kernels, block_product(): pl.pallas_call(product_kernel, out_shape=(piece,) * 4, in_specs=[pl.Block...  13.6 us
    all_to_all x1, waiting for transfers between devices, body(): landed = lax.all_to_all(spread, ('zl', 'y', 'zh', 'x'), 0, 0)  12.3 us
    unnamed x46, local copies, waits for them, and re-layouts  7.66 us
    all_to_all x1, starting transfers between devices, body(): landed = lax.all_to_all(spread, ('zl', 'y', 'zh', 'x'), 0, 0)  7.46 us
  transfers between devices with their start and end apart: 33, of which 24 were waited for; matrix products, arithmetic and copies ran while one was open for 12% of the time, Pallas kernels for 0%

profile of v1, /device:TPU:0, one launch (start us, length us, event | category | flops | bytes accessed | tf_op | source)
XLA Modules:
  0.0 235.5 jit_solution(9919421667575467512)
XLA Ops:
  3.0 3.1 %fusion.34 = (bf16[1,1,40,64,64]{2,4,3,1,0:T(8,128)(2,1)}, bf16[1,1,40,64,64]{2,4,3,1,0:T(8,128)(2,1)S(1)}) fusion(bf16[1,1,80,64,64]{2,4,3,1,0:T(8,128)(2,1)} %param.11), kind=kLoop, calls=%fused_computation.131 | loop fusion | bytes 1310720 | tf_op jit(solution)/shard_map/slice | solution.py:161
  6.1 2.1 copy.52
  12.8 2.0 multiply_convert_fusion.1
  17.0 4.0 %collective-permute-start.3 = (bf16[512,256]{1,0:T(8,128)(2,1)S(1)}, bf16[512,256]{1,0:T(8,128)(2,1)S(1)}, u32[]{:S(2)}, u32[]{:S(2)}) collective-permute-start(bf16[512,256]{1,0:T(8,128)(2,1)S(1)} %get-tuple-element.45), channel_id=1, source_target_pairs={{0,8},{1,65},{2,10},{3,67},{4,12},{5,69},{6,14},{7,71},{8,0},{9,73... | collective-permute-start | bytes 786440 | tf_op jit(solution)/shard_map/ppermute | solution.py:39
  21.1 5.8 %collective-permute-done.3 = bf16[512,256]{1,0:T(8,128)(2,1)S(1)} collective-permute-done((bf16[512,256]{1,0:T(8,128)(2,1)S(1)}, bf16[512,256]{1,0:T(8,128)(2,1)S(1)}, u32[]{:S(2)}, u32[]{:S(2)}) %collective-permute-start.3) | collective-permute-done | bytes 262176 | tf_op jit(solution)/shard_map/ppermute | solution.py:39
  26.9 2.8 %collective-permute-start.6 = (bf16[1024,256]{1,0:T(8,128)(2,1)S(1)}, bf16[1024,256]{1,0:T(8,128)(2,1)S(1)}, u32[]{:S(2)}, u32[]{:S(2)}) collective-permute-start(bf16[1024,256]{1,0:T(8,128)(2,1)S(1)} %pad_maximum_fusion.1.part0), channel_id=1, source_target_pairs={{0,6},{1,49},{2,0},{3,51},{4,2},{5,53},{6,4},{7,55},{8,14},{9,57},... | collective-permute-start | bytes 1572872 | tf_op jit(solution)/shard_map/ppermute | solution.py:39
  31.5 1.9 maximum_select_fusion
  33.4 2.0 slice_bitcast_fusion.1
  35.5 2.5 %copy.43 = bf16[2,40,64,64]{3,2,1,0:T(8,128)(2,1)} copy(bf16[2,40,64,64]{2,3,1,0:T(8,128)(2,1)} %get-tuple-element.35) | data formatting | bytes 1310720 | tf_op jit(solution)/shard_map/transpose | solution.py:176
  38.0 1.5 copy.44
  39.5 3.0 %maximum_select_fusion.1.values = bf16[80,64,128]{2,1,0:T(8,128)(2,1)S(1)} fusion(bf16[80,64,64]{2,1,0:T(8,128)(2,1)} %bitcast.81, bf16[80,64,64]{2,1,0:T(8,128)(2,1)} %bitcast.80, bf16[2,40,64,128]{3,2,1,0:T(8,128)(2,1)} %copy-done.3, pred[]{:T(512)S(6)} %eq.15), kind=kLoop, calls=%fused_computation.7 | loop fusion | flops 3276800 | bytes 3932161 | tf_op jit(solution)/shard_map/jit(_where)/select_n | solution.py:178
  43.3 2.9 %collective-permute-done.4.part1 = bf16[1024,256]{1,0:T(8,128)(2,1)} collective-permute-done((bf16[1024,256]{1,0:T(8,128)(2,1)S(1)}, bf16[1024,256]{1,0:T(8,128)(2,1)}, u32[]{:S(2)}, u32[]{:S(2)}) %collective-permute-start.4) | collective-permute-done | bytes 524320 | tf_op jit(solution)/shard_map/ppermute | solution.py:39
  47.2 5.0 %block_product.3 = (bf16[1024,256]{1,0:T(8,128)(2,1)S(1)}, bf16[1024,256]{1,0:T(8,128)(2,1)S(1)}, bf16[1024,256]{1,0:T(8,128)(2,1)S(1)}, bf16[1024,256]{1,0:T(8,128)(2,1)S(1)}) custom-call(s32[3,160]{1,0:T(4,128)S(1)} %pad_add_fusion.meta, bf16[80,64,128]{2,1,0:T(8,128)(2,1)S(1)} %maximum_select_fusion.1.values, ...), custom_call_target="tpu_custom_call" | custom-call | tf_op jit(solution)/shard_map/block_product/pallas_call | solution.py:102
  52.2 1.5 collective-permute-start.7
  53.7 3.5 %collective-permute-start.8 = (bf16[1024,256]{1,0:T(8,128)(2,1)S(1)}, bf16[1024,256]{1,0:T(8,128)(2,1)S(1)}, u32[]{:S(2)}, u32[]{:S(2)}) collective-permute-start(bf16[1024,256]{1,0:T(8,128)(2,1)S(1)} %get-tuple-element.17), channel_id=1, source_target_pairs={{0,32},{1,5},{2,34},{3,7},{4,36},{5,1},{6,38},{7,3},{8,40},{9,13},... | collective-permute-start | bytes 1572872 | tf_op jit(solution)/shard_map/ppermute | solution.py:39
  57.2 2.5 %collective-permute-start.9 = (bf16[1024,256]{1,0:T(8,128)(2,1)S(1)}, bf16[1024,256]{1,0:T(8,128)(2,1)S(1)}, u32[]{:S(2)}, u32[]{:S(2)}) collective-permute-start(bf16[1024,256]{1,0:T(8,128)(2,1)S(1)} %get-tuple-element.18), channel_id=1, source_target_pairs={{0,48},{1,7},{2,50},{3,1},{4,52},{5,3},{6,54},{7,5},{8,56},{9,15},... | collective-permute-start | bytes 1572872 | tf_op jit(solution)/shard_map/ppermute | solution.py:39
  59.8 2.9 %collective-permute-done.7 = bf16[1024,256]{1,0:T(8,128)(2,1)S(1)} collective-permute-done((bf16[1024,256]{1,0:T(8,128)(2,1)S(1)}, bf16[1024,256]{1,0:T(8,128)(2,1)S(1)}, u32[]{:S(2)}, u32[]{:S(2)}) %collective-permute-start.7) | collective-permute-done | bytes 524320 | tf_op jit(solution)/shard_map/ppermute | solution.py:39
  62.7 7.2 %collective-permute-done.8 = bf16[1024,256]{1,0:T(8,128)(2,1)S(1)} collective-permute-done((bf16[1024,256]{1,0:T(8,128)(2,1)S(1)}, bf16[1024,256]{1,0:T(8,128)(2,1)S(1)}, u32[]{:S(2)}, u32[]{:S(2)}) %collective-permute-start.8) | collective-permute-done | bytes 524320 | tf_op jit(solution)/shard_map/ppermute | solution.py:39
  72.2 7.1 %collective-permute-done.10 = bf16[512,256]{1,0:T(8,128)(2,1)} collective-permute-done((bf16[512,256]{1,0:T(8,128)(2,1)S(1)}, bf16[512,256]{1,0:T(8,128)(2,1)}, u32[]{:S(2)}, u32[]{:S(2)}) %collective-permute-start.10) | collective-permute-done | bytes 262176 | tf_op jit(solution)/shard_map/ppermute | solution.py:39
  80.6 2.4 %collective-permute-start.11 = (bf16[512,256]{1,0:T(8,128)(2,1)S(1)}, bf16[512,256]{1,0:T(8,128)(2,1)S(1)}, u32[]{:S(2)}, u32[]{:S(2)}) collective-permute-start(bf16[512,256]{1,0:T(8,128)(2,1)S(1)} %add_convert_fusion.5), channel_id=1, source_target_pairs={{0,8},{1,65},{2,10},{3,67},{4,12},{5,69},{6,14},{7,71},{8,0},{9,73... | collective-permute-start | bytes 786440 | tf_op jit(solution)/shard_map/ppermute | solution.py:39
  83.1 7.6 %collective-permute-done.11 = bf16[512,256]{1,0:T(8,128)(2,1)S(1)} collective-permute-done((bf16[512,256]{1,0:T(8,128)(2,1)S(1)}, bf16[512,256]{1,0:T(8,128)(2,1)S(1)}, u32[]{:S(2)}, u32[]{:S(2)}) %collective-permute-start.11) | collective-permute-done | bytes 262176 | tf_op jit(solution)/shard_map/ppermute | solution.py:39
  94.0 5.9 %collective-permute-done.14.part3 = bf16[1024,256]{1,0:T(8,128)(2,1)S(1)} collective-permute-done((bf16[1024,256]{1,0:T(8,128)(2,1)S(1)}, bf16[1024,256]{1,0:T(8,128)(2,1)S(1)}, u32[]{:S(2)}, u32[]{:S(2)}) %collective-permute-start.14) | collective-permute-done | bytes 524320 | tf_op jit(solution)/shard_map/ppermute | solution.py:39
  99.9 2.9 %collective-permute-done.13.part2 = bf16[1024,256]{1,0:T(8,128)(2,1)S(1)} collective-permute-done((bf16[1024,256]{1,0:T(8,128)(2,1)S(1)}, bf16[1024,256]{1,0:T(8,128)(2,1)S(1)}, u32[]{:S(2)}, u32[]{:S(2)}) %collective-permute-start.13) | collective-permute-done | bytes 524320 | tf_op jit(solution)/shard_map/ppermute | solution.py:39
  102.8 5.5 %collective-permute-done.12.part1 = bf16[1024,256]{1,0:T(8,128)(2,1)S(1)} collective-permute-done((bf16[1024,256]{1,0:T(8,128)(2,1)S(1)}, bf16[1024,256]{1,0:T(8,128)(2,1)S(1)}, u32[]{:S(2)}, u32[]{:S(2)}) %collective-permute-start.12) | collective-permute-done | bytes 524320 | tf_op jit(solution)/shard_map/ppermute | solution.py:39
  108.3 4.3 %block_product.4 = (bf16[1024,256]{1,0:T(8,128)(2,1)S(1)}, bf16[1024,256]{1,0:T(8,128)(2,1)S(1)}, bf16[1024,256]{1,0:T(8,128)(2,1)S(1)}, bf16[1024,256]{1,0:T(8,128)(2,1)S(1)}) custom-call(s32[3,160]{1,0:T(4,128)S(1)} %pad_add_fusion.meta, bf16[80,64,128]{2,1,0:T(8,128)(2,1)S(1)} %maximum_select_fusion.1.values, ...), custom_call_target="tpu_custom_call" | custom-call | tf_op jit(solution)/shard_map/block_product/pallas_call | solution.py:102
  112.8 2.0 collective-permute-start.16
  114.7 2.5 %collective-permute-start.17 = (bf16[1024,256]{1,0:T(8,128)(2,1)S(1)}, bf16[1024,256]{1,0:T(8,128)(2,1)S(1)}, u32[]{:S(2)}, u32[]{:S(2)}) collective-permute-start(bf16[1024,256]{1,0:T(8,128)(2,1)S(1)} %get-tuple-element.22), channel_id=1, source_target_pairs={{0,48},{1,7},{2,50},{3,1},{4,52},{5,3},{6,54},{7,5},{8,56},{9,15},... | collective-permute-start | bytes 1572872 | tf_op jit(solution)/shard_map/ppermute | solution.py:39
  117.3 11.5 %collective-permute-done.15 = bf16[1024,256]{1,0:T(8,128)(2,1)S(1)} collective-permute-done((bf16[1024,256]{1,0:T(8,128)(2,1)S(1)}, bf16[1024,256]{1,0:T(8,128)(2,1)S(1)}, u32[]{:S(2)}, u32[]{:S(2)}) %collective-permute-start.15) | collective-permute-done | bytes 524320 | tf_op jit(solution)/shard_map/ppermute | solution.py:39
  129.9 6.4 %collective-permute-done.18 = bf16[512,256]{1,0:T(8,128)(2,1)S(1)} collective-permute-done((bf16[512,256]{1,0:T(8,128)(2,1)S(1)}, bf16[512,256]{1,0:T(8,128)(2,1)S(1)}, u32[]{:S(2)}, u32[]{:S(2)}) %collective-permute-start.18) | collective-permute-done | bytes 262176 | tf_op jit(solution)/shard_map/ppermute | solution.py:39
  136.5 2.9 %collective-permute-start.19 = (bf16[512,256]{1,0:T(8,128)(2,1)S(1)}, bf16[512,256]{1,0:T(8,128)(2,1)S(1)}, u32[]{:S(2)}, u32[]{:S(2)}) collective-permute-start(bf16[512,256]{1,0:T(8,128)(2,1)S(1)} %add_convert_fusion.3), channel_id=1, source_target_pairs={{0,8},{1,65},{2,10},{3,67},{4,12},{5,69},{6,14},{7,71},{8,0},{9,73... | collective-permute-start | bytes 786440 | tf_op jit(solution)/shard_map/ppermute | solution.py:39
  139.4 5.5 %collective-permute-done.19 = bf16[512,256]{1,0:T(8,128)(2,1)S(1)} collective-permute-done((bf16[512,256]{1,0:T(8,128)(2,1)S(1)}, bf16[512,256]{1,0:T(8,128)(2,1)S(1)}, u32[]{:S(2)}, u32[]{:S(2)}) %collective-permute-start.19) | collective-permute-done | bytes 262176 | tf_op jit(solution)/shard_map/ppermute | solution.py:39
  145.0 2.9 %collective-permute-start.22 = (bf16[1024,256]{1,0:T(8,128)(2,1)S(1)}, bf16[1024,256]{1,0:T(8,128)(2,1)S(1)}, u32[]{:S(2)}, u32[]{:S(2)}) collective-permute-start(bf16[1024,256]{1,0:T(8,128)(2,1)S(1)} %pad_maximum_fusion.3.part0), channel_id=1, source_target_pairs={{0,6},{1,49},{2,0},{3,51},{4,2},{5,53},{6,4},{7,55},{8,14},{9,57},... | collective-permute-start | bytes 1572872 | tf_op jit(solution)/shard_map/ppermute | solution.py:39
  147.9 2.5 %collective-permute-start.21 = (bf16[1024,256]{1,0:T(8,128)(2,1)S(1)}, bf16[1024,256]{1,0:T(8,128)(2,1)S(1)}, u32[]{:S(2)}, u32[]{:S(2)}) collective-permute-start(bf16[1024,256]{1,0:T(8,128)(2,1)S(1)} %pad_maximum_fusion.3.part0), channel_id=1, source_target_pairs={{0,4},{1,33},{2,6},{3,35},{4,0},{5,37},{6,2},{7,39},{8,12},{9,41},... | collective-permute-start | bytes 1572872 | tf_op jit(solution)/shard_map/ppermute | solution.py:39
  151.7 8.5 %collective-permute-done.22.part3 = bf16[1024,256]{1,0:T(8,128)(2,1)S(1)} collective-permute-done((bf16[1024,256]{1,0:T(8,128)(2,1)S(1)}, bf16[1024,256]{1,0:T(8,128)(2,1)S(1)}, u32[]{:S(2)}, u32[]{:S(2)}) %collective-permute-start.22) | collective-permute-done | bytes 524320 | tf_op jit(solution)/shard_map/ppermute | solution.py:39
  160.2 4.0 %collective-permute-done.20.part1 = bf16[1024,256]{1,0:T(8,128)(2,1)S(1)} collective-permute-done((bf16[1024,256]{1,0:T(8,128)(2,1)S(1)}, bf16[1024,256]{1,0:T(8,128)(2,1)S(1)}, u32[]{:S(2)}, u32[]{:S(2)}) %collective-permute-start.20) | collective-permute-done | bytes 524320 | tf_op jit(solution)/shard_map/ppermute | solution.py:39
  164.2 4.3 %block_product.5 = (bf16[1024,256]{1,0:T(8,128)(2,1)S(1)}, bf16[1024,256]{1,0:T(8,128)(2,1)S(1)}, bf16[1024,256]{1,0:T(8,128)(2,1)S(1)}, bf16[1024,256]{1,0:T(8,128)(2,1)S(1)}) custom-call(s32[3,160]{1,0:T(4,128)S(1)} %pad_add_fusion.meta, bf16[80,64,128]{2,1,0:T(8,128)(2,1)S(1)} %maximum_select_fusion.1.values, ...), custom_call_target="tpu_custom_call" | custom-call | tf_op jit(solution)/shard_map/block_product/pallas_call | solution.py:102
  168.5 4.7 %collective-permute-start.23 = (bf16[1024,256]{1,0:T(8,128)(2,1)S(1)}, bf16[1024,256]{1,0:T(8,128)(2,1)S(1)}, u32[]{:S(2)}, u32[]{:S(2)}) collective-permute-start(bf16[1024,256]{1,0:T(8,128)(2,1)S(1)} %get-tuple-element.24), channel_id=1, source_target_pairs={{0,16},{1,3},{2,18},{3,5},{4,20},{5,7},{6,22},{7,1},{8,24},{9,11},... | collective-permute-start | bytes 1572872 | tf_op jit(solution)/shard_map/ppermute | solution.py:39
  174.4 1.6 collective-permute-start.25
  176.0 4.1 %collective-permute-done.23 = bf16[1024,256]{1,0:T(8,128)(2,1)S(1)} collective-permute-done((bf16[1024,256]{1,0:T(8,128)(2,1)S(1)}, bf16[1024,256]{1,0:T(8,128)(2,1)S(1)}, u32[]{:S(2)}, u32[]{:S(2)}) %collective-permute-start.23) | collective-permute-done | bytes 524320 | tf_op jit(solution)/shard_map/ppermute | solution.py:39
  180.1 7.1 %collective-permute-done.24 = bf16[1024,256]{1,0:T(8,128)(2,1)S(1)} collective-permute-done((bf16[1024,256]{1,0:T(8,128)(2,1)S(1)}, bf16[1024,256]{1,0:T(8,128)(2,1)S(1)}, u32[]{:S(2)}, u32[]{:S(2)}) %collective-permute-start.24) | collective-permute-done | bytes 524320 | tf_op jit(solution)/shard_map/ppermute | solution.py:39
  187.4 6.4 %collective-permute-done.26 = bf16[512,256]{1,0:T(8,128)(2,1)S(1)} collective-permute-done((bf16[512,256]{1,0:T(8,128)(2,1)S(1)}, bf16[512,256]{1,0:T(8,128)(2,1)S(1)}, u32[]{:S(2)}, u32[]{:S(2)}) %collective-permute-start.26) | collective-permute-done | bytes 262176 | tf_op jit(solution)/shard_map/ppermute | solution.py:39
  198.3 2.8 %fusion.2 = bf16[16,8,8,128]{3,1,2,0:T(8,128)(2,1)S(1)} fusion(bf16[512,128]{0,1:T(8,128)(2,1)S(1)} %bitcast.96, f32[512,1024]{1,0:T(8,128)} %get-tuple-element.44, bf16[1024,256]{1,0:T(8,128)(2,1)S(1)} %copy-done.14, bf16[512,256]{1,0:T(8,128)(2,1)} %collective-permute-done.27, bf16[512,256]{1,0:T(8,128)(2,1)S(1)} %get-tuple-element.28, pred[]{:T(512)S(6)} %eq.15), kind=kOutput, calls=%fused_computation.12 | convolution fusion | flops 407633920 | bytes 3538945 | tf_op jit(solution)/shard_map/dot_general | solution.py:207
  202.0 7.5 %all-to-all-start = ((bf16[64,32,128]{2,1,0:T(8,128)(2,1)}), bf16[64,32,128]{2,1,0:T(8,128)(2,1)S(1)}, u32[]{:S(2)}, u32[]{:S(2)}) async-start(bf16[64,32,128]{2,1,0:T(8,128)(2,1)} %pad_maximum_fusion.4), calls=%async_computation | async-start | bytes 1048576 | tf_op jit(solution)/shard_map/all_to_all | solution.py:212
  209.5 12.3 %all-to-all-done = bf16[64,32,128]{2,1,0:T(8,128)(2,1)S(1)} async-done(((bf16[64,32,128]{2,1,0:T(8,128)(2,1)}), bf16[64,32,128]{2,1,0:T(8,128)(2,1)S(1)}, u32[]{:S(2)}, u32[]{:S(2)}) %all-to-all-start) | async-done | bytes 524320 | tf_op jit(solution)/shard_map/all_to_all | solution.py:212
  222.8 1.6 fusion.4
  224.4 1.4 collective-permute-done.28
  226.8 1.6 collective-permute-start.30
  229.7 2.5 %collective-permute-done.30 = f32[2,32,128]{2,1,0:T(8,128)S(1)} collective-permute-done((f32[2,32,128]{2,1,0:T(8,128)S(1)}, f32[2,32,128]{2,1,0:T(8,128)S(1)}, u32[]{:S(2)}, u32[]{:S(2)}) %collective-permute-start.30) | collective-permute-done | bytes 32800 | tf_op jit(solution)/shard_map/ppermute | solution.py:39
  (126 shorter events, 35.8 us)
Async XLA Ops:
  0.6 12.1 %copy-start = (bf16[256,1024]{1,0:T(8,128)(2,1)S(1)}, bf16[256,1024]{1,0:T(8,128)(2,1)}, u32[]{:S(2)}) copy-start(bf16[256,1024]{1,0:T(8,128)(2,1)} %param.8) | copy-start | bytes 1572868
  1.5 10.4 %collective-permute-start = (s32[113]{0:T(128)S(1)}, s32[113]{0:T(128)S(1)}, u32[]{:S(2)}, u32[]{:S(2)}) collective-permute-start(s32[113]{0:T(128)S(1)} %pad_add_fusion.1), channel_id=1, source_target_pairs={{0,1},{1,0},{2,3},{3,2},{4,5},{5,4},{6,7},{7,6},{8,9},{9,8},{10,11... | collective-permute-start | bytes 1364 | tf_op jit(solution)/shard_map/ppermute | solution.py:39
  2.5 10.1 %collective-permute-start.2 = (bf16[512,256]{1,0:T(8,128)(2,1)S(1)}, bf16[512,256]{1,0:T(8,128)(2,1)S(1)}, u32[]{:S(2)}, u32[]{:S(2)}) collective-permute-start(bf16[512,256]{1,0:T(8,128)(2,1)S(1)} %pad_maximum_fusion.5), channel_id=1, source_target_pairs={{0,1},{1,0},{2,3},{3,2},{4,5},{5,4},{6,7},{7,6},{8,9},{9,8},{10,11... | collective-permute-start | bytes 786440 | tf_op jit(solution)/shard_map/ppermute | solution.py:39
  9.3 1.2 copy-start.19
  10.6 2.1 copy-start.17
  10.6 2.1 copy-start.18
  10.6 20.9 %collective-permute-start.1 = (bf16[40,64,128]{2,1,0:T(8,128)(2,1)}, bf16[40,64,128]{2,1,0:T(8,128)(2,1)}, u32[]{:S(2)}, u32[]{:S(2)}) collective-permute-start(bf16[40,64,128]{2,1,0:T(8,128)(2,1)} %pad_maximum_fusion), channel_id=1, source_target_pairs={{0,1},{1,0},{2,3},{3,2},{4,5},{5,4},{6,7},{7,6},{8,9},{9,8},{10,11... | collective-permute-start | bytes 1966088 | tf_op jit(solution)/shard_map/ppermute | solution.py:39
  12.7 2.0 copy-start.10
  12.7 3.0 %copy-start.13 = (bf16[1024,256]{1,0:T(8,128)(2,1)S(1)}, bf16[1024,256]{1,0:T(8,128)(2,1)}, u32[]{:S(2)}) copy-start(bf16[1024,256]{1,0:T(8,128)(2,1)} %param.9) | copy-start | bytes 1572868
  17.0 14.5 %copy-start.8 = (bf16[512,256]{1,0:T(8,128)(2,1)}, bf16[512,256]{1,0:T(8,128)(2,1)S(1)}, u32[]{:S(2)}) copy-start(bf16[512,256]{1,0:T(8,128)(2,1)S(1)} %get-tuple-element.45) | copy-start | bytes 786436
  17.0 9.9 %collective-permute-start.3 = (bf16[512,256]{1,0:T(8,128)(2,1)S(1)}, bf16[512,256]{1,0:T(8,128)(2,1)S(1)}, u32[]{:S(2)}, u32[]{:S(2)}) collective-permute-start(bf16[512,256]{1,0:T(8,128)(2,1)S(1)} %get-tuple-element.45), channel_id=1, source_target_pairs={{0,8},{1,65},{2,10},{3,67},{4,12},{5,69},{6,14},{7,71},{8,0},{9,73... | collective-permute-start | bytes 786440 | tf_op jit(solution)/shard_map/ppermute | solution.py:39
  26.9 15.5 %collective-permute-start.6 = (bf16[1024,256]{1,0:T(8,128)(2,1)S(1)}, bf16[1024,256]{1,0:T(8,128)(2,1)S(1)}, u32[]{:S(2)}, u32[]{:S(2)}) collective-permute-start(bf16[1024,256]{1,0:T(8,128)(2,1)S(1)} %pad_maximum_fusion.1.part0), channel_id=1, source_target_pairs={{0,6},{1,49},{2,0},{3,51},{4,2},{5,53},{6,4},{7,55},{8,14},{9,57},... | collective-permute-start | bytes 1572872 | tf_op jit(solution)/shard_map/ppermute | solution.py:39
  29.8 12.7 %collective-permute-start.5 = (bf16[1024,256]{1,0:T(8,128)(2,1)S(1)}, bf16[1024,256]{1,0:T(8,128)(2,1)S(1)}, u32[]{:S(2)}, u32[]{:S(2)}) collective-permute-start(bf16[1024,256]{1,0:T(8,128)(2,1)S(1)} %pad_maximum_fusion.1.part0), channel_id=1, source_target_pairs={{0,4},{1,33},{2,6},{3,35},{4,0},{5,37},{6,2},{7,39},{8,12},{9,41},... | collective-permute-start | bytes 1572872 | tf_op jit(solution)/shard_map/ppermute | solution.py:39
  30.6 15.6 %collective-permute-start.4 = (bf16[1024,256]{1,0:T(8,128)(2,1)S(1)}, bf16[1024,256]{1,0:T(8,128)(2,1)}, u32[]{:S(2)}, u32[]{:S(2)}) collective-permute-start(bf16[1024,256]{1,0:T(8,128)(2,1)S(1)} %pad_maximum_fusion.1.part0), channel_id=1, source_target_pairs={{0,2},{1,17},{2,4},{3,19},{4,6},{5,21},{6,0},{7,23},{8,10},{9,25},... | collective-permute-start | bytes 1572872 | tf_op jit(solution)/shard_map/ppermute | solution.py:39
  33.4 2.1 copy-start.3
  35.4 2.5 %copy-start.4 = (bf16[2,40,64,64]{2,3,1,0:T(8,128)(2,1)S(1)}, bf16[2,40,64,64]{2,3,1,0:T(8,128)(2,1)}, u32[]{:S(2)}) copy-start(bf16[2,40,64,64]{2,3,1,0:T(8,128)(2,1)} %get-tuple-element.36) | copy-start | bytes 1966084
  52.2 27.1 %copy-start.7 = (bf16[512,256]{1,0:T(8,128)(2,1)S(1)}, bf16[512,256]{1,0:T(8,128)(2,1)}, u32[]{:S(2)}) copy-start(bf16[512,256]{1,0:T(8,128)(2,1)} %get-tuple-element.46) | copy-start | bytes 786436
  52.2 10.5 %collective-permute-start.7 = (bf16[1024,256]{1,0:T(8,128)(2,1)S(1)}, bf16[1024,256]{1,0:T(8,128)(2,1)S(1)}, u32[]{:S(2)}, u32[]{:S(2)}) collective-permute-start(bf16[1024,256]{1,0:T(8,128)(2,1)S(1)} %get-tuple-element.16), channel_id=1, source_target_pairs={{0,16},{1,3},{2,18},{3,5},{4,20},{5,7},{6,22},{7,1},{8,24},{9,11},... | collective-permute-start | bytes 1572872 | tf_op jit(solution)/shard_map/ppermute | solution.py:39
  53.7 16.2 %collective-permute-start.8 = (bf16[1024,256]{1,0:T(8,128)(2,1)S(1)}, bf16[1024,256]{1,0:T(8,128)(2,1)S(1)}, u32[]{:S(2)}, u32[]{:S(2)}) collective-permute-start(bf16[1024,256]{1,0:T(8,128)(2,1)S(1)} %get-tuple-element.17), channel_id=1, source_target_pairs={{0,32},{1,5},{2,34},{3,7},{4,36},{5,1},{6,38},{7,3},{8,40},{9,13},... | collective-permute-start | bytes 1572872 | tf_op jit(solution)/shard_map/ppermute | solution.py:39
  57.2 12.7 %collective-permute-start.9 = (bf16[1024,256]{1,0:T(8,128)(2,1)S(1)}, bf16[1024,256]{1,0:T(8,128)(2,1)S(1)}, u32[]{:S(2)}, u32[]{:S(2)}) collective-permute-start(bf16[1024,256]{1,0:T(8,128)(2,1)S(1)} %get-tuple-element.18), channel_id=1, source_target_pairs={{0,48},{1,7},{2,50},{3,1},{4,52},{5,3},{6,54},{7,5},{8,56},{9,15},... | collective-permute-start | bytes 1572872 | tf_op jit(solution)/shard_map/ppermute | solution.py:39
  70.9 8.4 %collective-permute-start.10 = (bf16[512,256]{1,0:T(8,128)(2,1)S(1)}, bf16[512,256]{1,0:T(8,128)(2,1)}, u32[]{:S(2)}, u32[]{:S(2)}) collective-permute-start(bf16[512,256]{1,0:T(8,128)(2,1)S(1)} %add_convert_fusion.6), channel_id=1, source_target_pairs={{0,64},{1,9},{2,66},{3,11},{4,68},{5,13},{6,70},{7,15},{8,72},{9,1... | collective-permute-start | bytes 786440 | tf_op jit(solution)/shard_map/ppermute | solution.py:39
  80.6 10.0 %collective-permute-start.11 = (bf16[512,256]{1,0:T(8,128)(2,1)S(1)}, bf16[512,256]{1,0:T(8,128)(2,1)S(1)}, u32[]{:S(2)}, u32[]{:S(2)}) collective-permute-start(bf16[512,256]{1,0:T(8,128)(2,1)S(1)} %add_convert_fusion.5), channel_id=1, source_target_pairs={{0,8},{1,65},{2,10},{3,67},{4,12},{5,69},{6,14},{7,71},{8,0},{9,73... | collective-permute-start | bytes 786440 | tf_op jit(solution)/shard_map/ppermute | solution.py:39
  90.7 9.2 %collective-permute-start.14 = (bf16[1024,256]{1,0:T(8,128)(2,1)S(1)}, bf16[1024,256]{1,0:T(8,128)(2,1)S(1)}, u32[]{:S(2)}, u32[]{:S(2)}) collective-permute-start(bf16[1024,256]{1,0:T(8,128)(2,1)S(1)} %pad_maximum_fusion.2.part0), channel_id=1, source_target_pairs={{0,6},{1,49},{2,0},{3,51},{4,2},{5,53},{6,4},{7,55},{8,14},{9,57},... | collective-permute-start | bytes 1572872 | tf_op jit(solution)/shard_map/ppermute | solution.py:39
  92.0 10.8 %collective-permute-start.13 = (bf16[1024,256]{1,0:T(8,128)(2,1)S(1)}, bf16[1024,256]{1,0:T(8,128)(2,1)S(1)}, u32[]{:S(2)}, u32[]{:S(2)}) collective-permute-start(bf16[1024,256]{1,0:T(8,128)(2,1)S(1)} %pad_maximum_fusion.2.part0), channel_id=1, source_target_pairs={{0,4},{1,33},{2,6},{3,35},{4,0},{5,37},{6,2},{7,39},{8,12},{9,41},... | collective-permute-start | bytes 1572872 | tf_op jit(solution)/shard_map/ppermute | solution.py:39
  92.8 15.5 %collective-permute-start.12 = (bf16[1024,256]{1,0:T(8,128)(2,1)S(1)}, bf16[1024,256]{1,0:T(8,128)(2,1)S(1)}, u32[]{:S(2)}, u32[]{:S(2)}) collective-permute-start(bf16[1024,256]{1,0:T(8,128)(2,1)S(1)} %pad_maximum_fusion.2.part0), channel_id=1, source_target_pairs={{0,2},{1,17},{2,4},{3,19},{4,6},{5,21},{6,0},{7,23},{8,10},{9,25},... | collective-permute-start | bytes 1572872 | tf_op jit(solution)/shard_map/ppermute | solution.py:39
  112.7 16.1 %collective-permute-start.15 = (bf16[1024,256]{1,0:T(8,128)(2,1)S(1)}, bf16[1024,256]{1,0:T(8,128)(2,1)S(1)}, u32[]{:S(2)}, u32[]{:S(2)}) collective-permute-start(bf16[1024,256]{1,0:T(8,128)(2,1)S(1)} %get-tuple-element.20), channel_id=1, source_target_pairs={{0,16},{1,3},{2,18},{3,5},{4,20},{5,7},{6,22},{7,1},{8,24},{9,11},... | collective-permute-start | bytes 1572872 | tf_op jit(solution)/shard_map/ppermute | solution.py:39
  112.8 16.0 %collective-permute-start.16 = (bf16[1024,256]{1,0:T(8,128)(2,1)S(1)}, bf16[1024,256]{1,0:T(8,128)(2,1)S(1)}, u32[]{:S(2)}, u32[]{:S(2)}) collective-permute-start(bf16[1024,256]{1,0:T(8,128)(2,1)S(1)} %get-tuple-element.21), channel_id=1, source_target_pairs={{0,32},{1,5},{2,34},{3,7},{4,36},{5,1},{6,38},{7,3},{8,40},{9,13},... | collective-permute-start | bytes 1572872 | tf_op jit(solution)/shard_map/ppermute | solution.py:39
  114.7 14.9 %collective-permute-start.17 = (bf16[1024,256]{1,0:T(8,128)(2,1)S(1)}, bf16[1024,256]{1,0:T(8,128)(2,1)S(1)}, u32[]{:S(2)}, u32[]{:S(2)}) collective-permute-start(bf16[1024,256]{1,0:T(8,128)(2,1)S(1)} %get-tuple-element.22), channel_id=1, source_target_pairs={{0,48},{1,7},{2,50},{3,1},{4,52},{5,3},{6,54},{7,5},{8,56},{9,15},... | collective-permute-start | bytes 1572872 | tf_op jit(solution)/shard_map/ppermute | solution.py:39
  129.8 6.5 %collective-permute-start.18 = (bf16[512,256]{1,0:T(8,128)(2,1)S(1)}, bf16[512,256]{1,0:T(8,128)(2,1)S(1)}, u32[]{:S(2)}, u32[]{:S(2)}) collective-permute-start(bf16[512,256]{1,0:T(8,128)(2,1)S(1)} %add_convert_fusion.4), channel_id=1, source_target_pairs={{0,64},{1,9},{2,66},{3,11},{4,68},{5,13},{6,70},{7,15},{8,72},{9,1... | collective-permute-start | bytes 786440 | tf_op jit(solution)/shard_map/ppermute | solution.py:39
  136.5 8.4 %collective-permute-start.19 = (bf16[512,256]{1,0:T(8,128)(2,1)S(1)}, bf16[512,256]{1,0:T(8,128)(2,1)S(1)}, u32[]{:S(2)}, u32[]{:S(2)}) collective-permute-start(bf16[512,256]{1,0:T(8,128)(2,1)S(1)} %add_convert_fusion.3), channel_id=1, source_target_pairs={{0,8},{1,65},{2,10},{3,67},{4,12},{5,69},{6,14},{7,71},{8,0},{9,73... | collective-permute-start | bytes 786440 | tf_op jit(solution)/shard_map/ppermute | solution.py:39
  145.0 15.2 %collective-permute-start.22 = (bf16[1024,256]{1,0:T(8,128)(2,1)S(1)}, bf16[1024,256]{1,0:T(8,128)(2,1)S(1)}, u32[]{:S(2)}, u32[]{:S(2)}) collective-permute-start(bf16[1024,256]{1,0:T(8,128)(2,1)S(1)} %pad_maximum_fusion.3.part0), channel_id=1, source_target_pairs={{0,6},{1,49},{2,0},{3,51},{4,2},{5,53},{6,4},{7,55},{8,14},{9,57},... | collective-permute-start | bytes 1572872 | tf_op jit(solution)/shard_map/ppermute | solution.py:39
  147.9 12.3 %collective-permute-start.21 = (bf16[1024,256]{1,0:T(8,128)(2,1)S(1)}, bf16[1024,256]{1,0:T(8,128)(2,1)S(1)}, u32[]{:S(2)}, u32[]{:S(2)}) collective-permute-start(bf16[1024,256]{1,0:T(8,128)(2,1)S(1)} %pad_maximum_fusion.3.part0), channel_id=1, source_target_pairs={{0,4},{1,33},{2,6},{3,35},{4,0},{5,37},{6,2},{7,39},{8,12},{9,41},... | collective-permute-start | bytes 1572872 | tf_op jit(solution)/shard_map/ppermute | solution.py:39
  150.4 13.8 %collective-permute-start.20 = (bf16[1024,256]{1,0:T(8,128)(2,1)S(1)}, bf16[1024,256]{1,0:T(8,128)(2,1)S(1)}, u32[]{:S(2)}, u32[]{:S(2)}) collective-permute-start(bf16[1024,256]{1,0:T(8,128)(2,1)S(1)} %pad_maximum_fusion.3.part0), channel_id=1, source_target_pairs={{0,2},{1,17},{2,4},{3,19},{4,6},{5,21},{6,0},{7,23},{8,10},{9,25},... | collective-permute-start | bytes 1572872 | tf_op jit(solution)/shard_map/ppermute | solution.py:39
  168.5 25.3 %copy-start.9 = (bf16[512,256]{1,0:T(8,128)(2,1)S(1)}, bf16[512,256]{1,0:T(8,128)(2,1)}, u32[]{:S(2)}) copy-start(bf16[512,256]{1,0:T(8,128)(2,1)} %copy-done.8) | copy-start | bytes 786436
  168.5 11.6 %collective-permute-start.23 = (bf16[1024,256]{1,0:T(8,128)(2,1)S(1)}, bf16[1024,256]{1,0:T(8,128)(2,1)S(1)}, u32[]{:S(2)}, u32[]{:S(2)}) collective-permute-start(bf16[1024,256]{1,0:T(8,128)(2,1)S(1)} %get-tuple-element.24), channel_id=1, source_target_pairs={{0,16},{1,3},{2,18},{3,5},{4,20},{5,7},{6,22},{7,1},{8,24},{9,11},... | collective-permute-start | bytes 1572872 | tf_op jit(solution)/shard_map/ppermute | solution.py:39
  173.3 13.9 %collective-permute-start.24 = (bf16[1024,256]{1,0:T(8,128)(2,1)S(1)}, bf16[1024,256]{1,0:T(8,128)(2,1)S(1)}, u32[]{:S(2)}, u32[]{:S(2)}) collective-permute-start(bf16[1024,256]{1,0:T(8,128)(2,1)S(1)} %get-tuple-element.25), channel_id=1, source_target_pairs={{0,32},{1,5},{2,34},{3,7},{4,36},{5,1},{6,38},{7,3},{8,40},{9,13},... | collective-permute-start | bytes 1572872 | tf_op jit(solution)/shard_map/ppermute | solution.py:39
  174.4 12.8 %collective-permute-start.25 = (bf16[1024,256]{1,0:T(8,128)(2,1)S(1)}, bf16[1024,256]{1,0:T(8,128)(2,1)S(1)}, u32[]{:S(2)}, u32[]{:S(2)}) collective-permute-start(bf16[1024,256]{1,0:T(8,128)(2,1)S(1)} %get-tuple-element.26), channel_id=1, source_target_pairs={{0,48},{1,7},{2,50},{3,1},{4,52},{5,3},{6,54},{7,5},{8,56},{9,15},... | collective-permute-start | bytes 1572872 | tf_op jit(solution)/shard_map/ppermute | solution.py:39
  187.3 7.7 %copy-start.11 = (bf16[2,256,256]{2,1,0:T(8,128)(2,1)S(1)}, bf16[2,256,256]{2,1,0:T(8,128)(2,1)}, u32[]{:S(2)}) copy-start(bf16[2,256,256]{2,1,0:T(8,128)(2,1)} %copy-done.10) | copy-start | bytes 786436
  187.3 7.9 %copy-start.6 = (bf16[512,1024]{1,0:T(8,128)(2,1)S(1)}, bf16[512,1024]{1,0:T(8,128)(2,1)}, u32[]{:S(2)}) copy-start(bf16[512,1024]{1,0:T(8,128)(2,1)} %copy-done.5) | copy-start | bytes 3145732
  187.4 6.5 %collective-permute-start.26 = (bf16[512,256]{1,0:T(8,128)(2,1)S(1)}, bf16[512,256]{1,0:T(8,128)(2,1)S(1)}, u32[]{:S(2)}, u32[]{:S(2)}) collective-permute-start(bf16[512,256]{1,0:T(8,128)(2,1)S(1)} %add_convert_fusion.2), channel_id=1, source_target_pairs={{0,64},{1,9},{2,66},{3,11},{4,68},{5,13},{6,70},{7,15},{8,72},{9,1... | collective-permute-start | bytes 786440 | tf_op jit(solution)/shard_map/ppermute | solution.py:39
  195.0 1.9 collective-permute-start.27
  196.0 2.2 copy-start.14
  201.2 21.6 %copy-start.12 = (bf16[512,256]{1,0:T(8,128)(2,1)S(1)}, bf16[512,256]{1,0:T(8,128)(2,1)}, u32[]{:S(2)}) copy-start(bf16[512,256]{1,0:T(8,128)(2,1)} %get-tuple-element.29) | copy-start | bytes 786436
  202.0 19.8 %all-to-all-start = ((bf16[64,32,128]{2,1,0:T(8,128)(2,1)}), bf16[64,32,128]{2,1,0:T(8,128)(2,1)S(1)}, u32[]{:S(2)}, u32[]{:S(2)}) async-start(bf16[64,32,128]{2,1,0:T(8,128)(2,1)} %pad_maximum_fusion.4), calls=%async_computation | async-start | bytes 1048576 | tf_op jit(solution)/shard_map/all_to_all | solution.py:212
  221.9 3.8 %collective-permute-start.28 = (f32[32,128]{1,0:T(8,128)S(1)}, f32[32,128]{1,0:T(8,128)S(1)}, u32[]{:S(2)}, u32[]{:S(2)}) collective-permute-start(f32[32,128]{1,0:T(8,128)S(1)} %convert_reduce_fusion), channel_id=1, source_target_pairs={{0,64},{1,65},{2,66},{3,67},{4,68},{5,69},{6,70},{7,71},{8,72},{9,... | collective-permute-start | bytes 49160 | tf_op jit(solution)/shard_map/ppermute | solution.py:39
  225.7 3.9 %collective-permute-start.31 = (f32[2,32,128]{2,1,0:T(8,128)S(1)}, f32[2,32,128]{2,1,0:T(8,128)S(1)}, u32[]{:S(2)}, u32[]{:S(2)}) collective-permute-start(f32[2,32,128]{2,1,0:T(8,128)S(1)} %maximum_select_fusion.5), channel_id=1, source_target_pairs={{0,48},{1,49},{2,50},{3,51},{4,52},{5,53},{6,54},{7,55},{8,56},{9,... | collective-permute-start | bytes 98312 | tf_op jit(solution)/shard_map/ppermute | solution.py:39
  226.8 5.4 %collective-permute-start.30 = (f32[2,32,128]{2,1,0:T(8,128)S(1)}, f32[2,32,128]{2,1,0:T(8,128)S(1)}, u32[]{:S(2)}, u32[]{:S(2)}) collective-permute-start(f32[2,32,128]{2,1,0:T(8,128)S(1)} %maximum_select_fusion.5), channel_id=1, source_target_pairs={{0,32},{1,33},{2,34},{3,35},{4,36},{5,37},{6,38},{7,39},{8,40},{9,... | collective-permute-start | bytes 98312 | tf_op jit(solution)/shard_map/ppermute | solution.py:39
  228.4 5.1 %collective-permute-start.29 = (f32[2,32,128]{2,1,0:T(8,128)S(1)}, f32[2,32,128]{2,1,0:T(8,128)S(1)}, u32[]{:S(2)}, u32[]{:S(2)}) collective-permute-start(f32[2,32,128]{2,1,0:T(8,128)S(1)} %maximum_select_fusion.5), channel_id=1, source_target_pairs={{0,16},{1,17},{2,18},{3,19},{4,20},{5,21},{6,22},{7,23},{8,24},{9,... | collective-permute-start | bytes 98312 | tf_op jit(solution)/shard_map/ppermute | solution.py:39
  (6 other events, 5.9 us)

commit v2 on v1

v2 whole, which is shorter than its diff:
```python
import functools

import jax
import jax.numpy as jnp
import numpy as np
from jax import lax
from jax.experimental import pallas as pl
from jax.experimental.pallas import tpu as pltpu
from jax.sharding import Mesh
from jax.sharding import PartitionSpec as P

STEPS = 3
ALPHA = 0.1
AXES = ("zl", "y", "zh", "x", "c")
SIZES = (2, 4, 2, 4, 2)
LOOP = ("zl", "y")
WIDE = ("zh", "x", "c")
BLK = 64
DIM = 256
ITEMS = 256
PIECE = 2 * ITEMS
SLOTS = 80
PACK = 32
LANES = 128
STATE = 1024
GRAPH = 4 * STATE
TILES = 8
GROUP = 8


def permutation(move):
    pairs = []
    for source in range(int(np.prod(SIZES))):
        place = dict(zip(AXES, np.unravel_index(source, SIZES)))
        place = {name: int(value) for name, value in place.items()}
        place.update(move(place))
        pairs.append((source, int(np.ravel_multi_index([place[name] for name in AXES], SIZES))))
    return pairs


def send(value, move):
    return lax.ppermute(value, AXES, permutation(move))


def core_move(place):
    return {"c": 1 - place["c"]}


def z_move(step, place):
    spot = (2 * place["zh"] + place["zl"] + step) % 4
    return {"zh": spot // 2, "zl": spot % 2}


def gather_ring(step, place):
    return {"y": (place["y"] + step) % 4} if place["c"] else {"x": (place["x"] + step) % 4}


def scatter_ring(step, place):
    return {"x": (place["x"] + step) % 4} if place["c"] else {"y": (place["y"] + step) % 4}


def product_kernel(meta, masks, *refs):
    tiles, parts, outs = refs[:TILES], refs[TILES : TILES + 4], refs[TILES + 4 : TILES + 8]
    values, gathered, sums, sems = refs[TILES + 8 :]
    copies = [
        pltpu.make_async_copy(part, gathered.at[pl.ds(index * STATE, STATE)], sems.at[TILES + index])
        for index, part in enumerate(parts)
    ]
    copies += [
        pltpu.make_async_copy(tile.at[pl.ds(0, SLOTS)], values.at[pl.ds(index * SLOTS, SLOTS)], sems.at[index])
        for index, tile in enumerate(tiles)
    ]
    for copy in copies:
        copy.start()
    sums[...] = jnp.zeros_like(sums)
    for copy in copies:
        copy.wait()
    adjoint = meta[2, TILES]
    left, right = masks[0], masks[1]

    def one_tile(tile, carry):
        first = tile * SLOTS
        live = meta[2, tile]

        def group(index, inner):
            products = []
            for lane in range(GROUP):
                slot = first + index * GROUP + lane
                entries = values[slot]
                source = pl.multiple_of(meta[0, slot], PACK)
                vectors = gathered[pl.ds(source, PACK), :]
                rows = jnp.where(adjoint == 0, entries, vectors)
                cols = jnp.where(adjoint == 0, vectors, entries)
                turned = pltpu.roll(cols, BLK, 1)
                spread = jnp.concatenate([cols * left, turned * left, turned * right, cols * right], axis=0)
                products.append(jnp.dot(rows, spread, preferred_element_type=jnp.float32))
            for lane in range(GROUP):
                target = pl.multiple_of(meta[1, first + index * GROUP + lane], PACK)
                sums[pl.ds(target, PACK), :] += products[lane]
            return inner

        return lax.fori_loop(0, (live + GROUP - 1) // GROUP, group, carry)

    lax.fori_loop(0, TILES, one_tile, 0)
    for index, out in enumerate(outs):
        out[...] = sums[index * STATE : (index + 1) * STATE, :].astype(out.dtype)


def block_product(meta, masks, tiles, parts):
    piece = jax.ShapeDtypeStruct((STATE, LANES), jnp.bfloat16)
    return pl.pallas_call(
        product_kernel,
        out_shape=(piece,) * 4,
        in_specs=[
            pl.BlockSpec(memory_space=pltpu.SMEM),
            pl.BlockSpec(memory_space=pltpu.VMEM),
        ]
        + [pl.BlockSpec(memory_space=pl.ANY)] * (TILES + 4),
        out_specs=(pl.BlockSpec(memory_space=pltpu.VMEM),) * 4,
        scratch_shapes=[
            pltpu.VMEM((TILES * SLOTS, PACK, LANES), jnp.bfloat16),
            pltpu.VMEM((GRAPH, LANES), jnp.bfloat16),
            pltpu.VMEM((GRAPH + PACK, LANES), jnp.float32),
            pltpu.SemaphoreType.DMA((TILES + 4,)),
        ],
        compiler_params=pltpu.CompilerParams(vmem_limit_bytes=40 * 2**20),
        name="block_product",
    )(meta, masks, *tiles, *parts)


def slot_tables(pointers, columns, zl, y, zh, x, core):
    slot_ids = jnp.arange(SLOTS, dtype=jnp.int32)
    rows = jnp.sum((pointers[:, 1:, None] <= slot_ids).astype(jnp.int32), axis=1)
    rows = jnp.minimum(rows, pointers.shape[1] - 2)
    live_count = pointers[:, -1]
    live = slot_ids[None, :] < live_count[:, None]
    place = jnp.arange(TILES, dtype=jnp.int32)
    spot = 2 * zh + zl
    from_z = (spot - place // 2) % 4
    tile_zh, tile_zl = (from_z // 2)[:, None], (from_z % 2)[:, None]
    tile_core = (core ^ (place % 2))[:, None]
    row_l = rows // 4
    row_y, row_z = row_l % 4, 2 * tile_zh + row_l // 4
    row_base = ((spot - row_z) % 4) * 8 + tile_core * 4 + rows % 4
    col_w = columns // 4
    col_x, col_z = (col_w // 2) % 4, 2 * (col_w // 8) + tile_zl
    col_base = ((spot - col_z) % 4) * 8 + (col_w % 2) * 4 + columns % 4
    forward_source = ((x - col_x) % 4) * STATE + col_base * PACK
    forward_target = ((row_y - y) % 4) * STATE + row_base * PACK
    adjoint_source = ((y - row_y) % 4) * STATE + row_base * PACK
    adjoint_target = ((col_x - x) % 4) * STATE + col_base * PACK
    source = jnp.where(live, jnp.where(core == 0, forward_source, adjoint_source), 0)
    target = jnp.where(live, jnp.where(core == 0, forward_target, adjoint_target), GRAPH)
    counts = jnp.concatenate([live_count, core[None], jnp.zeros((TILES * SLOTS - TILES - 1,), jnp.int32)])
    return jnp.stack([source.reshape(-1), target.reshape(-1), counts])


def pack_rows(blocks):
    return jnp.concatenate([blocks[..., :PACK, :], blocks[..., PACK:, :]], axis=-1)


def unpack_rows(blocks):
    return jnp.concatenate([blocks[..., :BLK], blocks[..., BLK:]], axis=-2)


def split_features(chip_state, core):
    blocks = chip_state.reshape(8, BLK, 4, BLK).transpose(2, 0, 1, 3)
    blocks = jnp.where(core == 0, blocks, jnp.swapaxes(blocks, -1, -2))
    return pack_rows(blocks).reshape(4, 8 * PACK, LANES)


def join_features(pieces, core):
    blocks = unpack_rows(pieces.reshape(4, 8, PACK, LANES))
    blocks = jnp.where(core == 0, blocks, jnp.swapaxes(blocks, -1, -2))
    return blocks.transpose(1, 2, 0, 3).reshape(PIECE, DIM)


def silu_slope(value):
    sigma = jax.nn.sigmoid(value)
    return sigma * (1.0 + value * (1.0 - sigma))


def by_tile(own, other, core):
    return jnp.where(core == 0, jnp.stack([own, other]), jnp.stack([other, own]))


def body(feats, w_first, w_second, cotangent, block_values, row_ptr, col_idx):
    f32, bf16 = jnp.float32, jnp.bfloat16
    zl, y, zh, x, core = (lax.axis_index(name) for name in AXES)
    spot = 2 * zh + zl
    table = jnp.zeros((1, PACK, LANES), bf16)
    table = table.at[0, 0, :33].set(row_ptr[0, 0].astype(bf16)).at[0, 1, :SLOTS].set(col_idx[0, 0].astype(bf16))
    tile = jnp.concatenate([pack_rows(block_values[0, 0]), table])
    same_core = [tile] + [send(tile, functools.partial(z_move, hop)) for hop in (1, 2, 3)]
    tiles = []
    for mine in same_core:
        tiles += [mine, send(mine, core_move)]

    own_feats, own_cot = feats[0], cotangent[0]
    other = send(jnp.concatenate([own_feats, own_cot]), core_move)
    chip_feats = by_tile(own_feats, other[:ITEMS], core).reshape(PIECE, DIM)
    chip_cot = by_tile(own_cot, other[ITEMS:], core).reshape(PIECE, DIM)
    pre_act = jnp.dot(chip_feats, w_first, preferred_element_type=f32)
    hidden = jax.nn.silu(pre_act).astype(bf16)
    teleport = jnp.dot(hidden, w_second, preferred_element_type=f32).astype(bf16)

    tables = jnp.stack([piece[SLOTS] for piece in tiles])
    meta = slot_tables(
        tables[:, 0, :33].astype(jnp.int32), tables[:, 1, :SLOTS].astype(jnp.int32), zl, y, zh, x, core
    )
    lanes = jnp.arange(LANES)
    masks = jnp.stack([lanes < BLK, lanes >= BLK]).astype(bf16)
    masks = jnp.broadcast_to(masks[:, None, :], (2, PACK, LANES))

    start = split_features(jnp.where(core == 0, teleport, chip_cot), core)
    start = [lax.dynamic_index_in_dim(start, (spot + hop) % 4, 0, False) for hop in range(4)]
    state = jnp.concatenate(
        [start[0]] + [send(start[hop], functools.partial(z_move, hop)) for hop in (1, 2, 3)]
    )
    restart = jnp.where(core == 0, ALPHA, 0.0).astype(f32)
    constant = restart * state.astype(f32)
    collected = state.astype(f32)
    for step in range(STEPS):
        parts = [state] + [send(state, functools.partial(gather_ring, hop)) for hop in (1, 2, 3)]
        outs = block_product(meta, masks, tiles, parts)
        got = [outs[0]] + [send(outs[hop], functools.partial(scatter_ring, hop)) for hop in (1, 2, 3)]
        summed = sum(piece.astype(f32) for piece in got)
        state = ((1.0 - ALPHA) * summed + constant).astype(bf16)
        if step < STEPS - 1:
            collected = collected + state.astype(f32)
    last = jnp.where(core == 0, state, (ALPHA * collected + state.astype(f32)).astype(bf16))
    last = last.reshape(4, 8 * PACK, LANES)
    pieces = [last[0]] + [send(last[hop], functools.partial(z_move, -hop)) for hop in (1, 2, 3)]
    pieces = jnp.stack(pieces)[(jnp.arange(4) - spot) % 4]
    joined = join_features(pieces, core)
    ending = send(joined, core_move)
    propagated = jnp.where(core == 0, joined[:ITEMS], ending[ITEMS:])
    grad_teleport = jnp.where(core == 0, ending, joined)

    grad_hidden = lax.dot_general(
        grad_teleport, w_second, (((1,), (1,)), ((), ())), preferred_element_type=f32
    )
    grad_pre = (grad_hidden * silu_slope(pre_act)).astype(bf16)
    contract_items = (((0,), (0,)), ((), ()))
    feats_part = lax.dynamic_index_in_dim(chip_feats.reshape(PIECE, 8, 2, 16), core, 2, False).reshape(PIECE, 128)
    hidden_part = lax.dynamic_index_in_dim(hidden.reshape(PIECE, 8, 2, 64), core, 2, False).reshape(PIECE, 512)
    first = lax.dot_general(feats_part, grad_pre, contract_items, preferred_element_type=f32).astype(bf16)
    second = lax.dot_general(hidden_part, grad_teleport, contract_items, preferred_element_type=f32).astype(bf16)
    first = first.reshape(8, 16, 8, 128).transpose(2, 0, 1, 3)
    second = second.reshape(8, 4, 16, 2, 128).transpose(3, 1, 0, 2, 4).reshape(8, 8, 16, 128)
    spread = jnp.concatenate([first, second], axis=2).reshape(64, 32, 128)
    landed = lax.all_to_all(spread, ("zl", "y", "zh", "x"), 0, 0)
    mine = jnp.sum(landed.astype(f32), axis=0)
    z_mine = send(mine, lambda place: {"zl": 1 - place["zl"]})
    both = jnp.where(zl == 0, jnp.stack([mine, z_mine]), jnp.stack([z_mine, mine]))
    ring = [both] + [
        send(both, functools.partial(lambda hop, place: {"y": (place["y"] + hop) % 4}, hop)) for hop in (1, 2, 3)
    ]
    ring = jnp.stack(ring)
    order = (y - jnp.arange(4)) % 4
    ring = ring[order].transpose(1, 0, 2, 3).reshape(8, 32, 128)
    grad_first = ring[:, :16].transpose(1, 0, 2).reshape(16, 1024)
    grad_second = ring[:, 16:].reshape(2, 4, 16, 128).transpose(1, 2, 0, 3).reshape(64, 256)
    return (propagated[None], grad_first, grad_second)


def solution(mesh):
    fine = Mesh(mesh.devices.reshape(SIZES), AXES)
    return jax.shard_map(
        body,
        mesh=fine,
        in_specs=(
            P(WIDE, LOOP, None),
            P(),
            P(),
            P(WIDE, LOOP, None),
            P(LOOP, WIDE, None, None, None),
            P(LOOP, WIDE, None),
            P(LOOP, WIDE, None),
        ),
        out_specs=(P(WIDE, LOOP, None), P(WIDE, None), P(WIDE, None)),
        check_vma=False,
    )
```

time: 238 us -> 227 us (0.954); the launches traced: 235 us -> 231 us
  waiting for transfers between devices: 122 us -> 84 us
  Pallas kernels: 13.6 us -> 41.3 us
  local copies, waits for them, and re-layouts: 19.8 us -> 29.4 us
  other arithmetic: 15.5 us -> 8.49 us
  starting transfers between devices: 56.8 us -> 59.4 us
    ppermute x32 -> x37, waiting for transfers between devices: 109 us -> 70.9 us  [send(): return lax.ppermute(value, AXES, permutation(move))]
    pallas_call x3, Pallas kernels: 13.6 us -> 41.3 us  [block_product(): pl.pallas_call(product_kernel, out_shape=(piece,) * 4, in_specs=[pl.Block...]
    unnamed x46 -> x64, local copies, waits for them, and re-layouts: 7.66 us -> 17.6 us
    transpose x3 -> x1, local copies, waits for them, and re-layouts: 6.05 us -> 0.41 us  [join_features(): return blocks.transpose(1, 2, 0, 3).reshape(PIECE, DIM)]
    reshape x0 -> x3, local copies, waits for them, and re-layouts: none -> 3.51 us  [the longest x2 3.18 us: split_features(): blocks = chip_state.reshape(8, BLK, 4, BLK).transpose(2, 0, 1, 3)]
    select_n x4 -> x6, other arithmetic: 4.39 us -> 1.85 us  [the longest x1 1.3 us: split_features(): blocks = jnp.where(core == 0, blocks, jnp.swapaxes(blocks, -1, -2))]
    ppermute x32 -> x37, starting transfers between devices: 49.3 us -> 50 us  [send(): return lax.ppermute(value, AXES, permutation(move))]
  transfers between devices with their start and end apart: 33 -> 38, of which waited for: 24 -> 26; matrix products, arithmetic and copies ran while one was open for 12% -> 7% of each run, Pallas kernels for 0% -> 0%
where the time goes in v2:
time: 227 us; the launch traced here: 231 us
  waiting for transfers between devices  84 us (37%)
  starting transfers between devices  59.4 us (26%)
  Pallas kernels  41.3 us (18%)
  local copies, waits for them, and re-layouts  29.4 us (13%)
  other arithmetic  8.49 us (4%)
  matrix products  7.06 us (3%)
    ppermute x37, waiting for transfers between devices, send(): return lax.ppermute(value, AXES, permutation(move))  70.9 us
    ppermute x37, starting transfers between devices, send(): return lax.ppermute(value, AXES, permutation(move))  50 us
    pallas_call x3, Pallas kernels, block_product(): pl.pallas_call(product_kernel, out_shape=(piece,) * 4, in_specs=[pl.Block...  41.3 us
    unnamed x64, local copies, waits for them, and re-layouts  17.6 us
    all_to_all x1, waiting for transfers between devices, body(): landed = lax.all_to_all(spread, ('zl', 'y', 'zh', 'x'), 0, 0)  13.1 us
    all_to_all x1, starting transfers between devices, body(): landed = lax.all_to_all(spread, ('zl', 'y', 'zh', 'x'), 0, 0)  9.45 us
  transfers between devices with their start and end apart: 38, of which 26 were waited for; matrix products, arithmetic and copies ran while one was open for 7% of the time, Pallas kernels for 0%

profile of v2, /device:TPU:0, one launch (start us, length us, event | category | flops | bytes accessed | tf_op | source)
XLA Modules:
  0.0 231.1 jit_solution(13313696140173397722)
XLA Ops:
  2.0 2.9 %copy.39 = bf16[1,1,80,64,64]{4,3,2,1,0:T(8,128)(2,1)S(1)} copy(bf16[1,1,80,64,64]{2,4,3,1,0:T(8,128)(2,1)} %param.15) | data formatting | bytes 1310720 | tf_op args[4]
  5.8 4.0 %collective-permute-start.3 = (bf16[81,32,128]{2,1,0:T(8,128)(2,1)S(1)}, bf16[81,32,128]{2,1,0:T(8,128)(2,1)S(1)}, u32[]{:S(2)}, u32[]{:S(2)}) collective-permute-start(bf16[81,32,128]{2,1,0:T(8,128)(2,1)S(1)} %pad_maximum_fusion.refs_0_), channel_id=1, source_target_pairs={{0,8},{1,9},{2,10},{3,11},{4,12},{5,13},{6,14},{7,15},{8,0},{9,1},... | collective-permute-start | bytes 1990664 | tf_op jit(solution)/shard_map/ppermute | solution.py:42
  14.8 2.3 multiply_convert_fusion.1
  17.0 1.7 fusion.2
  19.8 2.1 copy.41
  21.9 1.3 bitcast_select_fusion.1
  23.4 2.3 collective-permute-start.10
  25.7 3.2 %collective-permute-done.10 = bf16[256,128]{1,0:T(8,128)(2,1)S(1)} collective-permute-done((bf16[256,128]{1,0:T(8,128)(2,1)S(1)}, bf16[256,128]{1,0:T(8,128)(2,1)S(1)}, u32[]{:S(2)}, u32[]{:S(2)}) %collective-permute-start.10) | collective-permute-done | bytes 65568 | tf_op jit(solution)/shard_map/ppermute | solution.py:42
  29.0 3.7 %collective-permute-start.5 = (bf16[81,32,128]{2,1,0:T(8,128)(2,1)S(1)}, bf16[81,32,128]{2,1,0:T(8,128)(2,1)S(1)}, u32[]{:S(2)}, u32[]{:S(2)}) collective-permute-start(bf16[81,32,128]{2,1,0:T(8,128)(2,1)S(1)} %pad_maximum_fusion.refs_0_), channel_id=1, source_target_pairs={{0,72},{1,73},{2,74},{3,75},{4,76},{5,77},{6,78},{7,79},{8,64},{9,... | collective-permute-start | bytes 1990664 | tf_op jit(solution)/shard_map/ppermute | solution.py:42
  32.6 7.8 %collective-permute-done.9 = bf16[256,128]{1,0:T(8,128)(2,1)S(1)} collective-permute-done((bf16[256,128]{1,0:T(8,128)(2,1)S(1)}, bf16[256,128]{1,0:T(8,128)(2,1)S(1)}, u32[]{:S(2)}, u32[]{:S(2)}) %collective-permute-start.9) | collective-permute-done | bytes 65568 | tf_op jit(solution)/shard_map/ppermute | solution.py:42
  40.5 5.4 %collective-permute-done.8 = bf16[256,128]{1,0:T(8,128)(2,1)S(1)} collective-permute-done((bf16[256,128]{1,0:T(8,128)(2,1)S(1)}, bf16[256,128]{1,0:T(8,128)(2,1)S(1)}, u32[]{:S(2)}, u32[]{:S(2)}) %collective-permute-start.8) | collective-permute-done | bytes 65568 | tf_op jit(solution)/shard_map/ppermute | solution.py:42
  45.9 2.8 %collective-permute-start.13 = (bf16[1024,128]{1,0:T(8,128)(2,1)S(1)}, bf16[1024,128]{1,0:T(8,128)(2,1)}, u32[]{:S(2)}, u32[]{:S(2)}) collective-permute-start(bf16[1024,128]{1,0:T(8,128)(2,1)S(1)} %pad_maximum_fusion.5.refs_8_), channel_id=1, source_target_pairs={{0,6},{1,49},{2,0},{3,51},{4,2},{5,53},{6,4},{7,55},{8,14},{9,57},... | collective-permute-start | bytes 786440 | tf_op jit(solution)/shard_map/ppermute | solution.py:42
  56.8 2.7 %collective-permute-done.11.refs_9_ = bf16[1024,128]{1,0:T(8,128)(2,1)} collective-permute-done((bf16[1024,128]{1,0:T(8,128)(2,1)S(1)}, bf16[1024,128]{1,0:T(8,128)(2,1)}, u32[]{:S(2)}, u32[]{:S(2)}) %collective-permute-start.11) | collective-permute-done | bytes 262176 | tf_op jit(solution)/shard_map/ppermute | solution.py:42
  59.5 1.1 copy-done.2
  63.9 14.3 %block_product.3 = (bf16[1024,128]{1,0:T(8,128)(2,1)S(1)}, bf16[1024,128]{1,0:T(8,128)(2,1)}, bf16[1024,128]{1,0:T(8,128)(2,1)}, bf16[1024,128]{1,0:T(8,128)(2,1)}) custom-call(s32[3,640]{1,0:T(4,128)S(1)} %pad_add_fusion.meta, bf16[2,32,128]{2,1,0:T(8,128)(2,1)S(1)} %broadcast_in_dim.16.masks, bf16[81,32,128]{2,1,0:T(8,128)(2,1)S(1)} %pad_maximum_fusion.refs_0_, ...), custom_call_target="tpu_custom_call" | custom-call | tf_op jit(solution)/shard_map/block_product/pallas_call | solution.py:111
  78.9 6.8 %collective-permute-start.15 = (bf16[1024,128]{1,0:T(8,128)(2,1)}, bf16[1024,128]{1,0:T(8,128)(2,1)}, u32[]{:S(2)}, u32[]{:S(2)}) collective-permute-start(bf16[1024,128]{1,0:T(8,128)(2,1)} %get-tuple-element.41), channel_id=1, source_target_pairs={{0,32},{1,5},{2,34},{3,7},{4,36},{5,1},{6,38},{7,3},{8,40},{9,13},... | collective-permute-start | bytes 786440 | tf_op jit(solution)/shard_map/ppermute | solution.py:42
  85.7 3.1 %collective-permute-done.14 = bf16[1024,128]{1,0:T(8,128)(2,1)S(1)} collective-permute-done((bf16[1024,128]{1,0:T(8,128)(2,1)}, bf16[1024,128]{1,0:T(8,128)(2,1)S(1)}, u32[]{:S(2)}, u32[]{:S(2)}) %collective-permute-start.14) | collective-permute-done | bytes 262176 | tf_op jit(solution)/shard_map/ppermute | solution.py:42
  88.8 4.4 %collective-permute-done.15 = bf16[1024,128]{1,0:T(8,128)(2,1)} collective-permute-done((bf16[1024,128]{1,0:T(8,128)(2,1)}, bf16[1024,128]{1,0:T(8,128)(2,1)}, u32[]{:S(2)}, u32[]{:S(2)}) %collective-permute-start.15) | collective-permute-done | bytes 262176 | tf_op jit(solution)/shard_map/ppermute | solution.py:42
  93.2 1.4 fusion.8.refs_8_
  94.8 1.9 collective-permute-start.17
  96.7 4.3 %collective-permute-done.19.refs_11_ = bf16[1024,128]{1,0:T(8,128)(2,1)S(1)} collective-permute-done((bf16[1024,128]{1,0:T(8,128)(2,1)S(1)}, bf16[1024,128]{1,0:T(8,128)(2,1)S(1)}, u32[]{:S(2)}, u32[]{:S(2)}) %collective-permute-start.19) | collective-permute-done | bytes 262176 | tf_op jit(solution)/shard_map/ppermute | solution.py:42
  101.0 1.7 collective-permute-done.18.refs_10_
  102.7 2.7 %collective-permute-done.17.refs_9_ = bf16[1024,128]{1,0:T(8,128)(2,1)S(1)} collective-permute-done((bf16[1024,128]{1,0:T(8,128)(2,1)S(1)}, bf16[1024,128]{1,0:T(8,128)(2,1)S(1)}, u32[]{:S(2)}, u32[]{:S(2)}) %collective-permute-start.17) | collective-permute-done | bytes 262176 | tf_op jit(solution)/shard_map/ppermute | solution.py:42
  105.4 1.1 copy-done.3
  109.8 13.5 %block_product.4 = (bf16[1024,128]{1,0:T(8,128)(2,1)S(1)}, bf16[1024,128]{1,0:T(8,128)(2,1)S(1)}, bf16[1024,128]{1,0:T(8,128)(2,1)S(1)}, bf16[1024,128]{1,0:T(8,128)(2,1)S(1)}) custom-call(s32[3,640]{1,0:T(4,128)S(1)} %pad_add_fusion.meta, bf16[2,32,128]{2,1,0:T(8,128)(2,1)S(1)} %broadcast_in_dim.16.masks, bf16[81,32,128]{2,1,0:T(8,128)(2,1)S(1)} %pad_maximum_fusion.refs_0_, ...), custom_call_target="tpu_custom_call" | custom-call | tf_op jit(solution)/shard_map/block_product/pallas_call | solution.py:111
  123.4 6.0 %collective-permute-start.21 = (bf16[1024,128]{1,0:T(8,128)(2,1)S(1)}, bf16[1024,128]{1,0:T(8,128)(2,1)S(1)}, u32[]{:S(2)}, u32[]{:S(2)}) collective-permute-start(bf16[1024,128]{1,0:T(8,128)(2,1)S(1)} %get-tuple-element.45), channel_id=1, source_target_pairs={{0,32},{1,5},{2,34},{3,7},{4,36},{5,1},{6,38},{7,3},{8,40},{9,13},... | collective-permute-start | bytes 786440 | tf_op jit(solution)/shard_map/ppermute | solution.py:42
  129.4 2.9 %collective-permute-done.20 = bf16[1024,128]{1,0:T(8,128)(2,1)S(1)} collective-permute-done((bf16[1024,128]{1,0:T(8,128)(2,1)S(1)}, bf16[1024,128]{1,0:T(8,128)(2,1)S(1)}, u32[]{:S(2)}, u32[]{:S(2)}) %collective-permute-start.20) | collective-permute-done | bytes 262176 | tf_op jit(solution)/shard_map/ppermute | solution.py:42
  132.3 4.3 %collective-permute-done.21 = bf16[1024,128]{1,0:T(8,128)(2,1)S(1)} collective-permute-done((bf16[1024,128]{1,0:T(8,128)(2,1)S(1)}, bf16[1024,128]{1,0:T(8,128)(2,1)S(1)}, u32[]{:S(2)}, u32[]{:S(2)}) %collective-permute-start.21) | collective-permute-done | bytes 262176 | tf_op jit(solution)/shard_map/ppermute | solution.py:42
  136.6 1.8 collective-permute-done.22
  138.8 1.9 collective-permute-start.23
  140.7 4.3 %collective-permute-done.25.refs_11_ = bf16[1024,128]{1,0:T(8,128)(2,1)S(1)} collective-permute-done((bf16[1024,128]{1,0:T(8,128)(2,1)S(1)}, bf16[1024,128]{1,0:T(8,128)(2,1)S(1)}, u32[]{:S(2)}, u32[]{:S(2)}) %collective-permute-start.25) | collective-permute-done | bytes 262176 | tf_op jit(solution)/shard_map/ppermute | solution.py:42
  145.0 1.7 collective-permute-done.24.refs_10_
  146.7 2.7 %collective-permute-done.23.refs_9_ = bf16[1024,128]{1,0:T(8,128)(2,1)S(1)} collective-permute-done((bf16[1024,128]{1,0:T(8,128)(2,1)S(1)}, bf16[1024,128]{1,0:T(8,128)(2,1)S(1)}, u32[]{:S(2)}, u32[]{:S(2)}) %collective-permute-start.23) | collective-permute-done | bytes 262176 | tf_op jit(solution)/shard_map/ppermute | solution.py:42
  149.4 13.5 %block_product.5 = (bf16[1024,128]{1,0:T(8,128)(2,1)S(1)}, bf16[1024,128]{1,0:T(8,128)(2,1)S(1)}, bf16[1024,128]{1,0:T(8,128)(2,1)S(1)}, bf16[1024,128]{1,0:T(8,128)(2,1)S(1)}) custom-call(s32[3,640]{1,0:T(4,128)S(1)} %pad_add_fusion.meta, bf16[2,32,128]{2,1,0:T(8,128)(2,1)S(1)} %broadcast_in_dim.16.masks, bf16[81,32,128]{2,1,0:T(8,128)(2,1)S(1)} %pad_maximum_fusion.refs_0_, ...), custom_call_target="tpu_custom_call" | custom-call | tf_op jit(solution)/shard_map/block_product/pallas_call | solution.py:111
  163.0 7.1 %collective-permute-start.27 = (bf16[1024,128]{1,0:T(8,128)(2,1)S(1)}, bf16[1024,128]{1,0:T(8,128)(2,1)S(1)}, u32[]{:S(2)}, u32[]{:S(2)}) collective-permute-start(bf16[1024,128]{1,0:T(8,128)(2,1)S(1)} %get-tuple-element.49), channel_id=1, source_target_pairs={{0,32},{1,5},{2,34},{3,7},{4,36},{5,1},{6,38},{7,3},{8,40},{9,13},... | collective-permute-start | bytes 786440 | tf_op jit(solution)/shard_map/ppermute | solution.py:42
  170.2 2.9 %collective-permute-done.26 = bf16[1024,128]{1,0:T(8,128)(2,1)S(1)} collective-permute-done((bf16[1024,128]{1,0:T(8,128)(2,1)S(1)}, bf16[1024,128]{1,0:T(8,128)(2,1)S(1)}, u32[]{:S(2)}, u32[]{:S(2)}) %collective-permute-start.26) | collective-permute-done | bytes 262176 | tf_op jit(solution)/shard_map/ppermute | solution.py:42
  173.0 4.3 %collective-permute-done.27 = bf16[1024,128]{1,0:T(8,128)(2,1)S(1)} collective-permute-done((bf16[1024,128]{1,0:T(8,128)(2,1)S(1)}, bf16[1024,128]{1,0:T(8,128)(2,1)S(1)}, u32[]{:S(2)}, u32[]{:S(2)}) %collective-permute-start.27) | collective-permute-done | bytes 262176 | tf_op jit(solution)/shard_map/ppermute | solution.py:42
  177.7 2.1 collective-permute-start.30
  179.9 2.5 %collective-permute-start.29 = (bf16[256,128]{1,0:T(8,128)(2,1)S(1)}, bf16[256,128]{1,0:T(8,128)(2,1)S(1)}, u32[]{:S(2)}, u32[]{:S(2)}) collective-permute-start(bf16[256,128]{1,0:T(8,128)(2,1)S(1)} %get-tuple-element.65), channel_id=1, source_target_pairs={{0,72},{1,73},{2,74},{3,75},{4,76},{5,77},{6,78},{7,79},{8,64},{9,... | collective-permute-start | bytes 196616 | tf_op jit(solution)/shard_map/ppermute | solution.py:42
  182.4 1.5 collective-permute-done.31
  187.2 1.5 copy.47
  190.5 2.8 %fusion.3 = bf16[16,8,8,128]{3,1,2,0:T(8,128)(2,1)S(1)} fusion(bf16[512,128]{0,1:T(8,128)(2,1)S(1)} %bitcast.105, f32[512,1024]{1,0:T(8,128)} %get-tuple-element.75, bf16[1024,256]{1,0:T(8,128)(2,1)} %param.13, bf16[512,256]{1,0:T(8,128)(2,1)S(1)} %collective-permute-done.32, bf16[512,256]{1,0:T(8,128)(2,1)S(1)} %reshape.1111, pred[]{:T(512)S(6)} %eq.40), kind=kOutput, calls=%fused_computation.10 | convolution fusion | flops 407633920 | bytes 3538945 | tf_op jit(solution)/shard_map/dot_general | solution.py:247
  194.3 9.4 %all-to-all-start = ((bf16[64,32,128]{2,1,0:T(8,128)(2,1)}), bf16[64,32,128]{2,1,0:T(8,128)(2,1)S(1)}, u32[]{:S(2)}, u32[]{:S(2)}) async-start(bf16[64,32,128]{2,1,0:T(8,128)(2,1)} %pad_maximum_fusion.2), calls=%async_computation | async-start | bytes 1048576 | tf_op jit(solution)/shard_map/all_to_all | solution.py:252
  204.3 13.1 %all-to-all-done = bf16[64,32,128]{2,1,0:T(8,128)(2,1)S(1)} async-done(((bf16[64,32,128]{2,1,0:T(8,128)(2,1)}), bf16[64,32,128]{2,1,0:T(8,128)(2,1)S(1)}, u32[]{:S(2)}, u32[]{:S(2)}) %all-to-all-start) | async-done | bytes 524320 | tf_op jit(solution)/shard_map/all_to_all | solution.py:252
  219.0 2.3 collective-permute-done.33
  222.4 1.6 collective-permute-start.35
  225.2 2.5 %collective-permute-done.35 = f32[2,32,128]{2,1,0:T(8,128)S(1)} collective-permute-done((f32[2,32,128]{2,1,0:T(8,128)S(1)}, f32[2,32,128]{2,1,0:T(8,128)S(1)}, u32[]{:S(2)}, u32[]{:S(2)}) %collective-permute-start.35) | collective-permute-done | bytes 32800 | tf_op jit(solution)/shard_map/ppermute | solution.py:42
  227.8 1.4 collective-permute-done.34
  (181 shorter events, 36.9 us)
Async XLA Ops:
  0.6 14.1 %copy-start = (bf16[256,1024]{1,0:T(8,128)(2,1)S(1)}, bf16[256,1024]{1,0:T(8,128)(2,1)}, u32[]{:S(2)}) copy-start(bf16[256,1024]{1,0:T(8,128)(2,1)} %param.12) | copy-start | bytes 1572868
  5.0 5.9 %copy-start.22 = (bf16[1,256,256]{2,1,0:T(8,128)(2,1)S(1)}, bf16[1,256,256]{2,1,0:T(8,128)(2,1)}, u32[]{:S(2)}) copy-start(bf16[1,256,256]{2,1,0:T(8,128)(2,1)} %param.14) | copy-start | bytes 393220
  5.0 5.9 %copy-start.23 = (bf16[1,256,256]{2,1,0:T(8,128)(2,1)S(1)}, bf16[1,256,256]{2,1,0:T(8,128)(2,1)}, u32[]{:S(2)}) copy-start(bf16[1,256,256]{2,1,0:T(8,128)(2,1)} %param.11) | copy-start | bytes 393220
  5.8 42.9 %collective-permute-start.3 = (bf16[81,32,128]{2,1,0:T(8,128)(2,1)S(1)}, bf16[81,32,128]{2,1,0:T(8,128)(2,1)S(1)}, u32[]{:S(2)}, u32[]{:S(2)}) collective-permute-start(bf16[81,32,128]{2,1,0:T(8,128)(2,1)S(1)} %pad_maximum_fusion.refs_0_), channel_id=1, source_target_pairs={{0,8},{1,9},{2,10},{3,11},{4,12},{5,13},{6,14},{7,15},{8,0},{9,1},... | collective-permute-start | bytes 1990664 | tf_op jit(solution)/shard_map/ppermute | solution.py:42
  9.8 30.6 %collective-permute-start.1 = (bf16[81,32,128]{2,1,0:T(8,128)(2,1)S(1)}, bf16[81,32,128]{2,1,0:T(8,128)(2,1)S(1)}, u32[]{:S(2)}, u32[]{:S(2)}) collective-permute-start(bf16[81,32,128]{2,1,0:T(8,128)(2,1)S(1)} %pad_maximum_fusion.refs_0_), channel_id=1, source_target_pairs={{0,64},{1,65},{2,66},{3,67},{4,68},{5,69},{6,70},{7,71},{8,72},{9,... | collective-permute-start | bytes 1990664 | tf_op jit(solution)/shard_map/ppermute | solution.py:42
  10.8 38.7 %collective-permute-start = (bf16[81,32,128]{2,1,0:T(8,128)(2,1)S(1)}, bf16[81,32,128]{2,1,0:T(8,128)(2,1)S(1)}, u32[]{:S(2)}, u32[]{:S(2)}) collective-permute-start(bf16[81,32,128]{2,1,0:T(8,128)(2,1)S(1)} %pad_maximum_fusion.refs_0_), channel_id=1, source_target_pairs={{0,1},{1,0},{2,3},{3,2},{4,5},{5,4},{6,7},{7,6},{8,9},{9,8},{10,11... | collective-permute-start | bytes 1990664 | tf_op jit(solution)/shard_map/ppermute | solution.py:42
  11.6 2.1 collective-permute-start.7
  21.9 27.7 %copy-start.25 = (bf16[8,32,128]{2,1,0:T(8,128)(2,1)S(1)}, bf16[8,32,128]{2,1,0:T(8,128)(2,1)}, u32[]{:S(2)}) copy-start(bf16[8,32,128]{2,1,0:T(8,128)(2,1)} %constant_dynamic-update-slice_fusion.7) | copy-start | bytes 196612
  23.4 5.5 %collective-permute-start.10 = (bf16[256,128]{1,0:T(8,128)(2,1)S(1)}, bf16[256,128]{1,0:T(8,128)(2,1)S(1)}, u32[]{:S(2)}, u32[]{:S(2)}) collective-permute-start(bf16[256,128]{1,0:T(8,128)(2,1)S(1)} %get-tuple-element.67), channel_id=1, source_target_pairs={{0,72},{1,73},{2,74},{3,75},{4,76},{5,77},{6,78},{7,79},{8,64},{9,... | collective-permute-start | bytes 196616 | tf_op jit(solution)/shard_map/ppermute | solution.py:42
  25.7 14.7 %collective-permute-start.9 = (bf16[256,128]{1,0:T(8,128)(2,1)S(1)}, bf16[256,128]{1,0:T(8,128)(2,1)S(1)}, u32[]{:S(2)}, u32[]{:S(2)}) collective-permute-start(bf16[256,128]{1,0:T(8,128)(2,1)S(1)} %get-tuple-element.68), channel_id=1, source_target_pairs={{0,8},{1,9},{2,10},{3,11},{4,12},{5,13},{6,14},{7,15},{8,0},{9,1},... | collective-permute-start | bytes 196616 | tf_op jit(solution)/shard_map/ppermute | solution.py:42
  29.0 25.1 %copy-start.16 = (bf16[256,128]{1,0:T(8,128)(2,1)}, bf16[256,128]{1,0:T(8,128)(2,1)S(1)}, u32[]{:S(2)}) copy-start(bf16[256,128]{1,0:T(8,128)(2,1)S(1)} %collective-permute-done.10) | copy-start | bytes 196612
  29.0 20.6 %collective-permute-start.5 = (bf16[81,32,128]{2,1,0:T(8,128)(2,1)S(1)}, bf16[81,32,128]{2,1,0:T(8,128)(2,1)S(1)}, u32[]{:S(2)}, u32[]{:S(2)}) collective-permute-start(bf16[81,32,128]{2,1,0:T(8,128)(2,1)S(1)} %pad_maximum_fusion.refs_0_), channel_id=1, source_target_pairs={{0,72},{1,73},{2,74},{3,75},{4,76},{5,77},{6,78},{7,79},{8,64},{9,... | collective-permute-start | bytes 1990664 | tf_op jit(solution)/shard_map/ppermute | solution.py:42
  40.4 14.5 %copy-start.18 = (bf16[256,128]{1,0:T(8,128)(2,1)}, bf16[256,128]{1,0:T(8,128)(2,1)S(1)}, u32[]{:S(2)}) copy-start(bf16[256,128]{1,0:T(8,128)(2,1)S(1)} %collective-permute-done.9) | copy-start | bytes 196612
  40.4 5.5 %collective-permute-start.8 = (bf16[256,128]{1,0:T(8,128)(2,1)S(1)}, bf16[256,128]{1,0:T(8,128)(2,1)S(1)}, u32[]{:S(2)}, u32[]{:S(2)}) collective-permute-start(bf16[256,128]{1,0:T(8,128)(2,1)S(1)} %get-tuple-element.69), channel_id=1, source_target_pairs={{0,64},{1,65},{2,66},{3,67},{4,68},{5,69},{6,70},{7,71},{8,72},{9,... | collective-permute-start | bytes 196616 | tf_op jit(solution)/shard_map/ppermute | solution.py:42
  40.4 10.1 %collective-permute-start.2 = (bf16[81,32,128]{2,1,0:T(8,128)(2,1)S(1)}, bf16[81,32,128]{2,1,0:T(8,128)(2,1)S(1)}, u32[]{:S(2)}, u32[]{:S(2)}) collective-permute-start(bf16[81,32,128]{2,1,0:T(8,128)(2,1)S(1)} %collective-permute-done.1.refs_2_), channel_id=1, source_target_pairs={{0,1},{1,0},{2,3},{3,2},{4,5},{5,4},{6,7},{7,6},{8,9},{9,8},{10,11... | collective-permute-start | bytes 1990664 | tf_op jit(solution)/shard_map/ppermute | solution.py:42
  45.9 9.1 %copy-start.20 = (bf16[256,128]{1,0:T(8,128)(2,1)}, bf16[256,128]{1,0:T(8,128)(2,1)S(1)}, u32[]{:S(2)}) copy-start(bf16[256,128]{1,0:T(8,128)(2,1)S(1)} %collective-permute-done.8) | copy-start | bytes 196612
  45.9 10.1 %collective-permute-start.13 = (bf16[1024,128]{1,0:T(8,128)(2,1)S(1)}, bf16[1024,128]{1,0:T(8,128)(2,1)}, u32[]{:S(2)}, u32[]{:S(2)}) collective-permute-start(bf16[1024,128]{1,0:T(8,128)(2,1)S(1)} %pad_maximum_fusion.5.refs_8_), channel_id=1, source_target_pairs={{0,6},{1,49},{2,0},{3,51},{4,2},{5,53},{6,4},{7,55},{8,14},{9,57},... | collective-permute-start | bytes 786440 | tf_op jit(solution)/shard_map/ppermute | solution.py:42
  48.7 8.1 %collective-permute-start.12 = (bf16[1024,128]{1,0:T(8,128)(2,1)S(1)}, bf16[1024,128]{1,0:T(8,128)(2,1)}, u32[]{:S(2)}, u32[]{:S(2)}) collective-permute-start(bf16[1024,128]{1,0:T(8,128)(2,1)S(1)} %pad_maximum_fusion.5.refs_8_), channel_id=1, source_target_pairs={{0,4},{1,33},{2,6},{3,35},{4,0},{5,37},{6,2},{7,39},{8,12},{9,41},... | collective-permute-start | bytes 786440 | tf_op jit(solution)/shard_map/ppermute | solution.py:42
  49.5 2.8 %collective-permute-start.4 = (bf16[81,32,128]{2,1,0:T(8,128)(2,1)S(1)}, bf16[81,32,128]{2,1,0:T(8,128)(2,1)S(1)}, u32[]{:S(2)}, u32[]{:S(2)}) collective-permute-start(bf16[81,32,128]{2,1,0:T(8,128)(2,1)S(1)} %collective-permute-done.3.refs_4_), channel_id=1, source_target_pairs={{0,1},{1,0},{2,3},{3,2},{4,5},{5,4},{6,7},{7,6},{8,9},{9,8},{10,11... | collective-permute-start | bytes 1990664 | tf_op jit(solution)/shard_map/ppermute | solution.py:42
  49.6 9.9 %collective-permute-start.11 = (bf16[1024,128]{1,0:T(8,128)(2,1)S(1)}, bf16[1024,128]{1,0:T(8,128)(2,1)}, u32[]{:S(2)}, u32[]{:S(2)}) collective-permute-start(bf16[1024,128]{1,0:T(8,128)(2,1)S(1)} %pad_maximum_fusion.5.refs_8_), channel_id=1, source_target_pairs={{0,2},{1,17},{2,4},{3,19},{4,6},{5,21},{6,0},{7,23},{8,10},{9,25},... | collective-permute-start | bytes 786440 | tf_op jit(solution)/shard_map/ppermute | solution.py:42
  50.5 3.5 %collective-permute-start.6 = (bf16[81,32,128]{2,1,0:T(8,128)(2,1)S(1)}, bf16[81,32,128]{2,1,0:T(8,128)(2,1)S(1)}, u32[]{:S(2)}, u32[]{:S(2)}) collective-permute-start(bf16[81,32,128]{2,1,0:T(8,128)(2,1)S(1)} %collective-permute-done.5.refs_6_), channel_id=1, source_target_pairs={{0,1},{1,0},{2,3},{3,2},{4,5},{5,4},{6,7},{7,6},{8,9},{9,8},{10,11... | collective-permute-start | bytes 1990664 | tf_op jit(solution)/shard_map/ppermute | solution.py:42
  78.9 9.9 %collective-permute-start.14 = (bf16[1024,128]{1,0:T(8,128)(2,1)}, bf16[1024,128]{1,0:T(8,128)(2,1)S(1)}, u32[]{:S(2)}, u32[]{:S(2)}) collective-permute-start(bf16[1024,128]{1,0:T(8,128)(2,1)} %get-tuple-element.40), channel_id=1, source_target_pairs={{0,16},{1,3},{2,18},{3,5},{4,20},{5,7},{6,22},{7,1},{8,24},{9,11},... | collective-permute-start | bytes 786440 | tf_op jit(solution)/shard_map/ppermute | solution.py:42
  78.9 14.3 %collective-permute-start.15 = (bf16[1024,128]{1,0:T(8,128)(2,1)}, bf16[1024,128]{1,0:T(8,128)(2,1)}, u32[]{:S(2)}, u32[]{:S(2)}) collective-permute-start(bf16[1024,128]{1,0:T(8,128)(2,1)} %get-tuple-element.41), channel_id=1, source_target_pairs={{0,32},{1,5},{2,34},{3,7},{4,36},{5,1},{6,38},{7,3},{8,40},{9,13},... | collective-permute-start | bytes 786440 | tf_op jit(solution)/shard_map/ppermute | solution.py:42
  85.7 7.5 %collective-permute-start.16 = (bf16[1024,128]{1,0:T(8,128)(2,1)}, bf16[1024,128]{1,0:T(8,128)(2,1)}, u32[]{:S(2)}, u32[]{:S(2)}) collective-permute-start(bf16[1024,128]{1,0:T(8,128)(2,1)} %get-tuple-element.42), channel_id=1, source_target_pairs={{0,48},{1,7},{2,50},{3,1},{4,52},{5,3},{6,54},{7,5},{8,56},{9,15},... | collective-permute-start | bytes 786440 | tf_op jit(solution)/shard_map/ppermute | solution.py:42
  93.2 45.1 %copy-start.17 = (bf16[256,128]{1,0:T(8,128)(2,1)S(1)}, bf16[256,128]{1,0:T(8,128)(2,1)}, u32[]{:S(2)}) copy-start(bf16[256,128]{1,0:T(8,128)(2,1)} %copy-done.16) | copy-start | bytes 196612
  93.2 45.1 %copy-start.19 = (bf16[256,128]{1,0:T(8,128)(2,1)S(1)}, bf16[256,128]{1,0:T(8,128)(2,1)}, u32[]{:S(2)}) copy-start(bf16[256,128]{1,0:T(8,128)(2,1)} %copy-done.18) | copy-start | bytes 196612
  93.2 45.1 %copy-start.21 = (bf16[256,128]{1,0:T(8,128)(2,1)S(1)}, bf16[256,128]{1,0:T(8,128)(2,1)}, u32[]{:S(2)}) copy-start(bf16[256,128]{1,0:T(8,128)(2,1)} %copy-done.20) | copy-start | bytes 196612
  94.6 6.4 %collective-permute-start.19 = (bf16[1024,128]{1,0:T(8,128)(2,1)S(1)}, bf16[1024,128]{1,0:T(8,128)(2,1)S(1)}, u32[]{:S(2)}, u32[]{:S(2)}) collective-permute-start(bf16[1024,128]{1,0:T(8,128)(2,1)S(1)} %fusion.8.refs_8_), channel_id=1, source_target_pairs={{0,6},{1,49},{2,0},{3,51},{4,2},{5,53},{6,4},{7,55},{8,14},{9,57},... | collective-permute-start | bytes 786440 | tf_op jit(solution)/shard_map/ppermute | solution.py:42
  94.7 8.1 %collective-permute-start.18 = (bf16[1024,128]{1,0:T(8,128)(2,1)S(1)}, bf16[1024,128]{1,0:T(8,128)(2,1)S(1)}, u32[]{:S(2)}, u32[]{:S(2)}) collective-permute-start(bf16[1024,128]{1,0:T(8,128)(2,1)S(1)} %fusion.8.refs_8_), channel_id=1, source_target_pairs={{0,4},{1,33},{2,6},{3,35},{4,0},{5,37},{6,2},{7,39},{8,12},{9,41},... | collective-permute-start | bytes 786440 | tf_op jit(solution)/shard_map/ppermute | solution.py:42
  94.8 10.7 %collective-permute-start.17 = (bf16[1024,128]{1,0:T(8,128)(2,1)S(1)}, bf16[1024,128]{1,0:T(8,128)(2,1)S(1)}, u32[]{:S(2)}, u32[]{:S(2)}) collective-permute-start(bf16[1024,128]{1,0:T(8,128)(2,1)S(1)} %fusion.8.refs_8_), channel_id=1, source_target_pairs={{0,2},{1,17},{2,4},{3,19},{4,6},{5,21},{6,0},{7,23},{8,10},{9,25},... | collective-permute-start | bytes 786440 | tf_op jit(solution)/shard_map/ppermute | solution.py:42
  123.3 9.0 %collective-permute-start.20 = (bf16[1024,128]{1,0:T(8,128)(2,1)S(1)}, bf16[1024,128]{1,0:T(8,128)(2,1)S(1)}, u32[]{:S(2)}, u32[]{:S(2)}) collective-permute-start(bf16[1024,128]{1,0:T(8,128)(2,1)S(1)} %get-tuple-element.44), channel_id=1, source_target_pairs={{0,16},{1,3},{2,18},{3,5},{4,20},{5,7},{6,22},{7,1},{8,24},{9,11},... | collective-permute-start | bytes 786440 | tf_op jit(solution)/shard_map/ppermute | solution.py:42
  123.4 13.2 %collective-permute-start.21 = (bf16[1024,128]{1,0:T(8,128)(2,1)S(1)}, bf16[1024,128]{1,0:T(8,128)(2,1)S(1)}, u32[]{:S(2)}, u32[]{:S(2)}) collective-permute-start(bf16[1024,128]{1,0:T(8,128)(2,1)S(1)} %get-tuple-element.45), channel_id=1, source_target_pairs={{0,32},{1,5},{2,34},{3,7},{4,36},{5,1},{6,38},{7,3},{8,40},{9,13},... | collective-permute-start | bytes 786440 | tf_op jit(solution)/shard_map/ppermute | solution.py:42
  129.4 8.9 %collective-permute-start.22 = (bf16[1024,128]{1,0:T(8,128)(2,1)S(1)}, bf16[1024,128]{1,0:T(8,128)(2,1)S(1)}, u32[]{:S(2)}, u32[]{:S(2)}) collective-permute-start(bf16[1024,128]{1,0:T(8,128)(2,1)S(1)} %get-tuple-element.46), channel_id=1, source_target_pairs={{0,48},{1,7},{2,50},{3,1},{4,52},{5,3},{6,54},{7,5},{8,56},{9,15},... | collective-permute-start | bytes 786440 | tf_op jit(solution)/shard_map/ppermute | solution.py:42
  138.6 6.4 %collective-permute-start.25 = (bf16[1024,128]{1,0:T(8,128)(2,1)S(1)}, bf16[1024,128]{1,0:T(8,128)(2,1)S(1)}, u32[]{:S(2)}, u32[]{:S(2)}) collective-permute-start(bf16[1024,128]{1,0:T(8,128)(2,1)S(1)} %fusion.9.refs_8_), channel_id=1, source_target_pairs={{0,6},{1,49},{2,0},{3,51},{4,2},{5,53},{6,4},{7,55},{8,14},{9,57},... | collective-permute-start | bytes 786440 | tf_op jit(solution)/shard_map/ppermute | solution.py:42
  138.7 8.1 %collective-permute-start.24 = (bf16[1024,128]{1,0:T(8,128)(2,1)S(1)}, bf16[1024,128]{1,0:T(8,128)(2,1)S(1)}, u32[]{:S(2)}, u32[]{:S(2)}) collective-permute-start(bf16[1024,128]{1,0:T(8,128)(2,1)S(1)} %fusion.9.refs_8_), channel_id=1, source_target_pairs={{0,4},{1,33},{2,6},{3,35},{4,0},{5,37},{6,2},{7,39},{8,12},{9,41},... | collective-permute-start | bytes 786440 | tf_op jit(solution)/shard_map/ppermute | solution.py:42
  138.8 10.7 %collective-permute-start.23 = (bf16[1024,128]{1,0:T(8,128)(2,1)S(1)}, bf16[1024,128]{1,0:T(8,128)(2,1)S(1)}, u32[]{:S(2)}, u32[]{:S(2)}) collective-permute-start(bf16[1024,128]{1,0:T(8,128)(2,1)S(1)} %fusion.9.refs_8_), channel_id=1, source_target_pairs={{0,2},{1,17},{2,4},{3,19},{4,6},{5,21},{6,0},{7,23},{8,10},{9,25},... | collective-permute-start | bytes 786440 | tf_op jit(solution)/shard_map/ppermute | solution.py:42
  162.9 10.1 %collective-permute-start.26 = (bf16[1024,128]{1,0:T(8,128)(2,1)S(1)}, bf16[1024,128]{1,0:T(8,128)(2,1)S(1)}, u32[]{:S(2)}, u32[]{:S(2)}) collective-permute-start(bf16[1024,128]{1,0:T(8,128)(2,1)S(1)} %get-tuple-element.48), channel_id=1, source_target_pairs={{0,16},{1,3},{2,18},{3,5},{4,20},{5,7},{6,22},{7,1},{8,24},{9,11},... | collective-permute-start | bytes 786440 | tf_op jit(solution)/shard_map/ppermute | solution.py:42
  163.0 14.3 %collective-permute-start.27 = (bf16[1024,128]{1,0:T(8,128)(2,1)S(1)}, bf16[1024,128]{1,0:T(8,128)(2,1)S(1)}, u32[]{:S(2)}, u32[]{:S(2)}) collective-permute-start(bf16[1024,128]{1,0:T(8,128)(2,1)S(1)} %get-tuple-element.49), channel_id=1, source_target_pairs={{0,32},{1,5},{2,34},{3,7},{4,36},{5,1},{6,38},{7,3},{8,40},{9,13},... | collective-permute-start | bytes 786440 | tf_op jit(solution)/shard_map/ppermute | solution.py:42
  170.2 7.2 %collective-permute-start.28 = (bf16[1024,128]{1,0:T(8,128)(2,1)S(1)}, bf16[1024,128]{1,0:T(8,128)(2,1)S(1)}, u32[]{:S(2)}, u32[]{:S(2)}) collective-permute-start(bf16[1024,128]{1,0:T(8,128)(2,1)S(1)} %get-tuple-element.50), channel_id=1, source_target_pairs={{0,48},{1,7},{2,50},{3,1},{4,52},{5,3},{6,54},{7,5},{8,56},{9,15},... | collective-permute-start | bytes 786440 | tf_op jit(solution)/shard_map/ppermute | solution.py:42
  177.7 6.2 %collective-permute-start.31 = (bf16[256,128]{1,0:T(8,128)(2,1)S(1)}, bf16[256,128]{1,0:T(8,128)(2,1)S(1)}, u32[]{:S(2)}, u32[]{:S(2)}) collective-permute-start(bf16[256,128]{1,0:T(8,128)(2,1)S(1)} %get-tuple-element.63), channel_id=1, source_target_pairs={{0,64},{1,65},{2,66},{3,67},{4,68},{5,69},{6,70},{7,71},{8,72},{9,... | collective-permute-start | bytes 196616 | tf_op jit(solution)/shard_map/ppermute | solution.py:42
  177.7 6.2 %collective-permute-start.30 = (bf16[256,128]{1,0:T(8,128)(2,1)S(1)}, bf16[256,128]{1,0:T(8,128)(2,1)S(1)}, u32[]{:S(2)}, u32[]{:S(2)}) collective-permute-start(bf16[256,128]{1,0:T(8,128)(2,1)S(1)} %get-tuple-element.64), channel_id=1, source_target_pairs={{0,8},{1,9},{2,10},{3,11},{4,12},{5,13},{6,14},{7,15},{8,0},{9,1},... | collective-permute-start | bytes 196616 | tf_op jit(solution)/shard_map/ppermute | solution.py:42
  179.9 4.9 %collective-permute-start.29 = (bf16[256,128]{1,0:T(8,128)(2,1)S(1)}, bf16[256,128]{1,0:T(8,128)(2,1)S(1)}, u32[]{:S(2)}, u32[]{:S(2)}) collective-permute-start(bf16[256,128]{1,0:T(8,128)(2,1)S(1)} %get-tuple-element.65), channel_id=1, source_target_pairs={{0,72},{1,73},{2,74},{3,75},{4,76},{5,77},{6,78},{7,79},{8,64},{9,... | collective-permute-start | bytes 196616 | tf_op jit(solution)/shard_map/ppermute | solution.py:42
  187.0 2.7 %collective-permute-start.32 = (bf16[512,256]{1,0:T(8,128)(2,1)S(1)}, bf16[512,256]{1,0:T(8,128)(2,1)S(1)}, u32[]{:S(2)}, u32[]{:S(2)}) collective-permute-start(bf16[512,256]{1,0:T(8,128)(2,1)S(1)} %reshape.1111), channel_id=1, source_target_pairs={{0,1},{1,0},{2,3},{3,2},{4,5},{5,4},{6,7},{7,6},{8,9},{9,8},{10,11... | collective-permute-start | bytes 786440 | tf_op jit(solution)/shard_map/ppermute | solution.py:42
  194.3 23.1 %all-to-all-start = ((bf16[64,32,128]{2,1,0:T(8,128)(2,1)}), bf16[64,32,128]{2,1,0:T(8,128)(2,1)S(1)}, u32[]{:S(2)}, u32[]{:S(2)}) async-start(bf16[64,32,128]{2,1,0:T(8,128)(2,1)} %pad_maximum_fusion.2), calls=%async_computation | async-start | bytes 1048576 | tf_op jit(solution)/shard_map/all_to_all | solution.py:252
  217.5 3.8 %collective-permute-start.33 = (f32[32,128]{1,0:T(8,128)S(1)}, f32[32,128]{1,0:T(8,128)S(1)}, u32[]{:S(2)}, u32[]{:S(2)}) collective-permute-start(f32[32,128]{1,0:T(8,128)S(1)} %convert_reduce_fusion), channel_id=1, source_target_pairs={{0,64},{1,65},{2,66},{3,67},{4,68},{5,69},{6,70},{7,71},{8,72},{9,... | collective-permute-start | bytes 49160 | tf_op jit(solution)/shard_map/ppermute | solution.py:42
  221.3 3.9 %collective-permute-start.36 = (f32[2,32,128]{2,1,0:T(8,128)S(1)}, f32[2,32,128]{2,1,0:T(8,128)S(1)}, u32[]{:S(2)}, u32[]{:S(2)}) collective-permute-start(f32[2,32,128]{2,1,0:T(8,128)S(1)} %maximum_select_fusion.3), channel_id=1, source_target_pairs={{0,48},{1,49},{2,50},{3,51},{4,52},{5,53},{6,54},{7,55},{8,56},{9,... | collective-permute-start | bytes 98312 | tf_op jit(solution)/shard_map/ppermute | solution.py:42
  222.4 5.4 %collective-permute-start.35 = (f32[2,32,128]{2,1,0:T(8,128)S(1)}, f32[2,32,128]{2,1,0:T(8,128)S(1)}, u32[]{:S(2)}, u32[]{:S(2)}) collective-permute-start(f32[2,32,128]{2,1,0:T(8,128)S(1)} %maximum_select_fusion.3), channel_id=1, source_target_pairs={{0,32},{1,33},{2,34},{3,35},{4,36},{5,37},{6,38},{7,39},{8,40},{9,... | collective-permute-start | bytes 98312 | tf_op jit(solution)/shard_map/ppermute | solution.py:42
  224.0 5.1 %collective-permute-start.34 = (f32[2,32,128]{2,1,0:T(8,128)S(1)}, f32[2,32,128]{2,1,0:T(8,128)S(1)}, u32[]{:S(2)}, u32[]{:S(2)}) collective-permute-start(f32[2,32,128]{2,1,0:T(8,128)S(1)} %maximum_select_fusion.3), channel_id=1, source_target_pairs={{0,16},{1,17},{2,18},{3,19},{4,20},{5,21},{6,22},{7,23},{8,24},{9,... | collective-permute-start | bytes 98312 | tf_op jit(solution)/shard_map/ppermute | solution.py:42
  (17 other events, 19.6 us)

commit v3 on v2

v3 whole, which is shorter than its diff:
```python
import functools

import jax
import jax.numpy as jnp
import numpy as np
from jax import lax
from jax.experimental import pallas as pl
from jax.experimental.pallas import tpu as pltpu
from jax.sharding import Mesh
from jax.sharding import PartitionSpec as P

STEPS = 3
ALPHA = 0.1
AXES = ("zl", "y", "zh", "x", "c")
SIZES = (2, 4, 2, 4, 2)
LOOP = ("zl", "y")
WIDE = ("zh", "x", "c")
BLK = 64
DIM = 256
ITEMS = 256
PIECE = 2 * ITEMS
SLOTS = 80
PACK = 32
LANES = 128
STATE = 1024
GRAPH = 4 * STATE
TILES = 8
GROUP = 32
LIST = TILES * SLOTS + 2 * GROUP


def permutation(move):
    pairs = []
    for source in range(int(np.prod(SIZES))):
        place = dict(zip(AXES, np.unravel_index(source, SIZES)))
        place = {name: int(value) for name, value in place.items()}
        place.update(move(place))
        pairs.append((source, int(np.ravel_multi_index([place[name] for name in AXES], SIZES))))
    return pairs


def send(value, move):
    return lax.ppermute(value, AXES, permutation(move))


def core_move(place):
    return {"c": 1 - place["c"]}


def z_move(step, place):
    spot = (2 * place["zh"] + place["zl"] + step) % 4
    return {"zh": spot // 2, "zl": spot % 2}


def relay_move(place):
    return z_move(3 if place["c"] else 1, place)


def gather_ring(step, place):
    return {"y": (place["y"] + step) % 4} if place["c"] else {"x": (place["x"] + step) % 4}


def scatter_ring(step, place):
    return {"x": (place["x"] + step) % 4} if place["c"] else {"y": (place["y"] + step) % 4}


def start_kernel(place, own, other, w_first, w_second, out):
    core, spot = place[0], place[1]
    for tile in range(2):
        rows = jnp.where(core == tile, own[...], other[...])
        pre_act = jnp.dot(rows[:ITEMS], w_first[...], preferred_element_type=jnp.float32)
        hidden = (pre_act / (1.0 + jnp.exp(-pre_act))).astype(jnp.bfloat16)
        teleport = jnp.dot(hidden, w_second[...], preferred_element_type=jnp.float32)
        straight = jnp.where(core == 0, teleport, rows[ITEMS:PIECE].astype(jnp.float32).T)
        for corner in range(4):
            pieces = []
            for block in range(4):
                low, high = block * BLK, corner * BLK
                first = jnp.where(core == 0, straight[low : low + BLK, high : high + BLK], straight[high : high + BLK, low : low + BLK])
                pieces.append(jnp.concatenate([first[:PACK], first[PACK:]], axis=1))
            spread = jnp.concatenate(pieces, axis=0).astype(jnp.bfloat16)
            out[(corner - spot) % 4, tile * ITEMS // 2 : (tile + 1) * ITEMS // 2, :] = spread
    for hop in range(4):
        out[hop, ITEMS : ITEMS + 16, :] = own[PIECE:, :LANES]
        out[hop, ITEMS + 16 :, :] = other[PIECE:, :LANES]


def start_pieces(place, own, other, w_first, w_second):
    return pl.pallas_call(
        start_kernel,
        out_shape=jax.ShapeDtypeStruct((4, 9 * PACK, LANES), jnp.bfloat16),
        in_specs=[pl.BlockSpec(memory_space=pltpu.SMEM)] + [pl.BlockSpec(memory_space=pltpu.VMEM)] * 4,
        out_specs=pl.BlockSpec(memory_space=pltpu.VMEM),
        compiler_params=pltpu.CompilerParams(vmem_limit_bytes=24 * 2**20),
        name="start_pieces",
    )(place, own, other, w_first, w_second)


def product_kernel(meta, masks, *refs):
    tiles, parts, outs = refs[:TILES], refs[TILES : TILES + 4], refs[TILES + 4 : TILES + 8]
    values, gathered, sums, sems = refs[TILES + 8 :]
    part_copies = [
        pltpu.make_async_copy(part, gathered.at[pl.ds(index * STATE, STATE)], sems.at[TILES + index])
        for index, part in enumerate(parts)
    ]
    tile_copies = [
        pltpu.make_async_copy(tile, values.at[pl.ds(index * SLOTS * PACK, SLOTS * PACK)], sems.at[index])
        for index, tile in enumerate(tiles)
    ]
    for copy in tile_copies[: TILES // 2] + part_copies + tile_copies[TILES // 2 :]:
        copy.start()
    sums[...] = jnp.zeros_like(sums)
    adjoint = meta[3, 2]
    left, right = masks[0], masks[1]

    def group(index, carry):
        first = index * GROUP
        products = []
        for lane in range(GROUP):
            entries = values[pl.ds(pl.multiple_of(meta[2, first + lane], PACK), PACK), :]
            source = pl.multiple_of(meta[0, first + lane], PACK)
            vectors = gathered[pl.ds(source, PACK), :]
            rows = jnp.where(adjoint == 0, entries, vectors)
            cols = jnp.where(adjoint == 0, vectors, entries)
            turned = pltpu.roll(cols, BLK, 1)
            spread = jnp.concatenate([cols * left, turned * left, turned * right, cols * right], axis=0)
            products.append(jnp.dot(rows, spread, preferred_element_type=jnp.float32))
        for lane in range(GROUP):
            target = pl.multiple_of(meta[1, first + lane], PACK)
            sums[pl.ds(target, PACK), :] += products[lane]
        return carry

    early = meta[3, 0] // GROUP
    total = (meta[3, 1] + GROUP - 1) // GROUP
    for copy in tile_copies[: TILES // 2] + part_copies:
        copy.wait()
    lax.fori_loop(0, early, group, 0)
    for copy in tile_copies[TILES // 2 :]:
        copy.wait()
    lax.fori_loop(early, total, group, 0)
    for index, out in enumerate(outs):
        out[...] = sums[index * STATE : (index + 1) * STATE, :].astype(out.dtype)


def block_product(meta, masks, tiles, parts):
    piece = jax.ShapeDtypeStruct((STATE, LANES), jnp.bfloat16)
    return pl.pallas_call(
        product_kernel,
        out_shape=(piece,) * 4,
        in_specs=[
            pl.BlockSpec(memory_space=pltpu.SMEM),
            pl.BlockSpec(memory_space=pltpu.VMEM),
        ]
        + [pl.BlockSpec(memory_space=pltpu.HBM)] * TILES
        + [pl.BlockSpec(memory_space=pl.ANY)] * 4,
        out_specs=(pl.BlockSpec(memory_space=pltpu.VMEM),) * 4,
        scratch_shapes=[
            pltpu.VMEM((TILES * SLOTS * PACK, LANES), jnp.bfloat16),
            pltpu.VMEM((GRAPH, LANES), jnp.bfloat16),
            pltpu.VMEM((GRAPH + PACK, LANES), jnp.float32),
            pltpu.SemaphoreType.DMA((TILES + 4,)),
        ],
        compiler_params=pltpu.CompilerParams(vmem_limit_bytes=20 * 2**20),
        name="block_product",
    )(meta, masks, *tiles, *parts)


def slot_tables(pointers, columns, zl, y, zh, x, core):
    slot_ids = jnp.arange(SLOTS, dtype=jnp.int32)
    rows = jnp.sum((pointers[:, 1:, None] <= slot_ids).astype(jnp.int32), axis=1)
    rows = jnp.minimum(rows, pointers.shape[1] - 2)
    live_count = pointers[:, -1]
    place = jnp.arange(TILES, dtype=jnp.int32)
    spot = 2 * zh + zl
    from_z = (spot - place) % 4
    tile_zh, tile_zl = (from_z // 2)[:, None], (from_z % 2)[:, None]
    tile_core = (core ^ (place // 4))[:, None]
    row_l = rows // 4
    row_y, row_z = row_l % 4, 2 * tile_zh + row_l // 4
    row_base = ((spot - row_z) % 4) * 8 + tile_core * 4 + rows % 4
    col_w = columns // 4
    col_x, col_z = (col_w // 2) % 4, 2 * (col_w // 8) + tile_zl
    col_base = ((spot - col_z) % 4) * 8 + (col_w % 2) * 4 + columns % 4
    forward_source = ((x - col_x) % 4) * STATE + col_base * PACK
    forward_target = ((row_y - y) % 4) * STATE + row_base * PACK
    adjoint_source = ((y - row_y) % 4) * STATE + row_base * PACK
    adjoint_target = ((col_x - x) % 4) * STATE + col_base * PACK
    source = jnp.where(core == 0, forward_source, adjoint_source)
    target = jnp.where(core == 0, forward_target, adjoint_target)
    codes = (source * (2 * GRAPH) + target).reshape(-1, 1)
    ends = jnp.cumsum(live_count)
    spots = jnp.arange(LIST, dtype=jnp.int32)
    passed = (spots[None, :] >= ends[:, None]).astype(jnp.int32)
    begin = jnp.sum(passed * live_count[:, None], axis=0)
    entry = jnp.minimum(jnp.sum(passed, axis=0), TILES - 1) * SLOTS + spots - begin
    hits = entry[None, :] == jnp.arange(TILES * SLOTS, dtype=jnp.int32)[:, None]
    codes = jnp.sum(jnp.where(hits, codes, 0), axis=0)
    listed = spots < ends[-1]
    source = jnp.where(listed, codes // (2 * GRAPH), 0)
    target = jnp.where(listed, codes % (2 * GRAPH), GRAPH)
    entry = jnp.where(listed, entry * PACK, 0)
    counts = jnp.where(spots == 0, ends[TILES // 2 - 1], jnp.where(spots == 1, ends[-1], core))
    return jnp.stack([source, target, entry, counts])


def pack_rows(blocks):
    return jnp.concatenate([blocks[..., :PACK, :], blocks[..., PACK:, :]], axis=-1)


def unpack_rows(blocks):
    return jnp.concatenate([blocks[..., :BLK], blocks[..., BLK:]], axis=-2)


def join_features(pieces, core):
    blocks = unpack_rows(pieces.reshape(4, 8, PACK, LANES))
    blocks = jnp.where(core == 0, blocks, jnp.swapaxes(blocks, -1, -2))
    return blocks.transpose(1, 2, 0, 3).reshape(PIECE, DIM)


def silu_slope(value):
    sigma = jax.nn.sigmoid(value)
    return sigma * (1.0 + value * (1.0 - sigma))


def by_tile(own, other, core):
    return jnp.where(core == 0, jnp.stack([own, other]), jnp.stack([other, own]))


def body(feats, w_first, w_second, cotangent, block_values, row_ptr, col_idx):
    f32, bf16 = jnp.float32, jnp.bfloat16
    zl, y, zh, x, core = (lax.axis_index(name) for name in AXES)
    spot = 2 * zh + zl
    table = jnp.concatenate([row_ptr[0, 0], col_idx[0, 0]]).astype(bf16)
    table = jnp.pad(table[None], ((0, 15), (0, DIM - 113)))
    message = jnp.concatenate([feats[0], cotangent[0], table])
    other = send(message, core_move)
    lanes = jnp.arange(LANES)
    masks = jnp.stack([lanes < BLK, lanes >= BLK]).astype(bf16)
    masks = jnp.broadcast_to(masks[:, None, :], (2, PACK, LANES))

    start = start_pieces(jnp.stack([core, spot]), message, other, w_first, w_second)
    tile = pack_rows(block_values[0, 0]).reshape(SLOTS * PACK, LANES)
    own_swapped = send(tile, core_move)
    start, own_swapped = lax.optimization_barrier((start, own_swapped))
    start = [start[0]] + [send(start[hop], functools.partial(z_move, hop)) for hop in (1, 2, 3)]
    ahead = send(tile, functools.partial(z_move, 1))
    behind = send(tile, functools.partial(z_move, 3))
    start, ahead, behind = lax.optimization_barrier((start, ahead, behind))
    across = send(jnp.where(core == 0, ahead, behind), relay_move)
    state = jnp.concatenate([piece[:ITEMS] for piece in start])
    tables = jnp.stack([piece[ITEMS : ITEMS + PACK : 16] for piece in start]).astype(jnp.int32)
    tables = tables.transpose(1, 0, 2).reshape(TILES, LANES)
    meta = slot_tables(tables[:, :33], tables[:, 33:113], zl, y, zh, x, core)
    first_parts = [state] + [send(state, functools.partial(gather_ring, hop)) for hop in (1, 2, 3)]
    first_parts, across, meta = lax.optimization_barrier((first_parts, across, meta))
    same_core = [tile, ahead, across, behind]
    tiles = same_core + [own_swapped] + [send(piece, core_move) for piece in same_core[1:]]

    chip_feats = by_tile(message[:ITEMS], other[:ITEMS], core).reshape(PIECE, DIM)
    pre_act = jnp.dot(chip_feats, w_first, preferred_element_type=f32)
    hidden = jax.nn.silu(pre_act).astype(bf16)
    restart = jnp.where(core == 0, ALPHA, 0.0).astype(f32)
    constant = restart * state.astype(f32)
    collected = state.astype(f32)
    for step in range(STEPS):
        if step == 0:
            parts = first_parts
        else:
            parts = [state] + [send(state, functools.partial(gather_ring, hop)) for hop in (1, 2, 3)]
        outs = block_product(meta, masks, tiles, parts)
        got = [outs[0]] + [send(outs[hop], functools.partial(scatter_ring, hop)) for hop in (1, 2, 3)]
        summed = sum(piece.astype(f32) for piece in got)
        state = ((1.0 - ALPHA) * summed + constant).astype(bf16)
        if step < STEPS - 1:
            collected = collected + state.astype(f32)
    last = jnp.where(core == 0, state, (ALPHA * collected + state.astype(f32)).astype(bf16))
    last = last.reshape(4, 8 * PACK, LANES)
    pieces = [last[0]] + [send(last[hop], functools.partial(z_move, -hop)) for hop in (1, 2, 3)]
    pieces = jnp.stack(pieces)[(jnp.arange(4) - spot) % 4]
    joined = join_features(pieces, core)
    ending = send(joined, core_move)
    propagated = jnp.where(core == 0, joined[:ITEMS], ending[ITEMS:])
    grad_teleport = jnp.where(core == 0, ending, joined)

    grad_hidden = lax.dot_general(
        grad_teleport, w_second, (((1,), (1,)), ((), ())), preferred_element_type=f32
    )
    grad_pre = (grad_hidden * silu_slope(pre_act)).astype(bf16)
    contract_items = (((0,), (0,)), ((), ()))
    first = lax.dot_general(chip_feats, grad_pre, contract_items, preferred_element_type=f32).astype(bf16)
    second = lax.dot_general(hidden, grad_teleport, contract_items, preferred_element_type=f32).astype(bf16)
    first = lax.dynamic_index_in_dim(first.reshape(8, 2, 16, 1024), core, 1, False)
    second = lax.dynamic_index_in_dim(second.reshape(8, 2, 64, 256), core, 1, False)
    first = first.reshape(8, 16, 2, 4, 128).transpose(2, 0, 3, 1, 4)
    second = second.reshape(8, 4, 16, 2, 128).transpose(3, 0, 1, 2, 4)
    spread = jnp.concatenate([first, second], axis=2).reshape(16, 128, 128)
    landed = lax.all_to_all(spread, ("zl", "zh", "x"), 0, 0)
    mine = jnp.sum(landed.astype(f32), axis=0).astype(bf16)
    shares = lax.all_to_all(jnp.broadcast_to(mine[None], (8, 128, 128)), LOOP, 0, 0)
    sums = jnp.sum(shares.reshape(2, 4, 8, 16, 128).astype(f32), axis=1)
    grad_first = sums[:, :4].transpose(2, 0, 1, 3).reshape(16, 1024)
    grad_second = sums[:, 4:].transpose(1, 2, 0, 3).reshape(64, 256)
    return (propagated[None], grad_first, grad_second)


def solution(mesh):
    fine = Mesh(mesh.devices.reshape(SIZES), AXES)
    return jax.shard_map(
        body,
        mesh=fine,
        in_specs=(
            P(WIDE, LOOP, None),
            P(),
            P(),
            P(WIDE, LOOP, None),
            P(LOOP, WIDE, None, None, None),
            P(LOOP, WIDE, None),
            P(LOOP, WIDE, None),
        ),
        out_specs=(P(WIDE, LOOP, None), P(WIDE, None), P(WIDE, None)),
        check_vma=False,
    )
```

time: 227 us -> 194 us (0.85); the launches traced: 231 us -> 194 us
  Pallas kernels: 41.3 us -> 23.1 us
  waiting for transfers between devices: 84 us -> 73 us
  local copies, waits for them, and re-layouts: 29.4 us -> 19.1 us
  other arithmetic: 8.49 us -> 15.2 us
  matrix products: 7.06 us -> 4.34 us
    pallas_call x3, Pallas kernels: 41.3 us -> 21.1 us  [block_product(): pl.pallas_call(product_kernel, out_shape=(piece,) * 4, in_specs=[pl.Block...]
    ppermute x37 -> x33, waiting for transfers between devices: 70.9 us -> 53.4 us  [send(): return lax.ppermute(value, AXES, permutation(move))]
    unnamed x64 -> x63, local copies, waits for them, and re-layouts: 17.6 us -> 7.04 us
    all_to_all x1 -> x2, waiting for transfers between devices: 13.1 us -> 19.5 us  [the longest x1 12.7 us: body(): landed = lax.all_to_all(spread, ('zl', 'zh', 'x'), 0, 0)]
    dot_general x3 -> x2, matrix products: 4.8 us -> 3.9 us  [the longest x1 3 us: body(): lax.dot_general(chip_feats, grad_pre, contract_items, preferred_element_t...]
    ppermute x37 -> x33, starting transfers between devices: 50 us -> 49.2 us  [send(): return lax.ppermute(value, AXES, permutation(move))]
    all_to_all x1 -> x2, starting transfers between devices: 9.45 us -> 9.03 us  [the longest x1 5.4 us: body(): landed = lax.all_to_all(spread, ('zl', 'zh', 'x'), 0, 0)]
  transfers between devices with their start and end apart: 38 -> 35, of which waited for: 26 -> 24; matrix products, arithmetic and copies ran while one was open for 7% -> 7% of each run, Pallas kernels for 0% -> 1%
where the time goes in v3:
time: 194 us
  waiting for transfers between devices  73 us (38%)
  starting transfers between devices  58.2 us (30%)
  Pallas kernels  23.1 us (12%)
  local copies, waits for them, and re-layouts  19.1 us (10%)
  other arithmetic  15.2 us (8%)
  matrix products  4.34 us (2%)
    ppermute x33, waiting for transfers between devices, send(): return lax.ppermute(value, AXES, permutation(move))  53.4 us
    ppermute x33, starting transfers between devices, send(): return lax.ppermute(value, AXES, permutation(move))  49.2 us
    pallas_call x3, Pallas kernels, block_product(): pl.pallas_call(product_kernel, out_shape=(piece,) * 4, in_specs=[pl.Block...  21.1 us
    all_to_all x1, waiting for transfers between devices, body(): landed = lax.all_to_all(spread, ('zl', 'zh', 'x'), 0, 0)  12.7 us
    unnamed x63, local copies, waits for them, and re-layouts  7.04 us
    all_to_all x1, waiting for transfers between devices, body(): lax.all_to_all(jnp.broadcast_to(mine[None], (8, 128, 128)), LOOP, 0, 0)  6.81 us
    all_to_all x1, starting transfers between devices, body(): landed = lax.all_to_all(spread, ('zl', 'zh', 'x'), 0, 0)  5.4 us
  transfers between devices with their start and end apart: 35, of which 24 were waited for; matrix products, arithmetic and copies ran while one was open for 7% of the time, Pallas kernels for 1%

profile of v3, /device:TPU:0, one launch (start us, length us, event | category | flops | bytes accessed | tf_op | source)
XLA Modules:
  0.0 194.3 jit_solution(896755265493430080)
XLA Ops:
  0.6 1.3 fusion.74
  3.0 4.2 %collective-permute-start.6 = (bf16[2560,128]{1,0:T(8,128)(2,1)S(1)}, bf16[2560,128]{1,0:T(8,128)(2,1)S(1)}, u32[]{:S(2)}, u32[]{:S(2)}) collective-permute-start(bf16[2560,128]{1,0:T(8,128)(2,1)S(1)} %bitcast.80), channel_id=1, source_target_pairs={{0,72},{1,73},{2,74},{3,75},{4,76},{5,77},{6,78},{7,79},{8,64},{9,... | collective-permute-start | bytes 1966088 | tf_op jit(solution)/shard_map/ppermute | solution.py:43
  10.1 1.0 copy-done.7
  11.1 2.0 %start_pieces.1 = bf16[4,288,128]{2,1,0:T(8,128)(2,1)S(1)} custom-call(s32[2]{0:T(128)S(1)} %pad_add_fusion.1.place, bf16[528,256]{1,0:T(8,128)(2,1)S(1)} %pad_maximum_fusion.3.own, bf16[528,256]{1,0:T(8,128)(2,1)} %collective-permute-done.other, bf16[256,1024]{1,0:T(8,128)(2,1)S(1)} %copy-done.5, bf16[1024,256]{1,0:T(8,128)(2,1)S(1)} %copy-done.7), custom_call_target="tpu_custom_call" | custom-call | tf_op jit(solution)/shard_map/start_pieces/pallas_call | solution.py:89
  13.2 3.3 %collective-permute-start.4 = (bf16[288,128]{1,0:T(8,128)(2,1)S(1)}, bf16[288,128]{1,0:T(8,128)(2,1)S(1)}, u32[]{:S(2)}, u32[]{:S(2)}) collective-permute-start(bf16[288,128]{1,0:T(8,128)(2,1)S(1)} %get-tuple-element.59), channel_id=1, source_target_pairs={{0,72},{1,73},{2,74},{3,75},{4,76},{5,77},{6,78},{7,79},{8,64},{9,... | collective-permute-start | bytes 221192 | tf_op jit(solution)/shard_map/ppermute | solution.py:43
  18.0 5.5 %collective-permute-done.6.refs_3_ = bf16[2560,128]{1,0:T(8,128)(2,1)S(1)} collective-permute-done((bf16[2560,128]{1,0:T(8,128)(2,1)S(1)}, bf16[2560,128]{1,0:T(8,128)(2,1)S(1)}, u32[]{:S(2)}, u32[]{:S(2)}) %collective-permute-start.6) | collective-permute-done | bytes 655392 | tf_op jit(solution)/shard_map/ppermute | solution.py:43
  23.5 3.4 %collective-permute-done.5.refs_1_ = bf16[2560,128]{1,0:T(8,128)(2,1)S(1)} collective-permute-done((bf16[2560,128]{1,0:T(8,128)(2,1)S(1)}, bf16[2560,128]{1,0:T(8,128)(2,1)S(1)}, u32[]{:S(2)}, u32[]{:S(2)}) %collective-permute-start.5) | collective-permute-done | bytes 655392 | tf_op jit(solution)/shard_map/ppermute | solution.py:43
  28.2 2.8 %collective-permute-start.9 = (bf16[1024,128]{1,0:T(8,128)(2,1)S(1)}, bf16[1024,128]{1,0:T(8,128)(2,1)}, u32[]{:S(2)}, u32[]{:S(2)}) collective-permute-start(bf16[1024,128]{1,0:T(8,128)(2,1)S(1)} %pad_maximum_fusion.4.refs_8_), channel_id=1, source_target_pairs={{0,6},{1,49},{2,0},{3,51},{4,2},{5,53},{6,4},{7,55},{8,14},{9,57},... | collective-permute-start | bytes 786440 | tf_op jit(solution)/shard_map/ppermute | solution.py:43
  36.4 1.4 fusion.28
  40.2 1.9 %compare_select_fusion.1 = (s32[1,704]{1,0:T(1,128)S(1)}, s32[1,704]{1,0:T(1,128)S(1)}) fusion(s32[]{:T(128)} %axis_index.52, s32[]{:T(128)} %bitcast.19, s32[]{:T(128)} %bitcast.18, s32[704]{0:T(1024)S(1)} %get-tuple-element.56, s32[704]{0:T(1024)} %get-tuple-element.74), kind=kLoop, calls=%fused_computation.63 | loop fusion | flops 6336 | bytes 11276 | tf_op jit(solution)/shard_map/jit(_where)/select_n | solution.py:202
  42.8 4.4 %collective-permute-done.10.refs_2_ = bf16[2560,128]{1,0:T(8,128)(2,1)} collective-permute-done((bf16[2560,128]{1,0:T(8,128)(2,1)}, bf16[2560,128]{1,0:T(8,128)(2,1)}, u32[]{:S(2)}, u32[]{:S(2)}) %collective-permute-start.10) | collective-permute-done | bytes 655392 | tf_op jit(solution)/shard_map/ppermute | solution.py:43
  47.2 2.2 %collective-permute-done.12.refs_6_ = bf16[2560,128]{1,0:T(8,128)(2,1)S(1)} collective-permute-done((bf16[2560,128]{1,0:T(8,128)(2,1)}, bf16[2560,128]{1,0:T(8,128)(2,1)S(1)}, u32[]{:S(2)}, u32[]{:S(2)}) %collective-permute-start.12) | collective-permute-done | bytes 655392 | tf_op jit(solution)/shard_map/ppermute | solution.py:43
  49.5 7.3 %block_product.3 = (bf16[1024,128]{1,0:T(8,128)(2,1)S(1)}, bf16[1024,128]{1,0:T(8,128)(2,1)}, bf16[1024,128]{1,0:T(8,128)(2,1)}, bf16[1024,128]{1,0:T(8,128)(2,1)}) custom-call(s32[4,704]{1,0:T(4,128)S(1)} %pad_add_fusion.meta, bf16[2,32,128]{2,1,0:T(8,128)(2,1)S(1)} %broadcast_in_dim.67.masks, bf16[2560,128]{1,0:T(8,128)(2,1)S(1)} %bitcast.83, ...), custom_call_target="tpu_custom_call" | custom-call | tf_op jit(solution)/shard_map/block_product/pallas_call | solution.py:147
  57.6 1.6 collective-permute-start.14
  59.2 3.4 %collective-permute-start.15 = (bf16[1024,128]{1,0:T(8,128)(2,1)}, bf16[1024,128]{1,0:T(8,128)(2,1)}, u32[]{:S(2)}, u32[]{:S(2)}) collective-permute-start(bf16[1024,128]{1,0:T(8,128)(2,1)} %get-tuple-element.45), channel_id=1, source_target_pairs={{0,32},{1,5},{2,34},{3,7},{4,36},{5,1},{6,38},{7,3},{8,40},{9,13},... | collective-permute-start | bytes 786440 | tf_op jit(solution)/shard_map/ppermute | solution.py:43
  62.5 2.3 %collective-permute-start.16 = (bf16[1024,128]{1,0:T(8,128)(2,1)}, bf16[1024,128]{1,0:T(8,128)(2,1)}, u32[]{:S(2)}, u32[]{:S(2)}) collective-permute-start(bf16[1024,128]{1,0:T(8,128)(2,1)} %get-tuple-element.46), channel_id=1, source_target_pairs={{0,48},{1,7},{2,50},{3,1},{4,52},{5,3},{6,54},{7,5},{8,56},{9,15},... | collective-permute-start | bytes 786440 | tf_op jit(solution)/shard_map/ppermute | solution.py:43
  65.6 4.4 %collective-permute-done.15 = bf16[1024,128]{1,0:T(8,128)(2,1)} collective-permute-done((bf16[1024,128]{1,0:T(8,128)(2,1)}, bf16[1024,128]{1,0:T(8,128)(2,1)}, u32[]{:S(2)}, u32[]{:S(2)}) %collective-permute-start.15) | collective-permute-done | bytes 262176 | tf_op jit(solution)/shard_map/ppermute | solution.py:43
  70.0 1.5 fusion.6.refs_8_
  71.6 2.4 %collective-permute-start.19 = (bf16[1024,128]{1,0:T(8,128)(2,1)S(1)}, bf16[1024,128]{1,0:T(8,128)(2,1)S(1)}, u32[]{:S(2)}, u32[]{:S(2)}) collective-permute-start(bf16[1024,128]{1,0:T(8,128)(2,1)S(1)} %fusion.6.refs_8_), channel_id=1, source_target_pairs={{0,6},{1,49},{2,0},{3,51},{4,2},{5,53},{6,4},{7,55},{8,14},{9,57},... | collective-permute-start | bytes 786440 | tf_op jit(solution)/shard_map/ppermute | solution.py:43
  74.0 2.6 %collective-permute-start.18 = (bf16[1024,128]{1,0:T(8,128)(2,1)S(1)}, bf16[1024,128]{1,0:T(8,128)(2,1)S(1)}, u32[]{:S(2)}, u32[]{:S(2)}) collective-permute-start(bf16[1024,128]{1,0:T(8,128)(2,1)S(1)} %fusion.6.refs_8_), channel_id=1, source_target_pairs={{0,4},{1,33},{2,6},{3,35},{4,0},{5,37},{6,2},{7,39},{8,12},{9,41},... | collective-permute-start | bytes 786440 | tf_op jit(solution)/shard_map/ppermute | solution.py:43
  76.6 2.3 %collective-permute-done.19.refs_11_ = bf16[1024,128]{1,0:T(8,128)(2,1)S(1)} collective-permute-done((bf16[1024,128]{1,0:T(8,128)(2,1)S(1)}, bf16[1024,128]{1,0:T(8,128)(2,1)S(1)}, u32[]{:S(2)}, u32[]{:S(2)}) %collective-permute-start.19) | collective-permute-done | bytes 262176 | tf_op jit(solution)/shard_map/ppermute | solution.py:43
  78.8 3.1 %collective-permute-done.18.refs_10_ = bf16[1024,128]{1,0:T(8,128)(2,1)S(1)} collective-permute-done((bf16[1024,128]{1,0:T(8,128)(2,1)S(1)}, bf16[1024,128]{1,0:T(8,128)(2,1)S(1)}, u32[]{:S(2)}, u32[]{:S(2)}) %collective-permute-start.18) | collective-permute-done | bytes 262176 | tf_op jit(solution)/shard_map/ppermute | solution.py:43
  81.9 2.8 %collective-permute-done.17.refs_9_ = bf16[1024,128]{1,0:T(8,128)(2,1)S(1)} collective-permute-done((bf16[1024,128]{1,0:T(8,128)(2,1)S(1)}, bf16[1024,128]{1,0:T(8,128)(2,1)S(1)}, u32[]{:S(2)}, u32[]{:S(2)}) %collective-permute-start.17) | collective-permute-done | bytes 262176 | tf_op jit(solution)/shard_map/ppermute | solution.py:43
  84.7 1.1 copy-done.1
  85.8 1.1 copy-done.3
  87.6 6.6 %block_product.4 = (bf16[1024,128]{1,0:T(8,128)(2,1)S(1)}, bf16[1024,128]{1,0:T(8,128)(2,1)S(1)}, bf16[1024,128]{1,0:T(8,128)(2,1)S(1)}, bf16[1024,128]{1,0:T(8,128)(2,1)S(1)}) custom-call(s32[4,704]{1,0:T(4,128)S(1)} %copy-done.12, bf16[2,32,128]{2,1,0:T(8,128)(2,1)S(1)} %broadcast_in_dim.67.masks, bf16[2560,128]{1,0:T(8,128)(2,1)S(1)} %bitcast.84, ...), custom_call_target="tpu_custom_call" | custom-call | tf_op jit(solution)/shard_map/block_product/pallas_call | solution.py:147
  94.1 1.5 collective-permute-start.20
  95.6 3.0 %collective-permute-start.21 = (bf16[1024,128]{1,0:T(8,128)(2,1)S(1)}, bf16[1024,128]{1,0:T(8,128)(2,1)S(1)}, u32[]{:S(2)}, u32[]{:S(2)}) collective-permute-start(bf16[1024,128]{1,0:T(8,128)(2,1)S(1)} %get-tuple-element.49), channel_id=1, source_target_pairs={{0,32},{1,5},{2,34},{3,7},{4,36},{5,1},{6,38},{7,3},{8,40},{9,13},... | collective-permute-start | bytes 786440 | tf_op jit(solution)/shard_map/ppermute | solution.py:43
  98.6 2.5 %collective-permute-start.22 = (bf16[1024,128]{1,0:T(8,128)(2,1)S(1)}, bf16[1024,128]{1,0:T(8,128)(2,1)S(1)}, u32[]{:S(2)}, u32[]{:S(2)}) collective-permute-start(bf16[1024,128]{1,0:T(8,128)(2,1)S(1)} %get-tuple-element.50), channel_id=1, source_target_pairs={{0,48},{1,7},{2,50},{3,1},{4,52},{5,3},{6,54},{7,5},{8,56},{9,15},... | collective-permute-start | bytes 786440 | tf_op jit(solution)/shard_map/ppermute | solution.py:43
  101.8 3.8 %collective-permute-done.21 = bf16[1024,128]{1,0:T(8,128)(2,1)S(1)} collective-permute-done((bf16[1024,128]{1,0:T(8,128)(2,1)S(1)}, bf16[1024,128]{1,0:T(8,128)(2,1)S(1)}, u32[]{:S(2)}, u32[]{:S(2)}) %collective-permute-start.21) | collective-permute-done | bytes 262176 | tf_op jit(solution)/shard_map/ppermute | solution.py:43
  106.5 5.8 %collective-permute-start.24 = (bf16[1024,128]{1,0:T(8,128)(2,1)S(1)}, bf16[1024,128]{1,0:T(8,128)(2,1)S(1)}, u32[]{:S(2)}, u32[]{:S(2)}) collective-permute-start(bf16[1024,128]{1,0:T(8,128)(2,1)S(1)} %fusion.7.refs_8_), channel_id=1, source_target_pairs={{0,4},{1,33},{2,6},{3,35},{4,0},{5,37},{6,2},{7,39},{8,12},{9,41},... | collective-permute-start | bytes 786440 | tf_op jit(solution)/shard_map/ppermute | solution.py:43
  112.4 2.3 %collective-permute-done.25.refs_11_ = bf16[1024,128]{1,0:T(8,128)(2,1)S(1)} collective-permute-done((bf16[1024,128]{1,0:T(8,128)(2,1)S(1)}, bf16[1024,128]{1,0:T(8,128)(2,1)S(1)}, u32[]{:S(2)}, u32[]{:S(2)}) %collective-permute-start.25) | collective-permute-done | bytes 262176 | tf_op jit(solution)/shard_map/ppermute | solution.py:43
  114.6 2.1 %collective-permute-done.24.refs_10_ = bf16[1024,128]{1,0:T(8,128)(2,1)S(1)} collective-permute-done((bf16[1024,128]{1,0:T(8,128)(2,1)S(1)}, bf16[1024,128]{1,0:T(8,128)(2,1)S(1)}, u32[]{:S(2)}, u32[]{:S(2)}) %collective-permute-start.24) | collective-permute-done | bytes 262176 | tf_op jit(solution)/shard_map/ppermute | solution.py:43
  116.7 3.2 %collective-permute-done.23.refs_9_ = bf16[1024,128]{1,0:T(8,128)(2,1)S(1)} collective-permute-done((bf16[1024,128]{1,0:T(8,128)(2,1)S(1)}, bf16[1024,128]{1,0:T(8,128)(2,1)S(1)}, u32[]{:S(2)}, u32[]{:S(2)}) %collective-permute-start.23) | collective-permute-done | bytes 262176 | tf_op jit(solution)/shard_map/ppermute | solution.py:43
  119.9 7.2 %block_product.5 = (bf16[1024,128]{1,0:T(8,128)(2,1)S(1)}, bf16[1024,128]{1,0:T(8,128)(2,1)}, bf16[1024,128]{1,0:T(8,128)(2,1)}, bf16[1024,128]{1,0:T(8,128)(2,1)}) custom-call(s32[4,704]{1,0:T(4,128)S(1)} %copy-done.13, bf16[2,32,128]{2,1,0:T(8,128)(2,1)S(1)} %broadcast_in_dim.67.masks, bf16[2560,128]{1,0:T(8,128)(2,1)S(1)} %bitcast.85, ...), custom_call_target="tpu_custom_call" | custom-call | tf_op jit(solution)/shard_map/block_product/pallas_call | solution.py:147
  127.9 5.6 %collective-permute-start.27 = (bf16[1024,128]{1,0:T(8,128)(2,1)}, bf16[1024,128]{1,0:T(8,128)(2,1)S(1)}, u32[]{:S(2)}, u32[]{:S(2)}) collective-permute-start(bf16[1024,128]{1,0:T(8,128)(2,1)} %get-tuple-element.53), channel_id=1, source_target_pairs={{0,32},{1,5},{2,34},{3,7},{4,36},{5,1},{6,38},{7,3},{8,40},{9,13},... | collective-permute-start | bytes 786440 | tf_op jit(solution)/shard_map/ppermute | solution.py:43
  135.4 1.2 collective-permute-done.26
  136.6 4.3 %collective-permute-done.27 = bf16[1024,128]{1,0:T(8,128)(2,1)S(1)} collective-permute-done((bf16[1024,128]{1,0:T(8,128)(2,1)}, bf16[1024,128]{1,0:T(8,128)(2,1)S(1)}, u32[]{:S(2)}, u32[]{:S(2)}) %collective-permute-start.27) | collective-permute-done | bytes 262176 | tf_op jit(solution)/shard_map/ppermute | solution.py:43
  140.9 1.4 fusion.14
  143.4 2.2 %collective-permute-start.29 = (bf16[256,128]{1,0:T(8,128)(2,1)S(1)}, bf16[256,128]{1,0:T(8,128)(2,1)S(1)}, u32[]{:S(2)}, u32[]{:S(2)}) collective-permute-start(bf16[256,128]{1,0:T(8,128)(2,1)S(1)} %get-tuple-element.68), channel_id=1, source_target_pairs={{0,72},{1,73},{2,74},{3,75},{4,76},{5,77},{6,78},{7,79},{8,64},{9,... | collective-permute-start | bytes 196616 | tf_op jit(solution)/shard_map/ppermute | solution.py:43
  145.7 2.9 %collective-permute-done.31 = bf16[256,128]{1,0:T(8,128)(2,1)S(1)} collective-permute-done((bf16[256,128]{1,0:T(8,128)(2,1)S(1)}, bf16[256,128]{1,0:T(8,128)(2,1)S(1)}, u32[]{:S(2)}, u32[]{:S(2)}) %collective-permute-start.31) | collective-permute-done | bytes 65568 | tf_op jit(solution)/shard_map/ppermute | solution.py:43
  152.8 1.3 collective-permute-done.32
  155.8 1.2 copy.59
  156.9 3.0 %fusion.1 = bf16[256,1024]{1,0:T(8,128)(2,1)} fusion(bf16[512,256]{1,0:T(8,128)(2,1)} %bitcast.92, f32[512,1024]{1,0:T(8,128)S(1)} %fusion.77, bf16[1024,256]{1,0:T(8,128)(2,1)S(1)} %copy-done.8, bf16[512,256]{1,0:T(8,128)(2,1)} %copy-done.26, bf16[512,256]{1,0:T(8,128)(2,1)} %reshape.392, pred[]{:T(512)S(6)} %eq.65), kind=kOutput, calls=%fused_computation.8 | convolution fusion | flops 541982720 | bytes 3932161 | tf_op jit(solution)/shard_map/dot_general | solution.py:290
  162.3 5.4 %all-to-all-start = ((bf16[16,128,128]{2,1,0:T(8,128)(2,1)}), bf16[16,128,128]{2,1,0:T(8,128)(2,1)S(1)}, u32[]{:S(2)}, u32[]{:S(2)}) async-start(bf16[16,128,128]{2,1,0:T(8,128)(2,1)} %bitcast.35), calls=%async_computation | async-start | bytes 1048576 | tf_op jit(solution)/shard_map/all_to_all | solution.py:297
  168.2 12.7 %all-to-all-done = bf16[16,128,128]{2,1,0:T(8,128)(2,1)S(1)} async-done(((bf16[16,128,128]{2,1,0:T(8,128)(2,1)}), bf16[16,128,128]{2,1,0:T(8,128)(2,1)S(1)}, u32[]{:S(2)}, u32[]{:S(2)}) %all-to-all-start) | async-done | bytes 524320 | tf_op jit(solution)/shard_map/all_to_all | solution.py:297
  181.7 3.6 %all-to-all-start.1 = ((bf16[8,128,128]{2,1,0:T(8,128)(2,1)}), bf16[8,128,128]{2,1,0:T(8,128)(2,1)S(1)}, u32[]{:S(2)}, u32[]{:S(2)}) async-start(bf16[8,128,128]{2,1,0:T(8,128)(2,1)} %broadcast_in_dim.69), calls=%async_computation.1 | async-start | bytes 524288 | tf_op jit(solution)/shard_map/all_to_all | solution.py:299
  186.1 6.8 %all-to-all-done.1 = bf16[8,128,128]{2,1,0:T(8,128)(2,1)S(1)} async-done(((bf16[8,128,128]{2,1,0:T(8,128)(2,1)}), bf16[8,128,128]{2,1,0:T(8,128)(2,1)S(1)}, u32[]{:S(2)}, u32[]{:S(2)}) %all-to-all-start.1) | async-done | bytes 262176 | tf_op jit(solution)/shard_map/all_to_all | solution.py:299
  (164 shorter events, 34.0 us)
Async XLA Ops:
  1.9 8.1 %copy-start.5 = (bf16[256,1024]{1,0:T(8,128)(2,1)S(1)}, bf16[256,1024]{1,0:T(8,128)(2,1)}, u32[]{:S(2)}) copy-start(bf16[256,1024]{1,0:T(8,128)(2,1)} %w_first.1) | copy-start | bytes 1572868
  3.0 20.6 %collective-permute-start.6 = (bf16[2560,128]{1,0:T(8,128)(2,1)S(1)}, bf16[2560,128]{1,0:T(8,128)(2,1)S(1)}, u32[]{:S(2)}, u32[]{:S(2)}) collective-permute-start(bf16[2560,128]{1,0:T(8,128)(2,1)S(1)} %bitcast.80), channel_id=1, source_target_pairs={{0,72},{1,73},{2,74},{3,75},{4,76},{5,77},{6,78},{7,79},{8,64},{9,... | collective-permute-start | bytes 1966088 | tf_op jit(solution)/shard_map/ppermute | solution.py:43
  7.2 19.8 %collective-permute-start.5 = (bf16[2560,128]{1,0:T(8,128)(2,1)S(1)}, bf16[2560,128]{1,0:T(8,128)(2,1)S(1)}, u32[]{:S(2)}, u32[]{:S(2)}) collective-permute-start(bf16[2560,128]{1,0:T(8,128)(2,1)S(1)} %bitcast.81), channel_id=1, source_target_pairs={{0,64},{1,65},{2,66},{3,67},{4,68},{5,69},{6,70},{7,71},{8,72},{9,... | collective-permute-start | bytes 1966088 | tf_op jit(solution)/shard_map/ppermute | solution.py:43
  7.2 6.0 %collective-permute-start.1 = (bf16[2560,128]{1,0:T(8,128)(2,1)S(1)}, bf16[2560,128]{1,0:T(8,128)(2,1)S(1)}, u32[]{:S(2)}, u32[]{:S(2)}) collective-permute-start(bf16[2560,128]{1,0:T(8,128)(2,1)S(1)} %bitcast.82), channel_id=1, source_target_pairs={{0,1},{1,0},{2,3},{3,2},{4,5},{5,4},{6,7},{7,6},{8,9},{9,8},{10,11... | collective-permute-start | bytes 1966088 | tf_op jit(solution)/shard_map/ppermute | solution.py:43
  8.2 1.9 collective-permute-start
  13.2 13.7 %collective-permute-start.4 = (bf16[288,128]{1,0:T(8,128)(2,1)S(1)}, bf16[288,128]{1,0:T(8,128)(2,1)S(1)}, u32[]{:S(2)}, u32[]{:S(2)}) collective-permute-start(bf16[288,128]{1,0:T(8,128)(2,1)S(1)} %get-tuple-element.59), channel_id=1, source_target_pairs={{0,72},{1,73},{2,74},{3,75},{4,76},{5,77},{6,78},{7,79},{8,64},{9,... | collective-permute-start | bytes 221192 | tf_op jit(solution)/shard_map/ppermute | solution.py:43
  16.5 10.4 %collective-permute-start.3 = (bf16[288,128]{1,0:T(8,128)(2,1)S(1)}, bf16[288,128]{1,0:T(8,128)(2,1)S(1)}, u32[]{:S(2)}, u32[]{:S(2)}) collective-permute-start(bf16[288,128]{1,0:T(8,128)(2,1)S(1)} %get-tuple-element.60), channel_id=1, source_target_pairs={{0,8},{1,9},{2,10},{3,11},{4,12},{5,13},{6,14},{7,15},{8,0},{9,1},... | collective-permute-start | bytes 221192 | tf_op jit(solution)/shard_map/ppermute | solution.py:43
  16.5 11.2 %collective-permute-start.2 = (bf16[288,128]{1,0:T(8,128)(2,1)S(1)}, bf16[288,128]{1,0:T(8,128)(2,1)S(1)}, u32[]{:S(2)}, u32[]{:S(2)}) collective-permute-start(bf16[288,128]{1,0:T(8,128)(2,1)S(1)} %get-tuple-element.61), channel_id=1, source_target_pairs={{0,64},{1,65},{2,66},{3,67},{4,68},{5,69},{6,70},{7,71},{8,72},{9,... | collective-permute-start | bytes 221192 | tf_op jit(solution)/shard_map/ppermute | solution.py:43
  28.2 14.0 %collective-permute-start.9 = (bf16[1024,128]{1,0:T(8,128)(2,1)S(1)}, bf16[1024,128]{1,0:T(8,128)(2,1)}, u32[]{:S(2)}, u32[]{:S(2)}) collective-permute-start(bf16[1024,128]{1,0:T(8,128)(2,1)S(1)} %pad_maximum_fusion.4.refs_8_), channel_id=1, source_target_pairs={{0,6},{1,49},{2,0},{3,51},{4,2},{5,53},{6,4},{7,55},{8,14},{9,57},... | collective-permute-start | bytes 786440 | tf_op jit(solution)/shard_map/ppermute | solution.py:43
  31.0 11.8 %collective-permute-start.8 = (bf16[1024,128]{1,0:T(8,128)(2,1)S(1)}, bf16[1024,128]{1,0:T(8,128)(2,1)}, u32[]{:S(2)}, u32[]{:S(2)}) collective-permute-start(bf16[1024,128]{1,0:T(8,128)(2,1)S(1)} %pad_maximum_fusion.4.refs_8_), channel_id=1, source_target_pairs={{0,4},{1,33},{2,6},{3,35},{4,0},{5,37},{6,2},{7,39},{8,12},{9,41},... | collective-permute-start | bytes 786440 | tf_op jit(solution)/shard_map/ppermute | solution.py:43
  31.8 11.0 %collective-permute-start.7 = (bf16[1024,128]{1,0:T(8,128)(2,1)S(1)}, bf16[1024,128]{1,0:T(8,128)(2,1)}, u32[]{:S(2)}, u32[]{:S(2)}) collective-permute-start(bf16[1024,128]{1,0:T(8,128)(2,1)S(1)} %pad_maximum_fusion.4.refs_8_), channel_id=1, source_target_pairs={{0,2},{1,17},{2,4},{3,19},{4,6},{5,21},{6,0},{7,23},{8,10},{9,25},... | collective-permute-start | bytes 786440 | tf_op jit(solution)/shard_map/ppermute | solution.py:43
  34.2 13.1 %collective-permute-start.11 = (bf16[2560,128]{1,0:T(8,128)(2,1)S(1)}, bf16[2560,128]{1,0:T(8,128)(2,1)S(1)}, u32[]{:S(2)}, u32[]{:S(2)}) collective-permute-start(bf16[2560,128]{1,0:T(8,128)(2,1)S(1)} %collective-permute-done.5.refs_1_), channel_id=1, source_target_pairs={{0,1},{1,0},{2,3},{3,2},{4,5},{5,4},{6,7},{7,6},{8,9},{9,8},{10,11... | collective-permute-start | bytes 1966088 | tf_op jit(solution)/shard_map/ppermute | solution.py:43
  35.1 12.1 %collective-permute-start.10 = (bf16[2560,128]{1,0:T(8,128)(2,1)}, bf16[2560,128]{1,0:T(8,128)(2,1)}, u32[]{:S(2)}, u32[]{:S(2)}) collective-permute-start(bf16[2560,128]{1,0:T(8,128)(2,1)} %broadcast_select_fusion), channel_id=1, source_target_pairs={{0,64},{1,73},{2,66},{3,75},{4,68},{5,77},{6,70},{7,79},{8,72},{9,... | collective-permute-start | bytes 1966088 | tf_op jit(solution)/shard_map/ppermute | solution.py:43
  42.2 14.7 %copy-start.11 = (s32[4,704]{1,0:T(4,128)}, s32[4,704]{1,0:T(4,128)S(1)}, u32[]{:S(2)}) copy-start(s32[4,704]{1,0:T(4,128)S(1)} %pad_add_fusion.meta) | copy-start | bytes 33796
  42.2 5.0 %collective-permute-start.13 = (bf16[2560,128]{1,0:T(8,128)(2,1)S(1)}, bf16[2560,128]{1,0:T(8,128)(2,1)S(1)}, u32[]{:S(2)}, u32[]{:S(2)}) collective-permute-start(bf16[2560,128]{1,0:T(8,128)(2,1)S(1)} %collective-permute-done.6.refs_3_), channel_id=1, source_target_pairs={{0,1},{1,0},{2,3},{3,2},{4,5},{5,4},{6,7},{7,6},{8,9},{9,8},{10,11... | collective-permute-start | bytes 1966088 | tf_op jit(solution)/shard_map/ppermute | solution.py:43
  47.2 2.3 %collective-permute-start.12 = (bf16[2560,128]{1,0:T(8,128)(2,1)}, bf16[2560,128]{1,0:T(8,128)(2,1)S(1)}, u32[]{:S(2)}, u32[]{:S(2)}) collective-permute-start(bf16[2560,128]{1,0:T(8,128)(2,1)} %collective-permute-done.10.refs_2_), channel_id=1, source_target_pairs={{0,1},{1,0},{2,3},{3,2},{4,5},{5,4},{6,7},{7,6},{8,9},{9,8},{10,11... | collective-permute-start | bytes 1966088 | tf_op jit(solution)/shard_map/ppermute | solution.py:43
  47.2 9.6 %copy-start = (bf16[2560,128]{1,0:T(8,128)(2,1)}, bf16[2560,128]{1,0:T(8,128)(2,1)S(1)}, u32[]{:S(2)}) copy-start(bf16[2560,128]{1,0:T(8,128)(2,1)S(1)} %collective-permute-done.13.refs_7_) | copy-start | bytes 1966084
  49.5 7.4 %copy-start.2 = (bf16[2560,128]{1,0:T(8,128)(2,1)}, bf16[2560,128]{1,0:T(8,128)(2,1)S(1)}, u32[]{:S(2)}) copy-start(bf16[2560,128]{1,0:T(8,128)(2,1)S(1)} %collective-permute-done.12.refs_6_) | copy-start | bytes 1966084
  57.6 8.1 %collective-permute-start.14 = (bf16[1024,128]{1,0:T(8,128)(2,1)}, bf16[1024,128]{1,0:T(8,128)(2,1)S(1)}, u32[]{:S(2)}, u32[]{:S(2)}) collective-permute-start(bf16[1024,128]{1,0:T(8,128)(2,1)} %get-tuple-element.44), channel_id=1, source_target_pairs={{0,16},{1,3},{2,18},{3,5},{4,20},{5,7},{6,22},{7,1},{8,24},{9,11},... | collective-permute-start | bytes 786440 | tf_op jit(solution)/shard_map/ppermute | solution.py:43
  59.2 10.8 %collective-permute-start.15 = (bf16[1024,128]{1,0:T(8,128)(2,1)}, bf16[1024,128]{1,0:T(8,128)(2,1)}, u32[]{:S(2)}, u32[]{:S(2)}) collective-permute-start(bf16[1024,128]{1,0:T(8,128)(2,1)} %get-tuple-element.45), channel_id=1, source_target_pairs={{0,32},{1,5},{2,34},{3,7},{4,36},{5,1},{6,38},{7,3},{8,40},{9,13},... | collective-permute-start | bytes 786440 | tf_op jit(solution)/shard_map/ppermute | solution.py:43
  62.5 7.5 %collective-permute-start.16 = (bf16[1024,128]{1,0:T(8,128)(2,1)}, bf16[1024,128]{1,0:T(8,128)(2,1)}, u32[]{:S(2)}, u32[]{:S(2)}) collective-permute-start(bf16[1024,128]{1,0:T(8,128)(2,1)} %get-tuple-element.46), channel_id=1, source_target_pairs={{0,48},{1,7},{2,50},{3,1},{4,52},{5,3},{6,54},{7,5},{8,56},{9,15},... | collective-permute-start | bytes 786440 | tf_op jit(solution)/shard_map/ppermute | solution.py:43
  70.0 36.2 %copy-start.15 = (bf16[256,128]{1,0:T(8,128)(2,1)S(1)}, bf16[256,128]{1,0:T(8,128)(2,1)}, u32[]{:S(2)}) copy-start(bf16[256,128]{1,0:T(8,128)(2,1)} %copy-done.14) | copy-start | bytes 196612
  70.0 36.2 %copy-start.17 = (bf16[256,128]{1,0:T(8,128)(2,1)S(1)}, bf16[256,128]{1,0:T(8,128)(2,1)}, u32[]{:S(2)}) copy-start(bf16[256,128]{1,0:T(8,128)(2,1)} %copy-done.16) | copy-start | bytes 196612
  70.0 36.2 %copy-start.19 = (bf16[256,128]{1,0:T(8,128)(2,1)S(1)}, bf16[256,128]{1,0:T(8,128)(2,1)}, u32[]{:S(2)}) copy-start(bf16[256,128]{1,0:T(8,128)(2,1)} %copy-done.18) | copy-start | bytes 196612
  70.0 36.2 %copy-start.21 = (bf16[256,128]{1,0:T(8,128)(2,1)S(1)}, bf16[256,128]{1,0:T(8,128)(2,1)}, u32[]{:S(2)}) copy-start(bf16[256,128]{1,0:T(8,128)(2,1)} %copy-done.20) | copy-start | bytes 196612
  70.0 49.9 %copy-start.13 = (s32[4,704]{1,0:T(4,128)S(1)}, s32[4,704]{1,0:T(4,128)}, u32[]{:S(2)}) copy-start(s32[4,704]{1,0:T(4,128)} %copy-done.11) | copy-start | bytes 33796
  71.6 7.3 %collective-permute-start.19 = (bf16[1024,128]{1,0:T(8,128)(2,1)S(1)}, bf16[1024,128]{1,0:T(8,128)(2,1)S(1)}, u32[]{:S(2)}, u32[]{:S(2)}) collective-permute-start(bf16[1024,128]{1,0:T(8,128)(2,1)S(1)} %fusion.6.refs_8_), channel_id=1, source_target_pairs={{0,6},{1,49},{2,0},{3,51},{4,2},{5,53},{6,4},{7,55},{8,14},{9,57},... | collective-permute-start | bytes 786440 | tf_op jit(solution)/shard_map/ppermute | solution.py:43
  74.0 7.9 %collective-permute-start.18 = (bf16[1024,128]{1,0:T(8,128)(2,1)S(1)}, bf16[1024,128]{1,0:T(8,128)(2,1)S(1)}, u32[]{:S(2)}, u32[]{:S(2)}) collective-permute-start(bf16[1024,128]{1,0:T(8,128)(2,1)S(1)} %fusion.6.refs_8_), channel_id=1, source_target_pairs={{0,4},{1,33},{2,6},{3,35},{4,0},{5,37},{6,2},{7,39},{8,12},{9,41},... | collective-permute-start | bytes 786440 | tf_op jit(solution)/shard_map/ppermute | solution.py:43
  76.6 8.1 %collective-permute-start.17 = (bf16[1024,128]{1,0:T(8,128)(2,1)S(1)}, bf16[1024,128]{1,0:T(8,128)(2,1)S(1)}, u32[]{:S(2)}, u32[]{:S(2)}) collective-permute-start(bf16[1024,128]{1,0:T(8,128)(2,1)S(1)} %fusion.6.refs_8_), channel_id=1, source_target_pairs={{0,2},{1,17},{2,4},{3,19},{4,6},{5,21},{6,0},{7,23},{8,10},{9,25},... | collective-permute-start | bytes 786440 | tf_op jit(solution)/shard_map/ppermute | solution.py:43
  94.1 7.7 %collective-permute-start.20 = (bf16[1024,128]{1,0:T(8,128)(2,1)S(1)}, bf16[1024,128]{1,0:T(8,128)(2,1)S(1)}, u32[]{:S(2)}, u32[]{:S(2)}) collective-permute-start(bf16[1024,128]{1,0:T(8,128)(2,1)S(1)} %get-tuple-element.48), channel_id=1, source_target_pairs={{0,16},{1,3},{2,18},{3,5},{4,20},{5,7},{6,22},{7,1},{8,24},{9,11},... | collective-permute-start | bytes 786440 | tf_op jit(solution)/shard_map/ppermute | solution.py:43
  95.6 10.0 %collective-permute-start.21 = (bf16[1024,128]{1,0:T(8,128)(2,1)S(1)}, bf16[1024,128]{1,0:T(8,128)(2,1)S(1)}, u32[]{:S(2)}, u32[]{:S(2)}) collective-permute-start(bf16[1024,128]{1,0:T(8,128)(2,1)S(1)} %get-tuple-element.49), channel_id=1, source_target_pairs={{0,32},{1,5},{2,34},{3,7},{4,36},{5,1},{6,38},{7,3},{8,40},{9,13},... | collective-permute-start | bytes 786440 | tf_op jit(solution)/shard_map/ppermute | solution.py:43
  98.6 7.6 %collective-permute-start.22 = (bf16[1024,128]{1,0:T(8,128)(2,1)S(1)}, bf16[1024,128]{1,0:T(8,128)(2,1)S(1)}, u32[]{:S(2)}, u32[]{:S(2)}) collective-permute-start(bf16[1024,128]{1,0:T(8,128)(2,1)S(1)} %get-tuple-element.50), channel_id=1, source_target_pairs={{0,48},{1,7},{2,50},{3,1},{4,52},{5,3},{6,54},{7,5},{8,56},{9,15},... | collective-permute-start | bytes 786440 | tf_op jit(solution)/shard_map/ppermute | solution.py:43
  106.4 20.8 %copy-start.4 = (bf16[1024,128]{1,0:T(8,128)(2,1)}, bf16[1024,128]{1,0:T(8,128)(2,1)S(1)}, u32[]{:S(2)}) copy-start(bf16[1024,128]{1,0:T(8,128)(2,1)S(1)} %fusion.7.refs_8_) | copy-start | bytes 786436
  106.4 8.2 %collective-permute-start.25 = (bf16[1024,128]{1,0:T(8,128)(2,1)S(1)}, bf16[1024,128]{1,0:T(8,128)(2,1)S(1)}, u32[]{:S(2)}, u32[]{:S(2)}) collective-permute-start(bf16[1024,128]{1,0:T(8,128)(2,1)S(1)} %fusion.7.refs_8_), channel_id=1, source_target_pairs={{0,6},{1,49},{2,0},{3,51},{4,2},{5,53},{6,4},{7,55},{8,14},{9,57},... | collective-permute-start | bytes 786440 | tf_op jit(solution)/shard_map/ppermute | solution.py:43
  106.5 10.2 %collective-permute-start.24 = (bf16[1024,128]{1,0:T(8,128)(2,1)S(1)}, bf16[1024,128]{1,0:T(8,128)(2,1)S(1)}, u32[]{:S(2)}, u32[]{:S(2)}) collective-permute-start(bf16[1024,128]{1,0:T(8,128)(2,1)S(1)} %fusion.7.refs_8_), channel_id=1, source_target_pairs={{0,4},{1,33},{2,6},{3,35},{4,0},{5,37},{6,2},{7,39},{8,12},{9,41},... | collective-permute-start | bytes 786440 | tf_op jit(solution)/shard_map/ppermute | solution.py:43
  112.4 7.6 %collective-permute-start.23 = (bf16[1024,128]{1,0:T(8,128)(2,1)S(1)}, bf16[1024,128]{1,0:T(8,128)(2,1)S(1)}, u32[]{:S(2)}, u32[]{:S(2)}) collective-permute-start(bf16[1024,128]{1,0:T(8,128)(2,1)S(1)} %fusion.7.refs_8_), channel_id=1, source_target_pairs={{0,2},{1,17},{2,4},{3,19},{4,6},{5,21},{6,0},{7,23},{8,10},{9,25},... | collective-permute-start | bytes 786440 | tf_op jit(solution)/shard_map/ppermute | solution.py:43
  127.9 17.7 %copy-start.24 = (bf16[1,256,256]{2,1,0:T(8,128)(2,1)S(1)}, bf16[1,256,256]{2,1,0:T(8,128)(2,1)}, u32[]{:S(2)}) copy-start(bf16[1,256,256]{2,1,0:T(8,128)(2,1)} %param.7) | copy-start | bytes 393220
  127.9 8.7 %collective-permute-start.26 = (bf16[1024,128]{1,0:T(8,128)(2,1)}, bf16[1024,128]{1,0:T(8,128)(2,1)S(1)}, u32[]{:S(2)}, u32[]{:S(2)}) collective-permute-start(bf16[1024,128]{1,0:T(8,128)(2,1)} %get-tuple-element.52), channel_id=1, source_target_pairs={{0,16},{1,3},{2,18},{3,5},{4,20},{5,7},{6,22},{7,1},{8,24},{9,11},... | collective-permute-start | bytes 786440 | tf_op jit(solution)/shard_map/ppermute | solution.py:43
  127.9 13.0 %collective-permute-start.27 = (bf16[1024,128]{1,0:T(8,128)(2,1)}, bf16[1024,128]{1,0:T(8,128)(2,1)S(1)}, u32[]{:S(2)}, u32[]{:S(2)}) collective-permute-start(bf16[1024,128]{1,0:T(8,128)(2,1)} %get-tuple-element.53), channel_id=1, source_target_pairs={{0,32},{1,5},{2,34},{3,7},{4,36},{5,1},{6,38},{7,3},{8,40},{9,13},... | collective-permute-start | bytes 786440 | tf_op jit(solution)/shard_map/ppermute | solution.py:43
  133.5 7.4 %collective-permute-start.28 = (bf16[1024,128]{1,0:T(8,128)(2,1)}, bf16[1024,128]{1,0:T(8,128)(2,1)S(1)}, u32[]{:S(2)}, u32[]{:S(2)}) collective-permute-start(bf16[1024,128]{1,0:T(8,128)(2,1)} %get-tuple-element.54), channel_id=1, source_target_pairs={{0,48},{1,7},{2,50},{3,1},{4,52},{5,3},{6,54},{7,5},{8,56},{9,15},... | collective-permute-start | bytes 786440 | tf_op jit(solution)/shard_map/ppermute | solution.py:43
  142.3 6.2 %collective-permute-start.31 = (bf16[256,128]{1,0:T(8,128)(2,1)S(1)}, bf16[256,128]{1,0:T(8,128)(2,1)S(1)}, u32[]{:S(2)}, u32[]{:S(2)}) collective-permute-start(bf16[256,128]{1,0:T(8,128)(2,1)S(1)} %get-tuple-element.66), channel_id=1, source_target_pairs={{0,64},{1,65},{2,66},{3,67},{4,68},{5,69},{6,70},{7,71},{8,72},{9,... | collective-permute-start | bytes 196616 | tf_op jit(solution)/shard_map/ppermute | solution.py:43
  142.4 6.2 %collective-permute-start.30 = (bf16[256,128]{1,0:T(8,128)(2,1)S(1)}, bf16[256,128]{1,0:T(8,128)(2,1)S(1)}, u32[]{:S(2)}, u32[]{:S(2)}) collective-permute-start(bf16[256,128]{1,0:T(8,128)(2,1)S(1)} %get-tuple-element.67), channel_id=1, source_target_pairs={{0,8},{1,9},{2,10},{3,11},{4,12},{5,13},{6,14},{7,15},{8,0},{9,1},... | collective-permute-start | bytes 196616 | tf_op jit(solution)/shard_map/ppermute | solution.py:43
  143.4 6.0 %collective-permute-start.29 = (bf16[256,128]{1,0:T(8,128)(2,1)S(1)}, bf16[256,128]{1,0:T(8,128)(2,1)S(1)}, u32[]{:S(2)}, u32[]{:S(2)}) collective-permute-start(bf16[256,128]{1,0:T(8,128)(2,1)S(1)} %get-tuple-element.68), channel_id=1, source_target_pairs={{0,72},{1,73},{2,74},{3,75},{4,76},{5,77},{6,78},{7,79},{8,64},{9,... | collective-permute-start | bytes 196616 | tf_op jit(solution)/shard_map/ppermute | solution.py:43
  145.6 6.7 %copy-start.22 = (bf16[2,256,256]{2,1,0:T(8,128)(2,1)}, bf16[2,256,256]{2,1,0:T(8,128)(2,1)S(1)}, u32[]{:S(2)}) copy-start(bf16[2,256,256]{2,1,0:T(8,128)(2,1)S(1)} %maximum_select_fusion) | copy-start | bytes 786436
  152.3 1.7 collective-permute-start.32
  162.3 23.1 %copy-start.27 = (bf16[512,256]{1,0:T(8,128)(2,1)S(1)}, bf16[512,256]{1,0:T(8,128)(2,1)}, u32[]{:S(2)}) copy-start(bf16[512,256]{1,0:T(8,128)(2,1)} %copy-done.26) | copy-start | bytes 786436
  162.3 18.6 %all-to-all-start = ((bf16[16,128,128]{2,1,0:T(8,128)(2,1)}), bf16[16,128,128]{2,1,0:T(8,128)(2,1)S(1)}, u32[]{:S(2)}, u32[]{:S(2)}) async-start(bf16[16,128,128]{2,1,0:T(8,128)(2,1)} %bitcast.35), calls=%async_computation | async-start | bytes 1048576 | tf_op jit(solution)/shard_map/all_to_all | solution.py:297
  181.7 11.1 %all-to-all-start.1 = ((bf16[8,128,128]{2,1,0:T(8,128)(2,1)}), bf16[8,128,128]{2,1,0:T(8,128)(2,1)S(1)}, u32[]{:S(2)}, u32[]{:S(2)}) async-start(bf16[8,128,128]{2,1,0:T(8,128)(2,1)} %broadcast_in_dim.69), calls=%async_computation.1 | async-start | bytes 524288 | tf_op jit(solution)/shard_map/all_to_all | solution.py:299
  (17 other events, 55.1 us)

commit v4 on v3

--- a/solution.py
+++ b/solution.py
@@ -25,8 +25,8 @@
 STATE = 1024
 GRAPH = 4 * STATE
 TILES = 8
-GROUP = 32
-LIST = TILES * SLOTS + 2 * GROUP
+GROUP = 64
+LIST = TILES * SLOTS + GROUP
 
 
 def permutation(move):
@@ -113,31 +113,34 @@
     adjoint = meta[3, 2]
     left, right = masks[0], masks[1]
 
-    def group(index, carry):
-        first = index * GROUP
-        products = []
-        for lane in range(GROUP):
-            entries = values[pl.ds(pl.multiple_of(meta[2, first + lane], PACK), PACK), :]
-            source = pl.multiple_of(meta[0, first + lane], PACK)
-            vectors = gathered[pl.ds(source, PACK), :]
-            rows = jnp.where(adjoint == 0, entries, vectors)
-            cols = jnp.where(adjoint == 0, vectors, entries)
-            turned = pltpu.roll(cols, BLK, 1)
-            spread = jnp.concatenate([cols * left, turned * left, turned * right, cols * right], axis=0)
-            products.append(jnp.dot(rows, spread, preferred_element_type=jnp.float32))
-        for lane in range(GROUP):
-            target = pl.multiple_of(meta[1, first + lane], PACK)
-            sums[pl.ds(target, PACK), :] += products[lane]
-        return carry
+    def run(forward, begin, end):
+        def group(index, carry):
+            first = index * GROUP
+            products = []
+            for lane in range(GROUP):
+                entries = values[pl.ds(pl.multiple_of(meta[2, first + lane], PACK), PACK), :]
+                vectors = gathered[pl.ds(pl.multiple_of(meta[0, first + lane], PACK), PACK), :]
+                rows, cols = (entries, vectors) if forward else (vectors, entries)
+                turned = pltpu.roll(cols, BLK, 1)
+                spread = jnp.concatenate([cols * left, turned * left, turned * right, cols * right], axis=0)
+                products.append(jnp.dot(rows, spread, preferred_element_type=jnp.float32))
+            for lane in range(GROUP):
+                target = pl.multiple_of(meta[1, first + lane], PACK)
+                sums[pl.ds(target, PACK), :] += products[lane]
+            return carry
+
+        lax.fori_loop(begin, end, group, 0)
 
     early = meta[3, 0] // GROUP
     total = (meta[3, 1] + GROUP - 1) // GROUP
     for copy in tile_copies[: TILES // 2] + part_copies:
         copy.wait()
-    lax.fori_loop(0, early, group, 0)
+    run(True, 0, jnp.where(adjoint == 0, early, 0))
+    run(False, 0, jnp.where(adjoint == 0, 0, early))
     for copy in tile_copies[TILES // 2 :]:
         copy.wait()
-    lax.fori_loop(early, total, group, 0)
+    run(True, early, jnp.where(adjoint == 0, total, early))
+    run(False, early, jnp.where(adjoint == 0, early, total))
     for index, out in enumerate(outs):
         out[...] = sums[index * STATE : (index + 1) * STATE, :].astype(out.dtype)
 
@@ -163,6 +166,57 @@
         compiler_params=pltpu.CompilerParams(vmem_limit_bytes=20 * 2**20),
         name="block_product",
     )(meta, masks, *tiles, *parts)
+
+
+def finish_kernel(place, own, other, feats, hidden, slope, w_second, spread, propagated):
+    core, spot = place[0], place[1]
+    f32, bf16 = jnp.float32, jnp.bfloat16
+    strips, columns = [], []
+    for corner in range(4):
+        hop = (corner - spot) % 4
+        piece = jnp.where(core == 1, own[hop], other[hop]).astype(f32)
+        blocks = [piece[block * PACK : (block + 1) * PACK] for block in range(8)]
+        top = jnp.concatenate([block[:, :BLK] for block in blocks], axis=1)
+        bottom = jnp.concatenate([block[:, BLK:] for block in blocks], axis=1)
+        strips += [top, bottom]
+        rows = pl.ds(pl.multiple_of(core * 4 * PACK, 4 * PACK), 4 * PACK)
+        piece = jnp.where(core == 0, own[hop, rows, :], other[hop, rows, :]).astype(f32)
+        blocks = [piece[block * PACK : (block + 1) * PACK] for block in range(4)]
+        columns.append(
+            jnp.concatenate([half for block in blocks for half in (block[:, :BLK], block[:, BLK:])], axis=0)
+        )
+    propagated[...] = jnp.concatenate(columns, axis=1).astype(bf16)
+    grad_teleport = jnp.concatenate(strips, axis=0).T.astype(bf16)
+    grad_hidden = lax.dot_general(
+        grad_teleport, w_second[...], (((1,), (1,)), ((), ())), preferred_element_type=f32
+    )
+    grad_pre = (grad_hidden * slope[...]).astype(bf16)
+    first = jnp.dot(feats[...], grad_pre, preferred_element_type=f32).astype(bf16)
+    second = jnp.dot(hidden[...], grad_teleport, preferred_element_type=f32).astype(bf16)
+    for half in range(2):
+        for owner in range(8):
+            base = (half * 8 + owner) * LANES
+            for part in range(4):
+                spread[base + part * 16 : base + part * 16 + 16, :] = first[
+                    owner * 16 : owner * 16 + 16, half * 512 + part * LANES : half * 512 + (part + 1) * LANES
+                ]
+            spread[base + BLK : base + 2 * BLK, :] = second[
+                owner * BLK : (owner + 1) * BLK, half * LANES : (half + 1) * LANES
+            ]
+
+
+def finish(place, own, other, feats, hidden, slope, w_second):
+    return pl.pallas_call(
+        finish_kernel,
+        out_shape=(
+            jax.ShapeDtypeStruct((16 * LANES, LANES), jnp.bfloat16),
+            jax.ShapeDtypeStruct((ITEMS, DIM), jnp.bfloat16),
+        ),
+        in_specs=[pl.BlockSpec(memory_space=pltpu.SMEM)] + [pl.BlockSpec(memory_space=pltpu.VMEM)] * 6,
+        out_specs=(pl.BlockSpec(memory_space=pltpu.VMEM),) * 2,
+        compiler_params=pltpu.CompilerParams(vmem_limit_bytes=24 * 2**20),
+        name="finish",
+    )(place, own, other, feats, hidden, slope, w_second)
 
 
 def slot_tables(pointers, columns, zl, y, zh, x, core):
@@ -207,16 +261,6 @@
     return jnp.concatenate([blocks[..., :PACK, :], blocks[..., PACK:, :]], axis=-1)
 
 
-def unpack_rows(blocks):
-    return jnp.concatenate([blocks[..., :BLK], blocks[..., BLK:]], axis=-2)
-
-
-def join_features(pieces, core):
-    blocks = unpack_rows(pieces.reshape(4, 8, PACK, LANES))
-    blocks = jnp.where(core == 0, blocks, jnp.swapaxes(blocks, -1, -2))
-    return blocks.transpose(1, 2, 0, 3).reshape(PIECE, DIM)
-
-
 def silu_slope(value):
     sigma = jax.nn.sigmoid(value)
     return sigma * (1.0 + value * (1.0 - sigma))
@@ -238,7 +282,8 @@
     masks = jnp.stack([lanes < BLK, lanes >= BLK]).astype(bf16)
     masks = jnp.broadcast_to(masks[:, None, :], (2, PACK, LANES))
 
-    start = start_pieces(jnp.stack([core, spot]), message, other, w_first, w_second)
+    place = jnp.stack([core, spot])
+    start = start_pieces(place, message, other, w_first, w_second)
     tile = pack_rows(block_values[0, 0]).reshape(SLOTS * PACK, LANES)
     own_swapped = send(tile, core_move)
     start, own_swapped = lax.optimization_barrier((start, own_swapped))
@@ -259,6 +304,9 @@
     chip_feats = by_tile(message[:ITEMS], other[:ITEMS], core).reshape(PIECE, DIM)
     pre_act = jnp.dot(chip_feats, w_first, preferred_element_type=f32)
     hidden = jax.nn.silu(pre_act).astype(bf16)
+    slope = silu_slope(pre_act)
+    feats_rows = lax.dynamic_index_in_dim(chip_feats.T.reshape(8, 2, 16, PIECE), core, 1, False).reshape(128, PIECE)
+    hidden_rows = lax.dynamic_index_in_dim(hidden.T.reshape(8, 2, 64, PIECE), core, 1, False).reshape(512, PIECE)
     restart = jnp.where(core == 0, ALPHA, 0.0).astype(f32)
     constant = restart * state.astype(f32)
     collected = state.astype(f32)
@@ -271,29 +319,19 @@
         got = [outs[0]] + [send(outs[hop], functools.partial(scatter_ring, hop)) for hop in (1, 2, 3)]
         summed = sum(piece.astype(f32) for piece in got)
         state = ((1.0 - ALPHA) * summed + constant).astype(bf16)
+        if step == 0:
+            state, slope, feats_rows, hidden_rows = lax.optimization_barrier(
+                (state, slope, feats_rows, hidden_rows)
+            )
         if step < STEPS - 1:
             collected = collected + state.astype(f32)
     last = jnp.where(core == 0, state, (ALPHA * collected + state.astype(f32)).astype(bf16))
     last = last.reshape(4, 8 * PACK, LANES)
-    pieces = [last[0]] + [send(last[hop], functools.partial(z_move, -hop)) for hop in (1, 2, 3)]
-    pieces = jnp.stack(pieces)[(jnp.arange(4) - spot) % 4]
-    joined = join_features(pieces, core)
-    ending = send(joined, core_move)
-    propagated = jnp.where(core == 0, joined[:ITEMS], ending[ITEMS:])
-    grad_teleport = jnp.where(core == 0, ending, joined)
-
-    grad_hidden = lax.dot_general(
-        grad_teleport, w_second, (((1,), (1,)), ((), ())), preferred_element_type=f32
+    pieces = jnp.stack([last[0]] + [send(last[hop], functools.partial(z_move, -hop)) for hop in (1, 2, 3)])
+    spread, propagated = finish(
+        place, pieces, send(pieces, core_move), feats_rows, hidden_rows, slope, w_second
     )
-    grad_pre = (grad_hidden * silu_slope(pre_act)).astype(bf16)
-    contract_items = (((0,), (0,)), ((), ()))
-    first = lax.dot_general(chip_feats, grad_pre, contract_items, preferred_element_type=f32).astype(bf16)
-    second = lax.dot_general(hidden, grad_teleport, contract_items, preferred_element_type=f32).astype(bf16)
-    first = lax.dynamic_index_in_dim(first.reshape(8, 2, 16, 1024), core, 1, False)
-    second = lax.dynamic_index_in_dim(second.reshape(8, 2, 64, 256), core, 1, False)
-    first = first.reshape(8, 16, 2, 4, 128).transpose(2, 0, 3, 1, 4)
-    second = second.reshape(8, 4, 16, 2, 128).transpose(3, 0, 1, 2, 4)
-    spread = jnp.concatenate([first, second], axis=2).reshape(16, 128, 128)
+    spread = spread.reshape(16, LANES, LANES)
     landed = lax.all_to_all(spread, ("zl", "zh", "x"), 0, 0)
     mine = jnp.sum(landed.astype(f32), axis=0).astype(bf16)
     shares = lax.all_to_all(jnp.broadcast_to(mine[None], (8, 128, 128)), LOOP, 0, 0)

time: 194 us -> 178 us (0.918)
  blocking collectives: 0 us -> 29.4 us
  waiting for transfers between devices: 73 us -> 51 us
  starting transfers between devices: 58.2 us -> 40.5 us
  local copies, waits for them, and re-layouts: 19.1 us -> 14.2 us
    all_to_all x0 -> x2, blocking collectives: none -> 29.4 us  [the longest x1 18.5 us: body(): landed = lax.all_to_all(spread, ('zl', 'zh', 'x'), 0, 0)]
    all_to_all x2 -> x0, waiting for transfers between devices: 19.5 us -> none  [the longest x1 12.7 us: body(): landed = lax.all_to_all(spread, ('zl', 'zh', 'x'), 0, 0)]
    all_to_all x2 -> x0, starting transfers between devices: 9.03 us -> none  [the longest x1 5.4 us: body(): landed = lax.all_to_all(spread, ('zl', 'zh', 'x'), 0, 0)]
    ppermute x33, starting transfers between devices: 49.2 us -> 40.5 us  [send(): return lax.ppermute(value, AXES, permutation(move))]
    unnamed x63 -> x55, local copies, waits for them, and re-layouts: 7.04 us -> 2.54 us
    dot_general x2 -> x0, matrix products: 3.9 us -> none  [the longest x1 3 us: body(): lax.dot_general(chip_feats, grad_pre, contract_items, preferred_element_t...]
    reshape x4 -> x0, local copies, waits for them, and re-layouts: 3.13 us -> none  [the longest x2 1.92 us: body(): second = second.reshape(8, 4, 16, 2, 128).transpose(3, 0, 1, 2, 4)]
    pallas_call x3, Pallas kernels: 21.1 us -> 18.1 us  [block_product(): pl.pallas_call(product_kernel, out_shape=(piece,) * 4, in_specs=[pl.Block...]
  transfers between devices with their start and end apart: 35 -> 33, of which waited for: 24 -> 18; matrix products, arithmetic and copies ran while one was open for 7% -> 14% of each run, Pallas kernels for 1% -> 1%
where the time goes in v4:
time: 178 us
  waiting for transfers between devices  51 us (29%)
  starting transfers between devices  40.5 us (23%)
  blocking collectives  29.4 us (17%)
  Pallas kernels  22.2 us (12%)
  other arithmetic  15.6 us (9%)
  local copies, waits for them, and re-layouts  14.2 us (8%)
  matrix products  3.35 us (2%)
    ppermute x33, waiting for transfers between devices, send(): return lax.ppermute(value, AXES, permutation(move))  51 us
    ppermute x33, starting transfers between devices, send(): return lax.ppermute(value, AXES, permutation(move))  40.5 us
    all_to_all x1, blocking collectives, body(): landed = lax.all_to_all(spread, ('zl', 'zh', 'x'), 0, 0)  18.5 us
    pallas_call x3, Pallas kernels, block_product(): pl.pallas_call(product_kernel, out_shape=(piece,) * 4, in_specs=[pl.Block...  18.1 us
    all_to_all x1, blocking collectives, body(): lax.all_to_all(jnp.broadcast_to(mine[None], (8, 128, 128)), LOOP, 0, 0)  11 us
  transfers between devices with their start and end apart: 33, of which 18 were waited for; matrix products, arithmetic and copies ran while one was open for 14% of the time, Pallas kernels for 1%

profile of v4, /device:TPU:0, one launch (start us, length us, event | category | flops | bytes accessed | tf_op | source)
XLA Modules:
  0.0 177.6 jit_solution(11771201255591349021)
XLA Ops:
  0.6 1.3 fusion.69
  3.0 4.2 %collective-permute-start.6 = (bf16[2560,128]{1,0:T(8,128)(2,1)S(1)}, bf16[2560,128]{1,0:T(8,128)(2,1)S(1)}, u32[]{:S(2)}, u32[]{:S(2)}) collective-permute-start(bf16[2560,128]{1,0:T(8,128)(2,1)S(1)} %bitcast.69), channel_id=1, source_target_pairs={{0,72},{1,73},{2,74},{3,75},{4,76},{5,77},{6,78},{7,79},{8,64},{9,... | collective-permute-start | bytes 1966088 | tf_op jit(solution)/shard_map/ppermute | solution.py:43
  10.1 1.0 copy-done.7
  11.1 2.0 %start_pieces.1 = bf16[4,288,128]{2,1,0:T(8,128)(2,1)S(1)} custom-call(s32[2]{0:T(128)S(1)} %pad_add_fusion.1.place, bf16[528,256]{1,0:T(8,128)(2,1)S(1)} %pad_maximum_fusion.1.own, bf16[528,256]{1,0:T(8,128)(2,1)} %collective-permute-done.other, bf16[256,1024]{1,0:T(8,128)(2,1)S(1)} %copy-done.7, bf16[1024,256]{1,0:T(8,128)(2,1)S(1)} %copy-done.5), custom_call_target="tpu_custom_call" | custom-call | tf_op jit(solution)/shard_map/start_pieces/pallas_call | solution.py:89
  13.2 3.3 %collective-permute-start.4 = (bf16[288,128]{1,0:T(8,128)(2,1)S(1)}, bf16[288,128]{1,0:T(8,128)(2,1)S(1)}, u32[]{:S(2)}, u32[]{:S(2)}) collective-permute-start(bf16[288,128]{1,0:T(8,128)(2,1)S(1)} %get-tuple-element.71), channel_id=1, source_target_pairs={{0,72},{1,73},{2,74},{3,75},{4,76},{5,77},{6,78},{7,79},{8,64},{9,... | collective-permute-start | bytes 221192 | tf_op jit(solution)/shard_map/ppermute | solution.py:43
  18.0 5.5 %collective-permute-done.6.refs_3_ = bf16[2560,128]{1,0:T(8,128)(2,1)S(1)} collective-permute-done((bf16[2560,128]{1,0:T(8,128)(2,1)S(1)}, bf16[2560,128]{1,0:T(8,128)(2,1)S(1)}, u32[]{:S(2)}, u32[]{:S(2)}) %collective-permute-start.6) | collective-permute-done | bytes 655392 | tf_op jit(solution)/shard_map/ppermute | solution.py:43
  23.5 3.4 %collective-permute-done.5.refs_1_ = bf16[2560,128]{1,0:T(8,128)(2,1)S(1)} collective-permute-done((bf16[2560,128]{1,0:T(8,128)(2,1)S(1)}, bf16[2560,128]{1,0:T(8,128)(2,1)S(1)}, u32[]{:S(2)}, u32[]{:S(2)}) %collective-permute-start.5) | collective-permute-done | bytes 655392 | tf_op jit(solution)/shard_map/ppermute | solution.py:43
  28.2 2.8 %collective-permute-start.9 = (bf16[1024,128]{1,0:T(8,128)(2,1)S(1)}, bf16[1024,128]{1,0:T(8,128)(2,1)}, u32[]{:S(2)}, u32[]{:S(2)}) collective-permute-start(bf16[1024,128]{1,0:T(8,128)(2,1)S(1)} %pad_maximum_fusion.2.refs_8_), channel_id=1, source_target_pairs={{0,6},{1,49},{2,0},{3,51},{4,2},{5,53},{6,4},{7,55},{8,14},{9,57},... | collective-permute-start | bytes 786440 | tf_op jit(solution)/shard_map/ppermute | solution.py:43
  36.4 1.4 fusion.27
  40.1 2.0 %compare_select_fusion.1 = (s32[1,704]{1,0:T(1,128)S(1)}, s32[1,704]{1,0:T(1,128)S(1)}) fusion(s32[]{:T(128)} %axis_index.52, s32[]{:T(128)} %bitcast.19, s32[]{:T(128)} %bitcast.18, s32[704]{0:T(1024)S(1)} %get-tuple-element.68, s32[704]{0:T(1024)} %get-tuple-element.84), kind=kLoop, calls=%fused_computation.52 | loop fusion | flops 6336 | bytes 11276 | tf_op jit(solution)/shard_map/jit(_where)/select_n | solution.py:256
  42.7 4.4 %collective-permute-done.10.refs_2_ = bf16[2560,128]{1,0:T(8,128)(2,1)} collective-permute-done((bf16[2560,128]{1,0:T(8,128)(2,1)}, bf16[2560,128]{1,0:T(8,128)(2,1)}, u32[]{:S(2)}, u32[]{:S(2)}) %collective-permute-start.10) | collective-permute-done | bytes 655392 | tf_op jit(solution)/shard_map/ppermute | solution.py:43
  49.1 3.4 %add_multiply_fusion = (f32[512,1024]{1,0:T(8,128)}, f32[512,1024]{1,0:T(8,128)S(1)}) fusion(bf16[512,256]{1,0:T(8,128)(2,1)S(1)} %bitcast.79, bf16[256,1024]{1,0:T(8,128)(2,1)} %w_first.1), kind=kOutput, calls=%fused_computation.5 | convolution fusion | flops 272105472 | bytes 4980736 | tf_op jit(solution)/shard_map/dot_general | solution.py:305
  52.5 6.6 %block_product.3 = (bf16[1024,128]{1,0:T(8,128)(2,1)S(1)}, bf16[1024,128]{1,0:T(8,128)(2,1)}, bf16[1024,128]{1,0:T(8,128)(2,1)}, bf16[1024,128]{1,0:T(8,128)(2,1)}) custom-call(s32[4,704]{1,0:T(4,128)S(1)} %pad_add_fusion.meta, bf16[2,32,128]{2,1,0:T(8,128)(2,1)S(1)} %broadcast_in_dim.66.masks, bf16[2560,128]{1,0:T(8,128)(2,1)S(1)} %bitcast.72, ...), custom_call_target="tpu_custom_call" | custom-call | tf_op jit(solution)/shard_map/block_product/pallas_call | solution.py:150
  59.9 2.4 %collective-permute-start.14 = (bf16[1024,128]{1,0:T(8,128)(2,1)}, bf16[1024,128]{1,0:T(8,128)(2,1)}, u32[]{:S(2)}, u32[]{:S(2)}) collective-permute-start(bf16[1024,128]{1,0:T(8,128)(2,1)} %get-tuple-element.50), channel_id=1, source_target_pairs={{0,16},{1,3},{2,18},{3,5},{4,20},{5,7},{6,22},{7,1},{8,24},{9,11},... | collective-permute-start | bytes 786440 | tf_op jit(solution)/shard_map/ppermute | solution.py:43
  62.3 1.3 collective-permute-start.15
  63.6 1.3 collective-permute-start.16
  65.0 1.5 fusion.3
  66.5 1.8 %copy.30 = bf16[512,256]{0,1:T(8,128)(2,1)} copy(bf16[512,256]{1,0:T(8,128)(2,1)} %bitcast.80) | data formatting | bytes 524288 | tf_op jit(solution)/shard_map/jit(_where)/select_n | solution.py:270
  68.3 2.3 %copy.31 = bf16[1024,512]{1,0:T(8,128)(2,1)} copy(bf16[1024,512]{0,1:T(8,128)(2,1)} %fusion.3) | data formatting | bytes 2097152 | tf_op jit(solution)/shard_map/convert_element_type | solution.py:306
  70.6 1.0 constant_dynamic-slice_fusion.1
  71.7 1.1 constant_dynamic-slice_fusion
  72.8 1.3 fusion.7.refs_8_
  74.2 4.0 %collective-permute-start.19 = (bf16[1024,128]{1,0:T(8,128)(2,1)S(1)}, bf16[1024,128]{1,0:T(8,128)(2,1)S(1)}, u32[]{:S(2)}, u32[]{:S(2)}) collective-permute-start(bf16[1024,128]{1,0:T(8,128)(2,1)S(1)} %fusion.7.refs_8_), channel_id=1, source_target_pairs={{0,6},{1,49},{2,0},{3,51},{4,2},{5,53},{6,4},{7,55},{8,14},{9,57},... | collective-permute-start | bytes 786440 | tf_op jit(solution)/shard_map/ppermute | solution.py:43
  78.2 1.5 collective-permute-start.18
  79.7 5.2 %collective-permute-done.19.refs_11_ = bf16[1024,128]{1,0:T(8,128)(2,1)S(1)} collective-permute-done((bf16[1024,128]{1,0:T(8,128)(2,1)S(1)}, bf16[1024,128]{1,0:T(8,128)(2,1)S(1)}, u32[]{:S(2)}, u32[]{:S(2)}) %collective-permute-start.19) | collective-permute-done | bytes 262176 | tf_op jit(solution)/shard_map/ppermute | solution.py:43
  84.9 1.2 collective-permute-done.18.refs_10_
  86.2 2.7 %collective-permute-done.17.refs_9_ = bf16[1024,128]{1,0:T(8,128)(2,1)S(1)} collective-permute-done((bf16[1024,128]{1,0:T(8,128)(2,1)S(1)}, bf16[1024,128]{1,0:T(8,128)(2,1)S(1)}, u32[]{:S(2)}, u32[]{:S(2)}) %collective-permute-start.17) | collective-permute-done | bytes 262176 | tf_op jit(solution)/shard_map/ppermute | solution.py:43
  88.9 5.6 %block_product.4 = (bf16[1024,128]{1,0:T(8,128)(2,1)S(1)}, bf16[1024,128]{1,0:T(8,128)(2,1)S(1)}, bf16[1024,128]{1,0:T(8,128)(2,1)S(1)}, bf16[1024,128]{1,0:T(8,128)(2,1)S(1)}) custom-call(s32[4,704]{1,0:T(4,128)S(1)} %copy-done.11, bf16[2,32,128]{2,1,0:T(8,128)(2,1)S(1)} %broadcast_in_dim.66.masks, bf16[2560,128]{1,0:T(8,128)(2,1)S(1)} %bitcast.73, ...), custom_call_target="tpu_custom_call" | custom-call | tf_op jit(solution)/shard_map/block_product/pallas_call | solution.py:150
  95.4 2.7 %collective-permute-start.22 = (bf16[1024,128]{1,0:T(8,128)(2,1)S(1)}, bf16[1024,128]{1,0:T(8,128)(2,1)S(1)}, u32[]{:S(2)}, u32[]{:S(2)}) collective-permute-start(bf16[1024,128]{1,0:T(8,128)(2,1)S(1)} %get-tuple-element.57), channel_id=1, source_target_pairs={{0,48},{1,7},{2,50},{3,1},{4,52},{5,3},{6,54},{7,5},{8,56},{9,15},... | collective-permute-start | bytes 786440 | tf_op jit(solution)/shard_map/ppermute | solution.py:43
  98.0 6.9 %collective-permute-done.20 = bf16[1024,128]{1,0:T(8,128)(2,1)S(1)} collective-permute-done((bf16[1024,128]{1,0:T(8,128)(2,1)S(1)}, bf16[1024,128]{1,0:T(8,128)(2,1)S(1)}, u32[]{:S(2)}, u32[]{:S(2)}) %collective-permute-start.20) | collective-permute-done | bytes 262176 | tf_op jit(solution)/shard_map/ppermute | solution.py:43
  105.0 1.9 %collective-permute-done.22 = bf16[1024,128]{1,0:T(8,128)(2,1)S(1)} collective-permute-done((bf16[1024,128]{1,0:T(8,128)(2,1)S(1)}, bf16[1024,128]{1,0:T(8,128)(2,1)S(1)}, u32[]{:S(2)}, u32[]{:S(2)}) %collective-permute-start.22) | collective-permute-done | bytes 262176 | tf_op jit(solution)/shard_map/ppermute | solution.py:43
  107.2 3.2 %collective-permute-start.24 = (bf16[1024,128]{1,0:T(8,128)(2,1)S(1)}, bf16[1024,128]{1,0:T(8,128)(2,1)S(1)}, u32[]{:S(2)}, u32[]{:S(2)}) collective-permute-start(bf16[1024,128]{1,0:T(8,128)(2,1)S(1)} %fusion.8.refs_8_), channel_id=1, source_target_pairs={{0,4},{1,33},{2,6},{3,35},{4,0},{5,37},{6,2},{7,39},{8,12},{9,41},... | collective-permute-start | bytes 786440 | tf_op jit(solution)/shard_map/ppermute | solution.py:43
  110.4 1.3 collective-permute-start.23
  111.7 1.8 %collective-permute-done.25.refs_11_ = bf16[1024,128]{1,0:T(8,128)(2,1)S(1)} collective-permute-done((bf16[1024,128]{1,0:T(8,128)(2,1)S(1)}, bf16[1024,128]{1,0:T(8,128)(2,1)S(1)}, u32[]{:S(2)}, u32[]{:S(2)}) %collective-permute-start.25) | collective-permute-done | bytes 262176 | tf_op jit(solution)/shard_map/ppermute | solution.py:43
  113.5 1.6 collective-permute-done.24.refs_10_
  115.1 2.8 %collective-permute-done.23.refs_9_ = bf16[1024,128]{1,0:T(8,128)(2,1)S(1)} collective-permute-done((bf16[1024,128]{1,0:T(8,128)(2,1)S(1)}, bf16[1024,128]{1,0:T(8,128)(2,1)S(1)}, u32[]{:S(2)}, u32[]{:S(2)}) %collective-permute-start.23) | collective-permute-done | bytes 262176 | tf_op jit(solution)/shard_map/ppermute | solution.py:43
  118.0 5.8 %block_product.5 = (bf16[1024,128]{1,0:T(8,128)(2,1)S(1)}, bf16[1024,128]{1,0:T(8,128)(2,1)S(1)}, bf16[1024,128]{1,0:T(8,128)(2,1)S(1)}, bf16[1024,128]{1,0:T(8,128)(2,1)S(1)}) custom-call(s32[4,704]{1,0:T(4,128)S(1)} %copy-done.11, bf16[2,32,128]{2,1,0:T(8,128)(2,1)S(1)} %broadcast_in_dim.66.masks, bf16[2560,128]{1,0:T(8,128)(2,1)S(1)} %bitcast.74, ...), custom_call_target="tpu_custom_call" | custom-call | tf_op jit(solution)/shard_map/block_product/pallas_call | solution.py:150
  123.9 1.6 collective-permute-start.26
  125.4 2.8 %collective-permute-start.27 = (bf16[1024,128]{1,0:T(8,128)(2,1)S(1)}, bf16[1024,128]{1,0:T(8,128)(2,1)S(1)}, u32[]{:S(2)}, u32[]{:S(2)}) collective-permute-start(bf16[1024,128]{1,0:T(8,128)(2,1)S(1)} %get-tuple-element.60), channel_id=1, source_target_pairs={{0,32},{1,5},{2,34},{3,7},{4,36},{5,1},{6,38},{7,3},{8,40},{9,13},... | collective-permute-start | bytes 786440 | tf_op jit(solution)/shard_map/ppermute | solution.py:43
  128.2 3.3 %collective-permute-done.26 = bf16[1024,128]{1,0:T(8,128)(2,1)S(1)} collective-permute-done((bf16[1024,128]{1,0:T(8,128)(2,1)S(1)}, bf16[1024,128]{1,0:T(8,128)(2,1)S(1)}, u32[]{:S(2)}, u32[]{:S(2)}) %collective-permute-start.26) | collective-permute-done | bytes 262176 | tf_op jit(solution)/shard_map/ppermute | solution.py:43
  131.5 3.8 %collective-permute-done.27 = bf16[1024,128]{1,0:T(8,128)(2,1)S(1)} collective-permute-done((bf16[1024,128]{1,0:T(8,128)(2,1)S(1)}, bf16[1024,128]{1,0:T(8,128)(2,1)S(1)}, u32[]{:S(2)}, u32[]{:S(2)}) %collective-permute-start.27) | collective-permute-done | bytes 262176 | tf_op jit(solution)/shard_map/ppermute | solution.py:43
  135.8 1.1 collective-permute-start.30
  136.9 2.1 %collective-permute-start.29 = (bf16[256,128]{1,0:T(8,128)(2,1)S(1)}, bf16[256,128]{1,0:T(8,128)(2,1)S(1)}, u32[]{:S(2)}, u32[]{:S(2)}) collective-permute-start(bf16[256,128]{1,0:T(8,128)(2,1)S(1)} %get-tuple-element.78), channel_id=1, source_target_pairs={{0,72},{1,73},{2,74},{3,75},{4,76},{5,77},{6,78},{7,79},{8,64},{9,... | collective-permute-start | bytes 196616 | tf_op jit(solution)/shard_map/ppermute | solution.py:43
  139.0 2.9 %collective-permute-done.31 = bf16[256,128]{1,0:T(8,128)(2,1)S(1)} collective-permute-done((bf16[256,128]{1,0:T(8,128)(2,1)S(1)}, bf16[256,128]{1,0:T(8,128)(2,1)S(1)}, u32[]{:S(2)}, u32[]{:S(2)}) %collective-permute-start.31) | collective-permute-done | bytes 65568 | tf_op jit(solution)/shard_map/ppermute | solution.py:43
  142.9 1.5 collective-permute-done.32.other
  144.5 2.1 %finish.1 = (bf16[2048,128]{1,0:T(8,128)(2,1)S(1)}, bf16[256,256]{1,0:T(8,128)(2,1)}) custom-call(s32[2]{0:T(128)S(1)} %copy-done.13, bf16[4,256,128]{2,1,0:T(8,128)(2,1)S(1)} %pad_maximum_fusion.3.own, bf16[4,256,128]{2,1,0:T(8,128)(2,1)S(1)} %collective-permute-done.32.other, bf16[128,512]{1,0:T(8,128)(2,1)S(1)} %bitcast.76, ...), custom_call_target="tpu_custom_call" | custom-call | tf_op jit(solution)/shard_map/finish/pallas_call | solution.py:209
  146.6 18.5 %all_to_all.10 = bf16[16,128,128]{2,1,0:T(8,128)(2,1)S(1)} all-to-all(bf16[16,128,128]{2,1,0:T(8,128)(2,1)S(1)} %bitcast.77), channel_id=1, replica_groups=mesh['zl'=2,'y'=4,'zh'=2,'x'=4,'c'=2] {'zl','zh','x'}, dimensions={0} | all-to-all | bytes 1048576 | tf_op jit(solution)/shard_map/all_to_all | solution.py:335
  165.2 11.0 %all_to_all.11 = bf16[8,128,128]{2,1,0:T(8,128)(2,1)S(1)} all-to-all(bf16[8,128,128]{2,1,0:T(8,128)(2,1)S(1)} %broadcast_in_dim.68), channel_id=1, replica_groups=mesh['zl'=2,'y'=4,'zh'=2,'x'=4,'c'=2] {'zl','y'}, dimensions={0} | all-to-all | bytes 524288 | tf_op jit(solution)/shard_map/all_to_all | solution.py:337
  (140 shorter events, 21.8 us)
Async XLA Ops:
  1.9 8.1 %copy-start.5 = (bf16[1024,256]{1,0:T(8,128)(2,1)S(1)}, bf16[1024,256]{1,0:T(8,128)(2,1)}, u32[]{:S(2)}) copy-start(bf16[1024,256]{1,0:T(8,128)(2,1)} %w_second.3) | copy-start | bytes 1572868
  3.0 20.6 %collective-permute-start.6 = (bf16[2560,128]{1,0:T(8,128)(2,1)S(1)}, bf16[2560,128]{1,0:T(8,128)(2,1)S(1)}, u32[]{:S(2)}, u32[]{:S(2)}) collective-permute-start(bf16[2560,128]{1,0:T(8,128)(2,1)S(1)} %bitcast.69), channel_id=1, source_target_pairs={{0,72},{1,73},{2,74},{3,75},{4,76},{5,77},{6,78},{7,79},{8,64},{9,... | collective-permute-start | bytes 1966088 | tf_op jit(solution)/shard_map/ppermute | solution.py:43
  7.2 19.8 %collective-permute-start.5 = (bf16[2560,128]{1,0:T(8,128)(2,1)S(1)}, bf16[2560,128]{1,0:T(8,128)(2,1)S(1)}, u32[]{:S(2)}, u32[]{:S(2)}) collective-permute-start(bf16[2560,128]{1,0:T(8,128)(2,1)S(1)} %bitcast.70), channel_id=1, source_target_pairs={{0,64},{1,65},{2,66},{3,67},{4,68},{5,69},{6,70},{7,71},{8,72},{9,... | collective-permute-start | bytes 1966088 | tf_op jit(solution)/shard_map/ppermute | solution.py:43
  7.2 6.0 %collective-permute-start.1 = (bf16[2560,128]{1,0:T(8,128)(2,1)S(1)}, bf16[2560,128]{1,0:T(8,128)(2,1)S(1)}, u32[]{:S(2)}, u32[]{:S(2)}) collective-permute-start(bf16[2560,128]{1,0:T(8,128)(2,1)S(1)} %bitcast.71), channel_id=1, source_target_pairs={{0,1},{1,0},{2,3},{3,2},{4,5},{5,4},{6,7},{7,6},{8,9},{9,8},{10,11... | collective-permute-start | bytes 1966088 | tf_op jit(solution)/shard_map/ppermute | solution.py:43
  8.2 1.9 %collective-permute-start = (bf16[528,256]{1,0:T(8,128)(2,1)S(1)}, bf16[528,256]{1,0:T(8,128)(2,1)}, u32[]{:S(2)}, u32[]{:S(2)}) collective-permute-start(bf16[528,256]{1,0:T(8,128)(2,1)S(1)} %pad_maximum_fusion.1.own), channel_id=1, source_target_pairs={{0,1},{1,0},{2,3},{3,2},{4,5},{5,4},{6,7},{7,6},{8,9},{9,8},{10,11... | collective-permute-start | bytes 811016 | tf_op jit(solution)/shard_map/ppermute | solution.py:43
  9.4 18.6 %copy-start.12 = (s32[2]{0:T(128)}, s32[2]{0:T(128)S(1)}, u32[]{:S(2)}) copy-start(s32[2]{0:T(128)S(1)} %pad_add_fusion.1.place) | copy-start | bytes 28
  13.2 13.7 %collective-permute-start.4 = (bf16[288,128]{1,0:T(8,128)(2,1)S(1)}, bf16[288,128]{1,0:T(8,128)(2,1)S(1)}, u32[]{:S(2)}, u32[]{:S(2)}) collective-permute-start(bf16[288,128]{1,0:T(8,128)(2,1)S(1)} %get-tuple-element.71), channel_id=1, source_target_pairs={{0,72},{1,73},{2,74},{3,75},{4,76},{5,77},{6,78},{7,79},{8,64},{9,... | collective-permute-start | bytes 221192 | tf_op jit(solution)/shard_map/ppermute | solution.py:43
  16.5 10.4 %collective-permute-start.3 = (bf16[288,128]{1,0:T(8,128)(2,1)S(1)}, bf16[288,128]{1,0:T(8,128)(2,1)S(1)}, u32[]{:S(2)}, u32[]{:S(2)}) collective-permute-start(bf16[288,128]{1,0:T(8,128)(2,1)S(1)} %get-tuple-element.72), channel_id=1, source_target_pairs={{0,8},{1,9},{2,10},{3,11},{4,12},{5,13},{6,14},{7,15},{8,0},{9,1},... | collective-permute-start | bytes 221192 | tf_op jit(solution)/shard_map/ppermute | solution.py:43
  16.5 11.2 %collective-permute-start.2 = (bf16[288,128]{1,0:T(8,128)(2,1)S(1)}, bf16[288,128]{1,0:T(8,128)(2,1)S(1)}, u32[]{:S(2)}, u32[]{:S(2)}) collective-permute-start(bf16[288,128]{1,0:T(8,128)(2,1)S(1)} %get-tuple-element.73), channel_id=1, source_target_pairs={{0,64},{1,65},{2,66},{3,67},{4,68},{5,69},{6,70},{7,71},{8,72},{9,... | collective-permute-start | bytes 221192 | tf_op jit(solution)/shard_map/ppermute | solution.py:43
  28.2 13.9 %collective-permute-start.9 = (bf16[1024,128]{1,0:T(8,128)(2,1)S(1)}, bf16[1024,128]{1,0:T(8,128)(2,1)}, u32[]{:S(2)}, u32[]{:S(2)}) collective-permute-start(bf16[1024,128]{1,0:T(8,128)(2,1)S(1)} %pad_maximum_fusion.2.refs_8_), channel_id=1, source_target_pairs={{0,6},{1,49},{2,0},{3,51},{4,2},{5,53},{6,4},{7,55},{8,14},{9,57},... | collective-permute-start | bytes 786440 | tf_op jit(solution)/shard_map/ppermute | solution.py:43
  31.0 11.7 %collective-permute-start.8 = (bf16[1024,128]{1,0:T(8,128)(2,1)S(1)}, bf16[1024,128]{1,0:T(8,128)(2,1)}, u32[]{:S(2)}, u32[]{:S(2)}) collective-permute-start(bf16[1024,128]{1,0:T(8,128)(2,1)S(1)} %pad_maximum_fusion.2.refs_8_), channel_id=1, source_target_pairs={{0,4},{1,33},{2,6},{3,35},{4,0},{5,37},{6,2},{7,39},{8,12},{9,41},... | collective-permute-start | bytes 786440 | tf_op jit(solution)/shard_map/ppermute | solution.py:43
  31.8 10.9 %collective-permute-start.7 = (bf16[1024,128]{1,0:T(8,128)(2,1)S(1)}, bf16[1024,128]{1,0:T(8,128)(2,1)}, u32[]{:S(2)}, u32[]{:S(2)}) collective-permute-start(bf16[1024,128]{1,0:T(8,128)(2,1)S(1)} %pad_maximum_fusion.2.refs_8_), channel_id=1, source_target_pairs={{0,2},{1,17},{2,4},{3,19},{4,6},{5,21},{6,0},{7,23},{8,10},{9,25},... | collective-permute-start | bytes 786440 | tf_op jit(solution)/shard_map/ppermute | solution.py:43
  34.1 18.4 %collective-permute-start.11 = (bf16[2560,128]{1,0:T(8,128)(2,1)S(1)}, bf16[2560,128]{1,0:T(8,128)(2,1)S(1)}, u32[]{:S(2)}, u32[]{:S(2)}) collective-permute-start(bf16[2560,128]{1,0:T(8,128)(2,1)S(1)} %collective-permute-done.5.refs_1_), channel_id=1, source_target_pairs={{0,1},{1,0},{2,3},{3,2},{4,5},{5,4},{6,7},{7,6},{8,9},{9,8},{10,11... | collective-permute-start | bytes 1966088 | tf_op jit(solution)/shard_map/ppermute | solution.py:43
  35.0 12.1 %collective-permute-start.10 = (bf16[2560,128]{1,0:T(8,128)(2,1)}, bf16[2560,128]{1,0:T(8,128)(2,1)}, u32[]{:S(2)}, u32[]{:S(2)}) collective-permute-start(bf16[2560,128]{1,0:T(8,128)(2,1)} %broadcast_select_fusion), channel_id=1, source_target_pairs={{0,64},{1,73},{2,66},{3,75},{4,68},{5,77},{6,70},{7,79},{8,72},{9,... | collective-permute-start | bytes 1966088 | tf_op jit(solution)/shard_map/ppermute | solution.py:43
  42.1 10.4 %copy-start.10 = (s32[4,704]{1,0:T(4,128)}, s32[4,704]{1,0:T(4,128)S(1)}, u32[]{:S(2)}) copy-start(s32[4,704]{1,0:T(4,128)S(1)} %pad_add_fusion.meta) | copy-start | bytes 33796
  42.1 10.3 %collective-permute-start.13 = (bf16[2560,128]{1,0:T(8,128)(2,1)S(1)}, bf16[2560,128]{1,0:T(8,128)(2,1)S(1)}, u32[]{:S(2)}, u32[]{:S(2)}) collective-permute-start(bf16[2560,128]{1,0:T(8,128)(2,1)S(1)} %collective-permute-done.6.refs_3_), channel_id=1, source_target_pairs={{0,1},{1,0},{2,3},{3,2},{4,5},{5,4},{6,7},{7,6},{8,9},{9,8},{10,11... | collective-permute-start | bytes 1966088 | tf_op jit(solution)/shard_map/ppermute | solution.py:43
  47.2 5.3 %collective-permute-start.12 = (bf16[2560,128]{1,0:T(8,128)(2,1)}, bf16[2560,128]{1,0:T(8,128)(2,1)S(1)}, u32[]{:S(2)}, u32[]{:S(2)}) collective-permute-start(bf16[2560,128]{1,0:T(8,128)(2,1)} %collective-permute-done.10.refs_2_), channel_id=1, source_target_pairs={{0,1},{1,0},{2,3},{3,2},{4,5},{5,4},{6,7},{7,6},{8,9},{9,8},{10,11... | collective-permute-start | bytes 1966088 | tf_op jit(solution)/shard_map/ppermute | solution.py:43
  52.5 6.7 %copy-start = (bf16[2560,128]{1,0:T(8,128)(2,1)}, bf16[2560,128]{1,0:T(8,128)(2,1)S(1)}, u32[]{:S(2)}) copy-start(bf16[2560,128]{1,0:T(8,128)(2,1)S(1)} %collective-permute-done.13.refs_7_) | copy-start | bytes 1966084
  52.5 6.6 %copy-start.2 = (bf16[2560,128]{1,0:T(8,128)(2,1)}, bf16[2560,128]{1,0:T(8,128)(2,1)S(1)}, u32[]{:S(2)}) copy-start(bf16[2560,128]{1,0:T(8,128)(2,1)S(1)} %collective-permute-done.12.refs_6_) | copy-start | bytes 1966084
  59.9 12.8 %collective-permute-start.14 = (bf16[1024,128]{1,0:T(8,128)(2,1)}, bf16[1024,128]{1,0:T(8,128)(2,1)}, u32[]{:S(2)}, u32[]{:S(2)}) collective-permute-start(bf16[1024,128]{1,0:T(8,128)(2,1)} %get-tuple-element.50), channel_id=1, source_target_pairs={{0,16},{1,3},{2,18},{3,5},{4,20},{5,7},{6,22},{7,1},{8,24},{9,11},... | collective-permute-start | bytes 786440 | tf_op jit(solution)/shard_map/ppermute | solution.py:43
  62.3 10.5 %collective-permute-start.15 = (bf16[1024,128]{1,0:T(8,128)(2,1)}, bf16[1024,128]{1,0:T(8,128)(2,1)}, u32[]{:S(2)}, u32[]{:S(2)}) collective-permute-start(bf16[1024,128]{1,0:T(8,128)(2,1)} %get-tuple-element.51), channel_id=1, source_target_pairs={{0,32},{1,5},{2,34},{3,7},{4,36},{5,1},{6,38},{7,3},{8,40},{9,13},... | collective-permute-start | bytes 786440 | tf_op jit(solution)/shard_map/ppermute | solution.py:43
  63.6 9.1 %collective-permute-start.16 = (bf16[1024,128]{1,0:T(8,128)(2,1)}, bf16[1024,128]{1,0:T(8,128)(2,1)}, u32[]{:S(2)}, u32[]{:S(2)}) collective-permute-start(bf16[1024,128]{1,0:T(8,128)(2,1)} %get-tuple-element.52), channel_id=1, source_target_pairs={{0,48},{1,7},{2,50},{3,1},{4,52},{5,3},{6,54},{7,5},{8,56},{9,15},... | collective-permute-start | bytes 786440 | tf_op jit(solution)/shard_map/ppermute | solution.py:43
  70.6 18.2 %copy-start.1 = (bf16[2560,128]{1,0:T(8,128)(2,1)S(1)}, bf16[2560,128]{1,0:T(8,128)(2,1)}, u32[]{:S(2)}) copy-start(bf16[2560,128]{1,0:T(8,128)(2,1)} %copy-done) | copy-start | bytes 1966084
  70.6 18.2 %copy-start.3 = (bf16[2560,128]{1,0:T(8,128)(2,1)S(1)}, bf16[2560,128]{1,0:T(8,128)(2,1)}, u32[]{:S(2)}) copy-start(bf16[2560,128]{1,0:T(8,128)(2,1)} %copy-done.2) | copy-start | bytes 1966084
  70.6 18.2 %copy-start.11 = (s32[4,704]{1,0:T(4,128)S(1)}, s32[4,704]{1,0:T(4,128)}, u32[]{:S(2)}) copy-start(s32[4,704]{1,0:T(4,128)} %copy-done.10) | copy-start | bytes 33796
  74.1 32.7 %copy-start.15 = (bf16[256,128]{1,0:T(8,128)(2,1)S(1)}, bf16[256,128]{1,0:T(8,128)(2,1)}, u32[]{:S(2)}) copy-start(bf16[256,128]{1,0:T(8,128)(2,1)} %copy-done.14) | copy-start | bytes 196612
  74.2 32.7 %copy-start.17 = (bf16[256,128]{1,0:T(8,128)(2,1)S(1)}, bf16[256,128]{1,0:T(8,128)(2,1)}, u32[]{:S(2)}) copy-start(bf16[256,128]{1,0:T(8,128)(2,1)} %copy-done.16) | copy-start | bytes 196612
  74.2 32.7 %copy-start.19 = (bf16[256,128]{1,0:T(8,128)(2,1)S(1)}, bf16[256,128]{1,0:T(8,128)(2,1)}, u32[]{:S(2)}) copy-start(bf16[256,128]{1,0:T(8,128)(2,1)} %copy-done.18) | copy-start | bytes 196612
  74.2 32.7 %copy-start.21 = (bf16[256,128]{1,0:T(8,128)(2,1)S(1)}, bf16[256,128]{1,0:T(8,128)(2,1)}, u32[]{:S(2)}) copy-start(bf16[256,128]{1,0:T(8,128)(2,1)} %copy-done.20) | copy-start | bytes 196612
  74.2 10.7 %collective-permute-start.19 = (bf16[1024,128]{1,0:T(8,128)(2,1)S(1)}, bf16[1024,128]{1,0:T(8,128)(2,1)S(1)}, u32[]{:S(2)}, u32[]{:S(2)}) collective-permute-start(bf16[1024,128]{1,0:T(8,128)(2,1)S(1)} %fusion.7.refs_8_), channel_id=1, source_target_pairs={{0,6},{1,49},{2,0},{3,51},{4,2},{5,53},{6,4},{7,55},{8,14},{9,57},... | collective-permute-start | bytes 786440 | tf_op jit(solution)/shard_map/ppermute | solution.py:43
  78.2 8.0 %collective-permute-start.18 = (bf16[1024,128]{1,0:T(8,128)(2,1)S(1)}, bf16[1024,128]{1,0:T(8,128)(2,1)S(1)}, u32[]{:S(2)}, u32[]{:S(2)}) collective-permute-start(bf16[1024,128]{1,0:T(8,128)(2,1)S(1)} %fusion.7.refs_8_), channel_id=1, source_target_pairs={{0,4},{1,33},{2,6},{3,35},{4,0},{5,37},{6,2},{7,39},{8,12},{9,41},... | collective-permute-start | bytes 786440 | tf_op jit(solution)/shard_map/ppermute | solution.py:43
  79.7 9.2 %collective-permute-start.17 = (bf16[1024,128]{1,0:T(8,128)(2,1)S(1)}, bf16[1024,128]{1,0:T(8,128)(2,1)S(1)}, u32[]{:S(2)}, u32[]{:S(2)}) collective-permute-start(bf16[1024,128]{1,0:T(8,128)(2,1)S(1)} %fusion.7.refs_8_), channel_id=1, source_target_pairs={{0,2},{1,17},{2,4},{3,19},{4,6},{5,21},{6,0},{7,23},{8,10},{9,25},... | collective-permute-start | bytes 786440 | tf_op jit(solution)/shard_map/ppermute | solution.py:43
  94.5 10.5 %collective-permute-start.20 = (bf16[1024,128]{1,0:T(8,128)(2,1)S(1)}, bf16[1024,128]{1,0:T(8,128)(2,1)S(1)}, u32[]{:S(2)}, u32[]{:S(2)}) collective-permute-start(bf16[1024,128]{1,0:T(8,128)(2,1)S(1)} %get-tuple-element.55), channel_id=1, source_target_pairs={{0,16},{1,3},{2,18},{3,5},{4,20},{5,7},{6,22},{7,1},{8,24},{9,11},... | collective-permute-start | bytes 786440 | tf_op jit(solution)/shard_map/ppermute | solution.py:43
  95.3 9.7 %collective-permute-start.21 = (bf16[1024,128]{1,0:T(8,128)(2,1)S(1)}, bf16[1024,128]{1,0:T(8,128)(2,1)S(1)}, u32[]{:S(2)}, u32[]{:S(2)}) collective-permute-start(bf16[1024,128]{1,0:T(8,128)(2,1)S(1)} %get-tuple-element.56), channel_id=1, source_target_pairs={{0,32},{1,5},{2,34},{3,7},{4,36},{5,1},{6,38},{7,3},{8,40},{9,13},... | collective-permute-start | bytes 786440 | tf_op jit(solution)/shard_map/ppermute | solution.py:43
  95.4 11.5 %collective-permute-start.22 = (bf16[1024,128]{1,0:T(8,128)(2,1)S(1)}, bf16[1024,128]{1,0:T(8,128)(2,1)S(1)}, u32[]{:S(2)}, u32[]{:S(2)}) collective-permute-start(bf16[1024,128]{1,0:T(8,128)(2,1)S(1)} %get-tuple-element.57), channel_id=1, source_target_pairs={{0,48},{1,7},{2,50},{3,1},{4,52},{5,3},{6,54},{7,5},{8,56},{9,15},... | collective-permute-start | bytes 786440 | tf_op jit(solution)/shard_map/ppermute | solution.py:43
  107.1 6.4 %collective-permute-start.25 = (bf16[1024,128]{1,0:T(8,128)(2,1)S(1)}, bf16[1024,128]{1,0:T(8,128)(2,1)S(1)}, u32[]{:S(2)}, u32[]{:S(2)}) collective-permute-start(bf16[1024,128]{1,0:T(8,128)(2,1)S(1)} %fusion.8.refs_8_), channel_id=1, source_target_pairs={{0,6},{1,49},{2,0},{3,51},{4,2},{5,53},{6,4},{7,55},{8,14},{9,57},... | collective-permute-start | bytes 786440 | tf_op jit(solution)/shard_map/ppermute | solution.py:43
  107.2 8.0 %collective-permute-start.24 = (bf16[1024,128]{1,0:T(8,128)(2,1)S(1)}, bf16[1024,128]{1,0:T(8,128)(2,1)S(1)}, u32[]{:S(2)}, u32[]{:S(2)}) collective-permute-start(bf16[1024,128]{1,0:T(8,128)(2,1)S(1)} %fusion.8.refs_8_), channel_id=1, source_target_pairs={{0,4},{1,33},{2,6},{3,35},{4,0},{5,37},{6,2},{7,39},{8,12},{9,41},... | collective-permute-start | bytes 786440 | tf_op jit(solution)/shard_map/ppermute | solution.py:43
  110.4 7.6 %collective-permute-start.23 = (bf16[1024,128]{1,0:T(8,128)(2,1)S(1)}, bf16[1024,128]{1,0:T(8,128)(2,1)S(1)}, u32[]{:S(2)}, u32[]{:S(2)}) collective-permute-start(bf16[1024,128]{1,0:T(8,128)(2,1)S(1)} %fusion.8.refs_8_), channel_id=1, source_target_pairs={{0,2},{1,17},{2,4},{3,19},{4,6},{5,21},{6,0},{7,23},{8,10},{9,25},... | collective-permute-start | bytes 786440 | tf_op jit(solution)/shard_map/ppermute | solution.py:43
  123.8 20.6 %copy-start.4 = (f32[512,1024]{1,0:T(8,128)S(1)}, f32[512,1024]{1,0:T(8,128)}, u32[]{:S(2)}) copy-start(f32[512,1024]{1,0:T(8,128)} %get-tuple-element.64.slope) | copy-start | bytes 6291460
  123.8 20.6 %copy-start.6 = (bf16[1024,256]{1,0:T(8,128)(2,1)S(1)}, bf16[1024,256]{1,0:T(8,128)(2,1)}, u32[]{:S(2)}) copy-start(bf16[1024,256]{1,0:T(8,128)(2,1)} %w_second.3) | copy-start | bytes 1572868
  123.9 20.6 %copy-start.13 = (s32[2]{0:T(128)S(1)}, s32[2]{0:T(128)}, u32[]{:S(2)}) copy-start(s32[2]{0:T(128)} %copy-done.12) | copy-start | bytes 28
  123.9 7.7 %collective-permute-start.26 = (bf16[1024,128]{1,0:T(8,128)(2,1)S(1)}, bf16[1024,128]{1,0:T(8,128)(2,1)S(1)}, u32[]{:S(2)}, u32[]{:S(2)}) collective-permute-start(bf16[1024,128]{1,0:T(8,128)(2,1)S(1)} %get-tuple-element.59), channel_id=1, source_target_pairs={{0,16},{1,3},{2,18},{3,5},{4,20},{5,7},{6,22},{7,1},{8,24},{9,11},... | collective-permute-start | bytes 786440 | tf_op jit(solution)/shard_map/ppermute | solution.py:43
  125.4 9.9 %collective-permute-start.27 = (bf16[1024,128]{1,0:T(8,128)(2,1)S(1)}, bf16[1024,128]{1,0:T(8,128)(2,1)S(1)}, u32[]{:S(2)}, u32[]{:S(2)}) collective-permute-start(bf16[1024,128]{1,0:T(8,128)(2,1)S(1)} %get-tuple-element.60), channel_id=1, source_target_pairs={{0,32},{1,5},{2,34},{3,7},{4,36},{5,1},{6,38},{7,3},{8,40},{9,13},... | collective-permute-start | bytes 786440 | tf_op jit(solution)/shard_map/ppermute | solution.py:43
  128.2 7.2 %collective-permute-start.28 = (bf16[1024,128]{1,0:T(8,128)(2,1)S(1)}, bf16[1024,128]{1,0:T(8,128)(2,1)S(1)}, u32[]{:S(2)}, u32[]{:S(2)}) collective-permute-start(bf16[1024,128]{1,0:T(8,128)(2,1)S(1)} %get-tuple-element.61), channel_id=1, source_target_pairs={{0,48},{1,7},{2,50},{3,1},{4,52},{5,3},{6,54},{7,5},{8,56},{9,15},... | collective-permute-start | bytes 786440 | tf_op jit(solution)/shard_map/ppermute | solution.py:43
  135.7 6.2 %collective-permute-start.31 = (bf16[256,128]{1,0:T(8,128)(2,1)S(1)}, bf16[256,128]{1,0:T(8,128)(2,1)S(1)}, u32[]{:S(2)}, u32[]{:S(2)}) collective-permute-start(bf16[256,128]{1,0:T(8,128)(2,1)S(1)} %get-tuple-element.76), channel_id=1, source_target_pairs={{0,64},{1,65},{2,66},{3,67},{4,68},{5,69},{6,70},{7,71},{8,72},{9,... | collective-permute-start | bytes 196616 | tf_op jit(solution)/shard_map/ppermute | solution.py:43
  135.8 6.2 %collective-permute-start.30 = (bf16[256,128]{1,0:T(8,128)(2,1)S(1)}, bf16[256,128]{1,0:T(8,128)(2,1)S(1)}, u32[]{:S(2)}, u32[]{:S(2)}) collective-permute-start(bf16[256,128]{1,0:T(8,128)(2,1)S(1)} %get-tuple-element.77), channel_id=1, source_target_pairs={{0,8},{1,9},{2,10},{3,11},{4,12},{5,13},{6,14},{7,15},{8,0},{9,1},... | collective-permute-start | bytes 196616 | tf_op jit(solution)/shard_map/ppermute | solution.py:43
  136.9 5.9 %collective-permute-start.29 = (bf16[256,128]{1,0:T(8,128)(2,1)S(1)}, bf16[256,128]{1,0:T(8,128)(2,1)S(1)}, u32[]{:S(2)}, u32[]{:S(2)}) collective-permute-start(bf16[256,128]{1,0:T(8,128)(2,1)S(1)} %get-tuple-element.78), channel_id=1, source_target_pairs={{0,72},{1,73},{2,74},{3,75},{4,76},{5,77},{6,78},{7,79},{8,64},{9,... | collective-permute-start | bytes 196616 | tf_op jit(solution)/shard_map/ppermute | solution.py:43
  142.9 1.6 collective-permute-start.32
  (12 other events, 53.2 us)

commit v5 on v4

--- a/solution.py
+++ b/solution.py
@@ -291,7 +291,9 @@
     ahead = send(tile, functools.partial(z_move, 1))
     behind = send(tile, functools.partial(z_move, 3))
     start, ahead, behind = lax.optimization_barrier((start, ahead, behind))
-    across = send(jnp.where(core == 0, ahead, behind), relay_move)
+    far = jnp.where(core == 0, ahead, behind)
+    far, start = lax.optimization_barrier((far, start))
+    across = send(far, relay_move)
     state = jnp.concatenate([piece[:ITEMS] for piece in start])
     tables = jnp.stack([piece[ITEMS : ITEMS + PACK : 16] for piece in start]).astype(jnp.int32)
     tables = tables.transpose(1, 0, 2).reshape(TILES, LANES)
@@ -301,12 +303,6 @@
     same_core = [tile, ahead, across, behind]
     tiles = same_core + [own_swapped] + [send(piece, core_move) for piece in same_core[1:]]
 
-    chip_feats = by_tile(message[:ITEMS], other[:ITEMS], core).reshape(PIECE, DIM)
-    pre_act = jnp.dot(chip_feats, w_first, preferred_element_type=f32)
-    hidden = jax.nn.silu(pre_act).astype(bf16)
-    slope = silu_slope(pre_act)
-    feats_rows = lax.dynamic_index_in_dim(chip_feats.T.reshape(8, 2, 16, PIECE), core, 1, False).reshape(128, PIECE)
-    hidden_rows = lax.dynamic_index_in_dim(hidden.T.reshape(8, 2, 64, PIECE), core, 1, False).reshape(512, PIECE)
     restart = jnp.where(core == 0, ALPHA, 0.0).astype(f32)
     constant = restart * state.astype(f32)
     collected = state.astype(f32)
@@ -316,13 +312,24 @@
         else:
             parts = [state] + [send(state, functools.partial(gather_ring, hop)) for hop in (1, 2, 3)]
         outs = block_product(meta, masks, tiles, parts)
+        if step == 0:
+            outs, mlp_own, mlp_other = lax.optimization_barrier((outs, message[:ITEMS], other[:ITEMS]))
+            chip_feats = by_tile(mlp_own, mlp_other, core).reshape(PIECE, DIM)
+            pre_act = jnp.dot(chip_feats, w_first, preferred_element_type=f32)
+            hidden = jax.nn.silu(pre_act).astype(bf16)
+            slope = silu_slope(pre_act)
+        if step == 1:
+            outs, hidden, chip_feats = lax.optimization_barrier((outs, hidden, chip_feats))
+            feats_rows = lax.dynamic_index_in_dim(chip_feats.T.reshape(8, 2, 16, PIECE), core, 1, False)
+            hidden_rows = lax.dynamic_index_in_dim(hidden.T.reshape(8, 2, 64, PIECE), core, 1, False)
+            feats_rows, hidden_rows = feats_rows.reshape(128, PIECE), hidden_rows.reshape(512, PIECE)
         got = [outs[0]] + [send(outs[hop], functools.partial(scatter_ring, hop)) for hop in (1, 2, 3)]
         summed = sum(piece.astype(f32) for piece in got)
         state = ((1.0 - ALPHA) * summed + constant).astype(bf16)
         if step == 0:
-            state, slope, feats_rows, hidden_rows = lax.optimization_barrier(
-                (state, slope, feats_rows, hidden_rows)
-            )
+            state, slope, hidden, chip_feats = lax.optimization_barrier((state, slope, hidden, chip_feats))
+        if step == 1:
+            state, feats_rows, hidden_rows = lax.optimization_barrier((state, feats_rows, hidden_rows))
         if step < STEPS - 1:
             collected = collected + state.astype(f32)
     last = jnp.where(core == 0, state, (ALPHA * collected + state.astype(f32)).astype(bf16))

time: 178 us -> 174 us (0.978)
  blocking collectives: 29.4 us -> 26.4 us
  other arithmetic: 15.6 us -> 13.4 us
  Pallas kernels: 22.2 us -> 24.3 us
    all_to_all x1, blocking collectives: 18.5 us -> 15.9 us  [body(): landed = lax.all_to_all(spread, ('zl', 'zh', 'x'), 0, 0)]
    convert_element_type x1 -> x0, local copies, waits for them, and re-layouts: 2.28 us -> none  [body(): hidden = jax.nn.silu(pre_act).astype(bf16)]
    transpose x0 -> x1, local copies, waits for them, and re-layouts: none -> 2.28 us  [body(): hidden.T.reshape(8, 2, 64, PIECE)]
    pallas_call x3, Pallas kernels: 18.1 us -> 20.2 us  [block_product(): pl.pallas_call(product_kernel, out_shape=(piece,) * 4, in_specs=[pl.Block...]
    select_n x1 -> x0, local copies, waits for them, and re-layouts: 1.85 us -> none  [by_tile(): jnp.where(core == 0, jnp.stack([own, other]), jnp.stack([other, own]))]
    optimization_barrier x0 -> x1, local copies, waits for them, and re-layouts: none -> 1.8 us  [body(): lax.optimization_barrier((outs, hidden, chip_feats))]
  transfers between devices with their start and end apart: 33 -> 33, of which waited for: 18 -> 20; matrix products, arithmetic and copies ran while one was open for 14% -> 12% of each run, Pallas kernels for 1% -> 1%
where the time goes in v5:
time: 174 us; the launch traced here: 173 us
  waiting for transfers between devices  49.3 us (28%)
  starting transfers between devices  40.5 us (23%)
  blocking collectives  26.4 us (15%)
  Pallas kernels  24.3 us (14%)
  local copies, waits for them, and re-layouts  14.8 us (9%)
  other arithmetic  13.4 us (8%)
  matrix products  2.69 us (2%)
    ppermute x33, waiting for transfers between devices, send(): return lax.ppermute(value, AXES, permutation(move))  49.3 us
    ppermute x33, starting transfers between devices, send(): return lax.ppermute(value, AXES, permutation(move))  40.5 us
    pallas_call x3, Pallas kernels, block_product(): pl.pallas_call(product_kernel, out_shape=(piece,) * 4, in_specs=[pl.Block...  20.2 us
    all_to_all x1, blocking collectives, body(): landed = lax.all_to_all(spread, ('zl', 'zh', 'x'), 0, 0)  15.9 us
    all_to_all x1, blocking collectives, body(): lax.all_to_all(jnp.broadcast_to(mine[None], (8, 128, 128)), LOOP, 0, 0)  10.5 us
  transfers between devices with their start and end apart: 33, of which 20 were waited for; matrix products, arithmetic and copies ran while one was open for 12% of the time, Pallas kernels for 1%

profile of v5, /device:TPU:0, one launch (start us, length us, event | category | flops | bytes accessed | tf_op | source)
XLA Modules:
  0.0 172.6 jit_solution(1409304661954150896)
XLA Ops:
  0.6 1.3 fusion.65
  3.0 4.2 %collective-permute-start.6 = (bf16[2560,128]{1,0:T(8,128)(2,1)S(1)}, bf16[2560,128]{1,0:T(8,128)(2,1)S(1)}, u32[]{:S(2)}, u32[]{:S(2)}) collective-permute-start(bf16[2560,128]{1,0:T(8,128)(2,1)S(1)} %bitcast.57), channel_id=1, source_target_pairs={{0,72},{1,73},{2,74},{3,75},{4,76},{5,77},{6,78},{7,79},{8,64},{9,... | collective-permute-start | bytes 1966088 | tf_op jit(solution)/shard_map/ppermute | solution.py:43
  10.1 1.0 copy-done.3
  11.1 2.0 %start_pieces.1 = bf16[4,288,128]{2,1,0:T(8,128)(2,1)S(1)} custom-call(s32[2]{0:T(128)S(1)} %pad_add_fusion.1.place, bf16[528,256]{1,0:T(8,128)(2,1)S(1)} %pad_maximum_fusion.1.own, bf16[528,256]{1,0:T(8,128)(2,1)} %collective-permute-done.other, bf16[256,1024]{1,0:T(8,128)(2,1)S(1)} %copy-done.3, bf16[1024,256]{1,0:T(8,128)(2,1)S(1)} %copy-done.1), custom_call_target="tpu_custom_call" | custom-call | tf_op jit(solution)/shard_map/start_pieces/pallas_call | solution.py:89
  13.2 3.3 %collective-permute-start.4 = (bf16[288,128]{1,0:T(8,128)(2,1)S(1)}, bf16[288,128]{1,0:T(8,128)(2,1)S(1)}, u32[]{:S(2)}, u32[]{:S(2)}) collective-permute-start(bf16[288,128]{1,0:T(8,128)(2,1)S(1)} %get-tuple-element.113), channel_id=1, source_target_pairs={{0,72},{1,73},{2,74},{3,75},{4,76},{5,77},{6,78},{7,79},{8,64},{9,... | collective-permute-start | bytes 221192 | tf_op jit(solution)/shard_map/ppermute | solution.py:43
  16.5 0.9 collective-permute-start.2
  18.0 5.5 %collective-permute-done.6.refs_3_ = bf16[2560,128]{1,0:T(8,128)(2,1)S(1)} collective-permute-done((bf16[2560,128]{1,0:T(8,128)(2,1)S(1)}, bf16[2560,128]{1,0:T(8,128)(2,1)S(1)}, u32[]{:S(2)}, u32[]{:S(2)}) %collective-permute-start.6) | collective-permute-done | bytes 655392 | tf_op jit(solution)/shard_map/ppermute | solution.py:43
  23.5 3.4 %collective-permute-done.5.refs_1_ = bf16[2560,128]{1,0:T(8,128)(2,1)S(1)} collective-permute-done((bf16[2560,128]{1,0:T(8,128)(2,1)S(1)}, bf16[2560,128]{1,0:T(8,128)(2,1)S(1)}, u32[]{:S(2)}, u32[]{:S(2)}) %collective-permute-start.5) | collective-permute-done | bytes 655392 | tf_op jit(solution)/shard_map/ppermute | solution.py:43
  27.7 0.9 broadcast_select_fusion
  29.1 2.8 %collective-permute-start.9 = (bf16[1024,128]{1,0:T(8,128)(2,1)S(1)}, bf16[1024,128]{1,0:T(8,128)(2,1)}, u32[]{:S(2)}, u32[]{:S(2)}) collective-permute-start(bf16[1024,128]{1,0:T(8,128)(2,1)S(1)} %pad_maximum_fusion.2.refs_8_), channel_id=1, source_target_pairs={{0,6},{1,49},{2,0},{3,51},{4,2},{5,53},{6,4},{7,55},{8,14},{9,57},... | collective-permute-start | bytes 786440 | tf_op jit(solution)/shard_map/ppermute | solution.py:43
  32.8 1.0 collective-permute-start.7
  36.4 1.4 fusion.23
  40.2 1.9 %compare_select_fusion.1 = (s32[1,704]{1,0:T(1,128)S(1)}, s32[1,704]{1,0:T(1,128)S(1)}) fusion(s32[]{:T(128)} %axis_index.52, s32[]{:T(128)} %bitcast.19, s32[]{:T(128)} %bitcast.18, s32[704]{0:T(1024)S(1)} %get-tuple-element.108, s32[704]{0:T(1024)} %get-tuple-element.126), kind=kLoop, calls=%fused_computation.47 | loop fusion | flops 6336 | bytes 11276 | tf_op jit(solution)/shard_map/jit(_where)/select_n | solution.py:256
  43.3 3.9 %collective-permute-done.10.refs_2_ = bf16[2560,128]{1,0:T(8,128)(2,1)} collective-permute-done((bf16[2560,128]{1,0:T(8,128)(2,1)}, bf16[2560,128]{1,0:T(8,128)(2,1)}, u32[]{:S(2)}, u32[]{:S(2)}) %collective-permute-start.10) | collective-permute-done | bytes 655392 | tf_op jit(solution)/shard_map/ppermute | solution.py:43
  48.2 1.5 collective-permute-done.12.refs_6_
  50.4 6.6 %block_product.3 = (bf16[1024,128]{1,0:T(8,128)(2,1)S(1)}, bf16[1024,128]{1,0:T(8,128)(2,1)S(1)}, bf16[1024,128]{1,0:T(8,128)(2,1)S(1)}, bf16[1024,128]{1,0:T(8,128)(2,1)S(1)}) custom-call(s32[4,704]{1,0:T(4,128)S(1)} %copy-done.6, bf16[2,32,128]{2,1,0:T(8,128)(2,1)S(1)} %broadcast_in_dim.66.masks, bf16[2560,128]{1,0:T(8,128)(2,1)S(1)} %bitcast.60, ...), custom_call_target="tpu_custom_call" | custom-call | tf_op jit(solution)/shard_map/block_product/pallas_call | solution.py:150
  57.0 1.6 collective-permute-start.14
  58.6 2.1 %collective-permute-start.15 = (bf16[1024,128]{1,0:T(8,128)(2,1)S(1)}, bf16[1024,128]{1,0:T(8,128)(2,1)S(1)}, u32[]{:S(2)}, u32[]{:S(2)}) collective-permute-start(bf16[1024,128]{1,0:T(8,128)(2,1)S(1)} %get-tuple-element.80), channel_id=1, source_target_pairs={{0,32},{1,5},{2,34},{3,7},{4,36},{5,1},{6,38},{7,3},{8,40},{9,13},... | collective-permute-start | bytes 786440 | tf_op jit(solution)/shard_map/ppermute | solution.py:43
  60.7 2.1 %collective-permute-start.16 = (bf16[1024,128]{1,0:T(8,128)(2,1)S(1)}, bf16[1024,128]{1,0:T(8,128)(2,1)S(1)}, u32[]{:S(2)}, u32[]{:S(2)}) collective-permute-start(bf16[1024,128]{1,0:T(8,128)(2,1)S(1)} %get-tuple-element.81), channel_id=1, source_target_pairs={{0,48},{1,7},{2,50},{3,1},{4,52},{5,3},{6,54},{7,5},{8,56},{9,15},... | collective-permute-start | bytes 786440 | tf_op jit(solution)/shard_map/ppermute | solution.py:43
  62.9 2.7 %multiply_convert_fusion = (bf16[512,1024]{1,0:T(8,128)(2,1)}, f32[512,1024]{1,0:T(8,128)}) fusion(bf16[512,256]{1,0:T(8,128)(2,1)S(1)} %bitcast.67, bf16[256,1024]{1,0:T(8,128)(2,1)S(1)} %copy-done.4), kind=kOutput, calls=%fused_computation | convolution fusion | flops 273154048 | bytes 3932160 | tf_op jit(solution)/shard_map/dot_general | solution.py:318
  65.6 2.2 %collective-permute-done.15 = bf16[1024,128]{1,0:T(8,128)(2,1)S(1)} collective-permute-done((bf16[1024,128]{1,0:T(8,128)(2,1)S(1)}, bf16[1024,128]{1,0:T(8,128)(2,1)S(1)}, u32[]{:S(2)}, u32[]{:S(2)}) %collective-permute-start.15) | collective-permute-done | bytes 262176 | tf_op jit(solution)/shard_map/ppermute | solution.py:43
  68.5 3.6 %collective-permute-start.19 = (bf16[1024,128]{1,0:T(8,128)(2,1)S(1)}, bf16[1024,128]{1,0:T(8,128)(2,1)S(1)}, u32[]{:S(2)}, u32[]{:S(2)}) collective-permute-start(bf16[1024,128]{1,0:T(8,128)(2,1)S(1)} %fusion.3.refs_8_), channel_id=1, source_target_pairs={{0,6},{1,49},{2,0},{3,51},{4,2},{5,53},{6,4},{7,55},{8,14},{9,57},... | collective-permute-start | bytes 786440 | tf_op jit(solution)/shard_map/ppermute | solution.py:43
  73.1 5.7 %collective-permute-done.19.refs_11_ = bf16[1024,128]{1,0:T(8,128)(2,1)S(1)} collective-permute-done((bf16[1024,128]{1,0:T(8,128)(2,1)S(1)}, bf16[1024,128]{1,0:T(8,128)(2,1)S(1)}, u32[]{:S(2)}, u32[]{:S(2)}) %collective-permute-start.19) | collective-permute-done | bytes 262176 | tf_op jit(solution)/shard_map/ppermute | solution.py:43
  78.8 1.3 collective-permute-done.18.refs_10_
  80.1 2.7 %collective-permute-done.17.refs_9_ = bf16[1024,128]{1,0:T(8,128)(2,1)S(1)} collective-permute-done((bf16[1024,128]{1,0:T(8,128)(2,1)S(1)}, bf16[1024,128]{1,0:T(8,128)(2,1)S(1)}, u32[]{:S(2)}, u32[]{:S(2)}) %collective-permute-start.17) | collective-permute-done | bytes 262176 | tf_op jit(solution)/shard_map/ppermute | solution.py:43
  82.8 7.2 %block_product.4 = (bf16[1024,128]{1,0:T(8,128)(2,1)S(1)}, bf16[1024,128]{1,0:T(8,128)(2,1)}, bf16[1024,128]{1,0:T(8,128)(2,1)}, bf16[1024,128]{1,0:T(8,128)(2,1)}) custom-call(s32[4,704]{1,0:T(4,128)S(1)} %copy-done.6, bf16[2,32,128]{2,1,0:T(8,128)(2,1)S(1)} %broadcast_in_dim.66.masks, bf16[2560,128]{1,0:T(8,128)(2,1)S(1)} %bitcast.61, ...), custom_call_target="tpu_custom_call" | custom-call | tf_op jit(solution)/shard_map/block_product/pallas_call | solution.py:150
  90.8 1.3 collective-permute-start.20
  92.0 1.6 collective-permute-start.21
  93.6 1.9 %collective-permute-start.22 = (bf16[1024,128]{1,0:T(8,128)(2,1)}, bf16[1024,128]{1,0:T(8,128)(2,1)}, u32[]{:S(2)}, u32[]{:S(2)}) collective-permute-start(bf16[1024,128]{1,0:T(8,128)(2,1)} %get-tuple-element.94), channel_id=1, source_target_pairs={{0,48},{1,7},{2,50},{3,1},{4,52},{5,3},{6,54},{7,5},{8,56},{9,15},... | collective-permute-start | bytes 786440 | tf_op jit(solution)/shard_map/ppermute | solution.py:43
  95.5 1.8 %copy.30 = bf16[512,256]{0,1:T(8,128)(2,1)} copy(bf16[512,256]{1,0:T(8,128)(2,1)} %bitcast.68) | data formatting | bytes 524288 | tf_op jit(solution)/shard_map/optimization_barrier | solution.py:322
  97.3 2.3 %copy.31 = bf16[1024,512]{1,0:T(8,128)(2,1)} copy(bf16[1024,512]{0,1:T(8,128)(2,1)} %bitcast.70) | data formatting | bytes 2097152 | tf_op jit(solution)/shard_map/transpose | solution.py:324
  100.5 1.1 constant_dynamic-slice_fusion
  102.4 1.4 fusion.4.refs_8_
  105.3 1.0 collective-permute-start.23
  106.3 4.0 %collective-permute-done.25.refs_11_ = bf16[1024,128]{1,0:T(8,128)(2,1)S(1)} collective-permute-done((bf16[1024,128]{1,0:T(8,128)(2,1)S(1)}, bf16[1024,128]{1,0:T(8,128)(2,1)S(1)}, u32[]{:S(2)}, u32[]{:S(2)}) %collective-permute-start.25) | collective-permute-done | bytes 262176 | tf_op jit(solution)/shard_map/ppermute | solution.py:43
  110.3 2.3 %collective-permute-done.24.refs_10_ = bf16[1024,128]{1,0:T(8,128)(2,1)S(1)} collective-permute-done((bf16[1024,128]{1,0:T(8,128)(2,1)S(1)}, bf16[1024,128]{1,0:T(8,128)(2,1)S(1)}, u32[]{:S(2)}, u32[]{:S(2)}) %collective-permute-start.24) | collective-permute-done | bytes 262176 | tf_op jit(solution)/shard_map/ppermute | solution.py:43
  112.6 2.7 %collective-permute-done.23.refs_9_ = bf16[1024,128]{1,0:T(8,128)(2,1)S(1)} collective-permute-done((bf16[1024,128]{1,0:T(8,128)(2,1)S(1)}, bf16[1024,128]{1,0:T(8,128)(2,1)S(1)}, u32[]{:S(2)}, u32[]{:S(2)}) %collective-permute-start.23) | collective-permute-done | bytes 262176 | tf_op jit(solution)/shard_map/ppermute | solution.py:43
  115.3 6.4 %block_product.5 = (bf16[1024,128]{1,0:T(8,128)(2,1)S(1)}, bf16[1024,128]{1,0:T(8,128)(2,1)S(1)}, bf16[1024,128]{1,0:T(8,128)(2,1)S(1)}, bf16[1024,128]{1,0:T(8,128)(2,1)S(1)}) custom-call(s32[4,704]{1,0:T(4,128)S(1)} %copy-done.7, bf16[2,32,128]{2,1,0:T(8,128)(2,1)S(1)} %broadcast_in_dim.66.masks, bf16[2560,128]{1,0:T(8,128)(2,1)S(1)} %bitcast.62, ...), custom_call_target="tpu_custom_call" | custom-call | tf_op jit(solution)/shard_map/block_product/pallas_call | solution.py:150
  121.8 2.6 %collective-permute-start.26 = (bf16[1024,128]{1,0:T(8,128)(2,1)S(1)}, bf16[1024,128]{1,0:T(8,128)(2,1)S(1)}, u32[]{:S(2)}, u32[]{:S(2)}) collective-permute-start(bf16[1024,128]{1,0:T(8,128)(2,1)S(1)} %get-tuple-element.99), channel_id=1, source_target_pairs={{0,16},{1,3},{2,18},{3,5},{4,20},{5,7},{6,22},{7,1},{8,24},{9,11},... | collective-permute-start | bytes 786440 | tf_op jit(solution)/shard_map/ppermute | solution.py:43
  125.1 2.0 %collective-permute-start.28 = (bf16[1024,128]{1,0:T(8,128)(2,1)S(1)}, bf16[1024,128]{1,0:T(8,128)(2,1)S(1)}, u32[]{:S(2)}, u32[]{:S(2)}) collective-permute-start(bf16[1024,128]{1,0:T(8,128)(2,1)S(1)} %get-tuple-element.101), channel_id=1, source_target_pairs={{0,48},{1,7},{2,50},{3,1},{4,52},{5,3},{6,54},{7,5},{8,56},{9,15},... | collective-permute-start | bytes 786440 | tf_op jit(solution)/shard_map/ppermute | solution.py:43
  127.1 5.3 %collective-permute-done.26 = bf16[1024,128]{1,0:T(8,128)(2,1)S(1)} collective-permute-done((bf16[1024,128]{1,0:T(8,128)(2,1)S(1)}, bf16[1024,128]{1,0:T(8,128)(2,1)S(1)}, u32[]{:S(2)}, u32[]{:S(2)}) %collective-permute-start.26) | collective-permute-done | bytes 262176 | tf_op jit(solution)/shard_map/ppermute | solution.py:43
  133.8 1.2 collective-permute-start.30
  135.0 2.0 %collective-permute-start.29 = (bf16[256,128]{1,0:T(8,128)(2,1)S(1)}, bf16[256,128]{1,0:T(8,128)(2,1)S(1)}, u32[]{:S(2)}, u32[]{:S(2)}) collective-permute-start(bf16[256,128]{1,0:T(8,128)(2,1)S(1)} %get-tuple-element.120), channel_id=1, source_target_pairs={{0,72},{1,73},{2,74},{3,75},{4,76},{5,77},{6,78},{7,79},{8,64},{9,... | collective-permute-start | bytes 196616 | tf_op jit(solution)/shard_map/ppermute | solution.py:43
  137.0 2.9 %collective-permute-done.31 = bf16[256,128]{1,0:T(8,128)(2,1)S(1)} collective-permute-done((bf16[256,128]{1,0:T(8,128)(2,1)S(1)}, bf16[256,128]{1,0:T(8,128)(2,1)S(1)}, u32[]{:S(2)}, u32[]{:S(2)}) %collective-permute-start.31) | collective-permute-done | bytes 65568 | tf_op jit(solution)/shard_map/ppermute | solution.py:43
  140.9 1.5 collective-permute-done.32.other
  142.5 2.1 %finish.1 = (bf16[2048,128]{1,0:T(8,128)(2,1)S(1)}, bf16[256,256]{1,0:T(8,128)(2,1)}) custom-call(s32[2]{0:T(128)S(1)} %copy-done.9, bf16[4,256,128]{2,1,0:T(8,128)(2,1)S(1)} %pad_maximum_fusion.3.own, bf16[4,256,128]{2,1,0:T(8,128)(2,1)S(1)} %collective-permute-done.32.other, bf16[128,512]{1,0:T(8,128)(2,1)S(1)} %bitcast.64, bf16[512,512]{1,0:T(8,128)(2,1)S(1)} %bitcast.63, ...), custom_call_target="tpu_custom_call" | custom-call | tf_op jit(solution)/shard_map/finish/pallas_call | solution.py:209
  144.6 15.9 %all_to_all.10 = bf16[16,128,128]{2,1,0:T(8,128)(2,1)S(1)} all-to-all(bf16[16,128,128]{2,1,0:T(8,128)(2,1)S(1)} %bitcast.65), channel_id=1, replica_groups=mesh['zl'=2,'y'=4,'zh'=2,'x'=4,'c'=2] {'zl','zh','x'}, dimensions={0} | all-to-all | bytes 1048576 | tf_op jit(solution)/shard_map/all_to_all | solution.py:342
  160.6 10.5 %all_to_all.11 = bf16[8,128,128]{2,1,0:T(8,128)(2,1)S(1)} all-to-all(bf16[8,128,128]{2,1,0:T(8,128)(2,1)S(1)} %broadcast_in_dim.68), channel_id=1, replica_groups=mesh['zl'=2,'y'=4,'zh'=2,'x'=4,'c'=2] {'zl','y'}, dimensions={0} | all-to-all | bytes 524288 | tf_op jit(solution)/shard_map/all_to_all | solution.py:344
  (139 shorter events, 24.6 us)
Async XLA Ops:
  1.9 8.1 %copy-start.1 = (bf16[1024,256]{1,0:T(8,128)(2,1)S(1)}, bf16[1024,256]{1,0:T(8,128)(2,1)}, u32[]{:S(2)}) copy-start(bf16[1024,256]{1,0:T(8,128)(2,1)} %w_second.3) | copy-start | bytes 1572868
  3.0 20.6 %collective-permute-start.6 = (bf16[2560,128]{1,0:T(8,128)(2,1)S(1)}, bf16[2560,128]{1,0:T(8,128)(2,1)S(1)}, u32[]{:S(2)}, u32[]{:S(2)}) collective-permute-start(bf16[2560,128]{1,0:T(8,128)(2,1)S(1)} %bitcast.57), channel_id=1, source_target_pairs={{0,72},{1,73},{2,74},{3,75},{4,76},{5,77},{6,78},{7,79},{8,64},{9,... | collective-permute-start | bytes 1966088 | tf_op jit(solution)/shard_map/ppermute | solution.py:43
  7.2 19.8 %collective-permute-start.5 = (bf16[2560,128]{1,0:T(8,128)(2,1)S(1)}, bf16[2560,128]{1,0:T(8,128)(2,1)S(1)}, u32[]{:S(2)}, u32[]{:S(2)}) collective-permute-start(bf16[2560,128]{1,0:T(8,128)(2,1)S(1)} %bitcast.58), channel_id=1, source_target_pairs={{0,64},{1,65},{2,66},{3,67},{4,68},{5,69},{6,70},{7,71},{8,72},{9,... | collective-permute-start | bytes 1966088 | tf_op jit(solution)/shard_map/ppermute | solution.py:43
  7.2 6.0 %collective-permute-start.1 = (bf16[2560,128]{1,0:T(8,128)(2,1)S(1)}, bf16[2560,128]{1,0:T(8,128)(2,1)S(1)}, u32[]{:S(2)}, u32[]{:S(2)}) collective-permute-start(bf16[2560,128]{1,0:T(8,128)(2,1)S(1)} %bitcast.59), channel_id=1, source_target_pairs={{0,1},{1,0},{2,3},{3,2},{4,5},{5,4},{6,7},{7,6},{8,9},{9,8},{10,11... | collective-permute-start | bytes 1966088 | tf_op jit(solution)/shard_map/ppermute | solution.py:43
  8.2 1.9 %collective-permute-start = (bf16[528,256]{1,0:T(8,128)(2,1)S(1)}, bf16[528,256]{1,0:T(8,128)(2,1)}, u32[]{:S(2)}, u32[]{:S(2)}) collective-permute-start(bf16[528,256]{1,0:T(8,128)(2,1)S(1)} %pad_maximum_fusion.1.own), channel_id=1, source_target_pairs={{0,1},{1,0},{2,3},{3,2},{4,5},{5,4},{6,7},{7,6},{8,9},{9,8},{10,11... | collective-permute-start | bytes 811016 | tf_op jit(solution)/shard_map/ppermute | solution.py:43
  8.9 19.8 %copy-start.8 = (s32[2]{0:T(128)}, s32[2]{0:T(128)S(1)}, u32[]{:S(2)}) copy-start(s32[2]{0:T(128)S(1)} %pad_add_fusion.1.place) | copy-start | bytes 28
  13.2 13.7 %collective-permute-start.4 = (bf16[288,128]{1,0:T(8,128)(2,1)S(1)}, bf16[288,128]{1,0:T(8,128)(2,1)S(1)}, u32[]{:S(2)}, u32[]{:S(2)}) collective-permute-start(bf16[288,128]{1,0:T(8,128)(2,1)S(1)} %get-tuple-element.113), channel_id=1, source_target_pairs={{0,72},{1,73},{2,74},{3,75},{4,76},{5,77},{6,78},{7,79},{8,64},{9,... | collective-permute-start | bytes 221192 | tf_op jit(solution)/shard_map/ppermute | solution.py:43
  16.5 10.4 %collective-permute-start.3 = (bf16[288,128]{1,0:T(8,128)(2,1)S(1)}, bf16[288,128]{1,0:T(8,128)(2,1)S(1)}, u32[]{:S(2)}, u32[]{:S(2)}) collective-permute-start(bf16[288,128]{1,0:T(8,128)(2,1)S(1)} %get-tuple-element.114), channel_id=1, source_target_pairs={{0,8},{1,9},{2,10},{3,11},{4,12},{5,13},{6,14},{7,15},{8,0},{9,1},... | collective-permute-start | bytes 221192 | tf_op jit(solution)/shard_map/ppermute | solution.py:43
  16.5 11.2 %collective-permute-start.2 = (bf16[288,128]{1,0:T(8,128)(2,1)S(1)}, bf16[288,128]{1,0:T(8,128)(2,1)S(1)}, u32[]{:S(2)}, u32[]{:S(2)}) collective-permute-start(bf16[288,128]{1,0:T(8,128)(2,1)S(1)} %get-tuple-element.115), channel_id=1, source_target_pairs={{0,64},{1,65},{2,66},{3,67},{4,68},{5,69},{6,70},{7,71},{8,72},{9,... | collective-permute-start | bytes 221192 | tf_op jit(solution)/shard_map/ppermute | solution.py:43
  29.1 13.7 %collective-permute-start.9 = (bf16[1024,128]{1,0:T(8,128)(2,1)S(1)}, bf16[1024,128]{1,0:T(8,128)(2,1)}, u32[]{:S(2)}, u32[]{:S(2)}) collective-permute-start(bf16[1024,128]{1,0:T(8,128)(2,1)S(1)} %pad_maximum_fusion.2.refs_8_), channel_id=1, source_target_pairs={{0,6},{1,49},{2,0},{3,51},{4,2},{5,53},{6,4},{7,55},{8,14},{9,57},... | collective-permute-start | bytes 786440 | tf_op jit(solution)/shard_map/ppermute | solution.py:43
  32.0 11.3 %collective-permute-start.8 = (bf16[1024,128]{1,0:T(8,128)(2,1)S(1)}, bf16[1024,128]{1,0:T(8,128)(2,1)}, u32[]{:S(2)}, u32[]{:S(2)}) collective-permute-start(bf16[1024,128]{1,0:T(8,128)(2,1)S(1)} %pad_maximum_fusion.2.refs_8_), channel_id=1, source_target_pairs={{0,4},{1,33},{2,6},{3,35},{4,0},{5,37},{6,2},{7,39},{8,12},{9,41},... | collective-permute-start | bytes 786440 | tf_op jit(solution)/shard_map/ppermute | solution.py:43
  32.8 10.5 %collective-permute-start.7 = (bf16[1024,128]{1,0:T(8,128)(2,1)S(1)}, bf16[1024,128]{1,0:T(8,128)(2,1)}, u32[]{:S(2)}, u32[]{:S(2)}) collective-permute-start(bf16[1024,128]{1,0:T(8,128)(2,1)S(1)} %pad_maximum_fusion.2.refs_8_), channel_id=1, source_target_pairs={{0,2},{1,17},{2,4},{3,19},{4,6},{5,21},{6,0},{7,23},{8,10},{9,25},... | collective-permute-start | bytes 786440 | tf_op jit(solution)/shard_map/ppermute | solution.py:43
  33.7 14.5 %collective-permute-start.11 = (bf16[2560,128]{1,0:T(8,128)(2,1)S(1)}, bf16[2560,128]{1,0:T(8,128)(2,1)S(1)}, u32[]{:S(2)}, u32[]{:S(2)}) collective-permute-start(bf16[2560,128]{1,0:T(8,128)(2,1)S(1)} %collective-permute-done.5.refs_1_), channel_id=1, source_target_pairs={{0,1},{1,0},{2,3},{3,2},{4,5},{5,4},{6,7},{7,6},{8,9},{9,8},{10,11... | collective-permute-start | bytes 1966088 | tf_op jit(solution)/shard_map/ppermute | solution.py:43
  35.1 12.1 %collective-permute-start.10 = (bf16[2560,128]{1,0:T(8,128)(2,1)}, bf16[2560,128]{1,0:T(8,128)(2,1)}, u32[]{:S(2)}, u32[]{:S(2)}) collective-permute-start(bf16[2560,128]{1,0:T(8,128)(2,1)} %broadcast_select_fusion), channel_id=1, source_target_pairs={{0,64},{1,73},{2,66},{3,75},{4,68},{5,77},{6,70},{7,79},{8,72},{9,... | collective-permute-start | bytes 1966088 | tf_op jit(solution)/shard_map/ppermute | solution.py:43
  42.8 5.4 %collective-permute-start.13 = (bf16[2560,128]{1,0:T(8,128)(2,1)S(1)}, bf16[2560,128]{1,0:T(8,128)(2,1)}, u32[]{:S(2)}, u32[]{:S(2)}) collective-permute-start(bf16[2560,128]{1,0:T(8,128)(2,1)S(1)} %collective-permute-done.6.refs_3_), channel_id=1, source_target_pairs={{0,1},{1,0},{2,3},{3,2},{4,5},{5,4},{6,7},{7,6},{8,9},{9,8},{10,11... | collective-permute-start | bytes 1966088 | tf_op jit(solution)/shard_map/ppermute | solution.py:43
  47.2 2.4 %collective-permute-start.12 = (bf16[2560,128]{1,0:T(8,128)(2,1)}, bf16[2560,128]{1,0:T(8,128)(2,1)}, u32[]{:S(2)}, u32[]{:S(2)}) collective-permute-start(bf16[2560,128]{1,0:T(8,128)(2,1)} %collective-permute-done.10.refs_2_), channel_id=1, source_target_pairs={{0,1},{1,0},{2,3},{3,2},{4,5},{5,4},{6,7},{7,6},{8,9},{9,8},{10,11... | collective-permute-start | bytes 1966088 | tf_op jit(solution)/shard_map/ppermute | solution.py:43
  50.4 12.5 %copy-start.24 = (bf16[1,256,256]{2,1,0:T(8,128)(2,1)S(1)}, bf16[1,256,256]{2,1,0:T(8,128)(2,1)}, u32[]{:S(2)}) copy-start(bf16[1,256,256]{2,1,0:T(8,128)(2,1)} %param.7) | copy-start | bytes 393220
  50.4 12.5 %copy-start.4 = (bf16[256,1024]{1,0:T(8,128)(2,1)S(1)}, bf16[256,1024]{1,0:T(8,128)(2,1)}, u32[]{:S(2)}) copy-start(bf16[256,1024]{1,0:T(8,128)(2,1)} %w_first.1) | copy-start | bytes 1572868
  57.0 8.7 %collective-permute-start.14 = (bf16[1024,128]{1,0:T(8,128)(2,1)S(1)}, bf16[1024,128]{1,0:T(8,128)(2,1)S(1)}, u32[]{:S(2)}, u32[]{:S(2)}) collective-permute-start(bf16[1024,128]{1,0:T(8,128)(2,1)S(1)} %get-tuple-element.79), channel_id=1, source_target_pairs={{0,16},{1,3},{2,18},{3,5},{4,20},{5,7},{6,22},{7,1},{8,24},{9,11},... | collective-permute-start | bytes 786440 | tf_op jit(solution)/shard_map/ppermute | solution.py:43
  58.6 9.3 %collective-permute-start.15 = (bf16[1024,128]{1,0:T(8,128)(2,1)S(1)}, bf16[1024,128]{1,0:T(8,128)(2,1)S(1)}, u32[]{:S(2)}, u32[]{:S(2)}) collective-permute-start(bf16[1024,128]{1,0:T(8,128)(2,1)S(1)} %get-tuple-element.80), channel_id=1, source_target_pairs={{0,32},{1,5},{2,34},{3,7},{4,36},{5,1},{6,38},{7,3},{8,40},{9,13},... | collective-permute-start | bytes 786440 | tf_op jit(solution)/shard_map/ppermute | solution.py:43
  60.7 7.6 %collective-permute-start.16 = (bf16[1024,128]{1,0:T(8,128)(2,1)S(1)}, bf16[1024,128]{1,0:T(8,128)(2,1)S(1)}, u32[]{:S(2)}, u32[]{:S(2)}) collective-permute-start(bf16[1024,128]{1,0:T(8,128)(2,1)S(1)} %get-tuple-element.81), channel_id=1, source_target_pairs={{0,48},{1,7},{2,50},{3,1},{4,52},{5,3},{6,54},{7,5},{8,56},{9,15},... | collective-permute-start | bytes 786440 | tf_op jit(solution)/shard_map/ppermute | solution.py:43
  62.9 5.4 %copy-start.11 = (bf16[256,128]{1,0:T(8,128)(2,1)S(1)}, bf16[256,128]{1,0:T(8,128)(2,1)}, u32[]{:S(2)}) copy-start(bf16[256,128]{1,0:T(8,128)(2,1)} %copy-done.10) | copy-start | bytes 196612
  62.9 5.4 %copy-start.14 = (bf16[256,128]{1,0:T(8,128)(2,1)S(1)}, bf16[256,128]{1,0:T(8,128)(2,1)}, u32[]{:S(2)}) copy-start(bf16[256,128]{1,0:T(8,128)(2,1)} %copy-done.13) | copy-start | bytes 196612
  62.9 5.4 %copy-start.17 = (bf16[256,128]{1,0:T(8,128)(2,1)S(1)}, bf16[256,128]{1,0:T(8,128)(2,1)}, u32[]{:S(2)}) copy-start(bf16[256,128]{1,0:T(8,128)(2,1)} %copy-done.16) | copy-start | bytes 196612
  68.5 10.3 %collective-permute-start.19 = (bf16[1024,128]{1,0:T(8,128)(2,1)S(1)}, bf16[1024,128]{1,0:T(8,128)(2,1)S(1)}, u32[]{:S(2)}, u32[]{:S(2)}) collective-permute-start(bf16[1024,128]{1,0:T(8,128)(2,1)S(1)} %fusion.3.refs_8_), channel_id=1, source_target_pairs={{0,6},{1,49},{2,0},{3,51},{4,2},{5,53},{6,4},{7,55},{8,14},{9,57},... | collective-permute-start | bytes 786440 | tf_op jit(solution)/shard_map/ppermute | solution.py:43
  72.1 8.0 %collective-permute-start.18 = (bf16[1024,128]{1,0:T(8,128)(2,1)S(1)}, bf16[1024,128]{1,0:T(8,128)(2,1)S(1)}, u32[]{:S(2)}, u32[]{:S(2)}) collective-permute-start(bf16[1024,128]{1,0:T(8,128)(2,1)S(1)} %fusion.3.refs_8_), channel_id=1, source_target_pairs={{0,4},{1,33},{2,6},{3,35},{4,0},{5,37},{6,2},{7,39},{8,12},{9,41},... | collective-permute-start | bytes 786440 | tf_op jit(solution)/shard_map/ppermute | solution.py:43
  72.4 10.3 %collective-permute-start.17 = (bf16[1024,128]{1,0:T(8,128)(2,1)S(1)}, bf16[1024,128]{1,0:T(8,128)(2,1)S(1)}, u32[]{:S(2)}, u32[]{:S(2)}) collective-permute-start(bf16[1024,128]{1,0:T(8,128)(2,1)S(1)} %fusion.3.refs_8_), channel_id=1, source_target_pairs={{0,2},{1,17},{2,4},{3,19},{4,6},{5,21},{6,0},{7,23},{8,10},{9,25},... | collective-permute-start | bytes 786440 | tf_op jit(solution)/shard_map/ppermute | solution.py:43
  90.8 10.8 %collective-permute-start.20 = (bf16[1024,128]{1,0:T(8,128)(2,1)}, bf16[1024,128]{1,0:T(8,128)(2,1)}, u32[]{:S(2)}, u32[]{:S(2)}) collective-permute-start(bf16[1024,128]{1,0:T(8,128)(2,1)} %get-tuple-element.92), channel_id=1, source_target_pairs={{0,16},{1,3},{2,18},{3,5},{4,20},{5,7},{6,22},{7,1},{8,24},{9,11},... | collective-permute-start | bytes 786440 | tf_op jit(solution)/shard_map/ppermute | solution.py:43
  92.0 9.6 %collective-permute-start.21 = (bf16[1024,128]{1,0:T(8,128)(2,1)}, bf16[1024,128]{1,0:T(8,128)(2,1)}, u32[]{:S(2)}, u32[]{:S(2)}) collective-permute-start(bf16[1024,128]{1,0:T(8,128)(2,1)} %get-tuple-element.93), channel_id=1, source_target_pairs={{0,32},{1,5},{2,34},{3,7},{4,36},{5,1},{6,38},{7,3},{8,40},{9,13},... | collective-permute-start | bytes 786440 | tf_op jit(solution)/shard_map/ppermute | solution.py:43
  93.6 8.8 %collective-permute-start.22 = (bf16[1024,128]{1,0:T(8,128)(2,1)}, bf16[1024,128]{1,0:T(8,128)(2,1)}, u32[]{:S(2)}, u32[]{:S(2)}) collective-permute-start(bf16[1024,128]{1,0:T(8,128)(2,1)} %get-tuple-element.94), channel_id=1, source_target_pairs={{0,48},{1,7},{2,50},{3,1},{4,52},{5,3},{6,54},{7,5},{8,56},{9,15},... | collective-permute-start | bytes 786440 | tf_op jit(solution)/shard_map/ppermute | solution.py:43
  99.6 15.7 %copy-start.7 = (s32[4,704]{1,0:T(4,128)S(1)}, s32[4,704]{1,0:T(4,128)}, u32[]{:S(2)}) copy-start(s32[4,704]{1,0:T(4,128)} %pad_add_fusion.meta) | copy-start | bytes 33796
  103.8 29.5 %copy-start.12 = (bf16[256,128]{1,0:T(8,128)(2,1)S(1)}, bf16[256,128]{1,0:T(8,128)(2,1)}, u32[]{:S(2)}) copy-start(bf16[256,128]{1,0:T(8,128)(2,1)} %copy-done.10) | copy-start | bytes 196612
  103.8 29.5 %copy-start.15 = (bf16[256,128]{1,0:T(8,128)(2,1)S(1)}, bf16[256,128]{1,0:T(8,128)(2,1)}, u32[]{:S(2)}) copy-start(bf16[256,128]{1,0:T(8,128)(2,1)} %copy-done.13) | copy-start | bytes 196612
  103.8 29.5 %copy-start.18 = (bf16[256,128]{1,0:T(8,128)(2,1)S(1)}, bf16[256,128]{1,0:T(8,128)(2,1)}, u32[]{:S(2)}) copy-start(bf16[256,128]{1,0:T(8,128)(2,1)} %copy-done.16) | copy-start | bytes 196612
  103.8 29.5 %copy-start.21 = (bf16[256,128]{1,0:T(8,128)(2,1)S(1)}, bf16[256,128]{1,0:T(8,128)(2,1)}, u32[]{:S(2)}) copy-start(bf16[256,128]{1,0:T(8,128)(2,1)} %copy-done.19) | copy-start | bytes 196612
  103.8 6.4 %collective-permute-start.25 = (bf16[1024,128]{1,0:T(8,128)(2,1)S(1)}, bf16[1024,128]{1,0:T(8,128)(2,1)S(1)}, u32[]{:S(2)}, u32[]{:S(2)}) collective-permute-start(bf16[1024,128]{1,0:T(8,128)(2,1)S(1)} %fusion.4.refs_8_), channel_id=1, source_target_pairs={{0,6},{1,49},{2,0},{3,51},{4,2},{5,53},{6,4},{7,55},{8,14},{9,57},... | collective-permute-start | bytes 786440 | tf_op jit(solution)/shard_map/ppermute | solution.py:43
  104.6 8.0 %collective-permute-start.24 = (bf16[1024,128]{1,0:T(8,128)(2,1)S(1)}, bf16[1024,128]{1,0:T(8,128)(2,1)S(1)}, u32[]{:S(2)}, u32[]{:S(2)}) collective-permute-start(bf16[1024,128]{1,0:T(8,128)(2,1)S(1)} %fusion.4.refs_8_), channel_id=1, source_target_pairs={{0,4},{1,33},{2,6},{3,35},{4,0},{5,37},{6,2},{7,39},{8,12},{9,41},... | collective-permute-start | bytes 786440 | tf_op jit(solution)/shard_map/ppermute | solution.py:43
  105.3 10.0 %collective-permute-start.23 = (bf16[1024,128]{1,0:T(8,128)(2,1)S(1)}, bf16[1024,128]{1,0:T(8,128)(2,1)S(1)}, u32[]{:S(2)}, u32[]{:S(2)}) collective-permute-start(bf16[1024,128]{1,0:T(8,128)(2,1)S(1)} %fusion.4.refs_8_), channel_id=1, source_target_pairs={{0,2},{1,17},{2,4},{3,19},{4,6},{5,21},{6,0},{7,23},{8,10},{9,25},... | collective-permute-start | bytes 786440 | tf_op jit(solution)/shard_map/ppermute | solution.py:43
  121.7 20.7 %copy-start = (f32[512,1024]{1,0:T(8,128)S(1)}, f32[512,1024]{1,0:T(8,128)}, u32[]{:S(2)}) copy-start(f32[512,1024]{1,0:T(8,128)} %get-tuple-element.104.slope) | copy-start | bytes 6291460
  121.8 20.7 %copy-start.2 = (bf16[1024,256]{1,0:T(8,128)(2,1)S(1)}, bf16[1024,256]{1,0:T(8,128)(2,1)}, u32[]{:S(2)}) copy-start(bf16[1024,256]{1,0:T(8,128)(2,1)} %w_second.3) | copy-start | bytes 1572868
  121.8 20.7 %copy-start.9 = (s32[2]{0:T(128)S(1)}, s32[2]{0:T(128)}, u32[]{:S(2)}) copy-start(s32[2]{0:T(128)} %copy-done.8) | copy-start | bytes 28
  121.8 10.7 %collective-permute-start.26 = (bf16[1024,128]{1,0:T(8,128)(2,1)S(1)}, bf16[1024,128]{1,0:T(8,128)(2,1)S(1)}, u32[]{:S(2)}, u32[]{:S(2)}) collective-permute-start(bf16[1024,128]{1,0:T(8,128)(2,1)S(1)} %get-tuple-element.99), channel_id=1, source_target_pairs={{0,16},{1,3},{2,18},{3,5},{4,20},{5,7},{6,22},{7,1},{8,24},{9,11},... | collective-permute-start | bytes 786440 | tf_op jit(solution)/shard_map/ppermute | solution.py:43
  124.3 8.1 %collective-permute-start.27 = (bf16[1024,128]{1,0:T(8,128)(2,1)S(1)}, bf16[1024,128]{1,0:T(8,128)(2,1)S(1)}, u32[]{:S(2)}, u32[]{:S(2)}) collective-permute-start(bf16[1024,128]{1,0:T(8,128)(2,1)S(1)} %get-tuple-element.100), channel_id=1, source_target_pairs={{0,32},{1,5},{2,34},{3,7},{4,36},{5,1},{6,38},{7,3},{8,40},{9,13},... | collective-permute-start | bytes 786440 | tf_op jit(solution)/shard_map/ppermute | solution.py:43
  125.1 8.2 %collective-permute-start.28 = (bf16[1024,128]{1,0:T(8,128)(2,1)S(1)}, bf16[1024,128]{1,0:T(8,128)(2,1)S(1)}, u32[]{:S(2)}, u32[]{:S(2)}) collective-permute-start(bf16[1024,128]{1,0:T(8,128)(2,1)S(1)} %get-tuple-element.101), channel_id=1, source_target_pairs={{0,48},{1,7},{2,50},{3,1},{4,52},{5,3},{6,54},{7,5},{8,56},{9,15},... | collective-permute-start | bytes 786440 | tf_op jit(solution)/shard_map/ppermute | solution.py:43
  133.7 6.2 %collective-permute-start.31 = (bf16[256,128]{1,0:T(8,128)(2,1)S(1)}, bf16[256,128]{1,0:T(8,128)(2,1)S(1)}, u32[]{:S(2)}, u32[]{:S(2)}) collective-permute-start(bf16[256,128]{1,0:T(8,128)(2,1)S(1)} %get-tuple-element.118), channel_id=1, source_target_pairs={{0,64},{1,65},{2,66},{3,67},{4,68},{5,69},{6,70},{7,71},{8,72},{9,... | collective-permute-start | bytes 196616 | tf_op jit(solution)/shard_map/ppermute | solution.py:43
  133.8 6.2 %collective-permute-start.30 = (bf16[256,128]{1,0:T(8,128)(2,1)S(1)}, bf16[256,128]{1,0:T(8,128)(2,1)S(1)}, u32[]{:S(2)}, u32[]{:S(2)}) collective-permute-start(bf16[256,128]{1,0:T(8,128)(2,1)S(1)} %get-tuple-element.119), channel_id=1, source_target_pairs={{0,8},{1,9},{2,10},{3,11},{4,12},{5,13},{6,14},{7,15},{8,0},{9,1},... | collective-permute-start | bytes 196616 | tf_op jit(solution)/shard_map/ppermute | solution.py:43
  135.0 5.8 %collective-permute-start.29 = (bf16[256,128]{1,0:T(8,128)(2,1)S(1)}, bf16[256,128]{1,0:T(8,128)(2,1)S(1)}, u32[]{:S(2)}, u32[]{:S(2)}) collective-permute-start(bf16[256,128]{1,0:T(8,128)(2,1)S(1)} %get-tuple-element.120), channel_id=1, source_target_pairs={{0,72},{1,73},{2,74},{3,75},{4,76},{5,77},{6,78},{7,79},{8,64},{9,... | collective-permute-start | bytes 196616 | tf_op jit(solution)/shard_map/ppermute | solution.py:43
  140.8 1.6 collective-permute-start.32
  (12 other events, 42.6 us)

commit v6 on v5

--- a/solution.py
+++ b/solution.py
@@ -285,21 +285,20 @@
     place = jnp.stack([core, spot])
     start = start_pieces(place, message, other, w_first, w_second)
     tile = pack_rows(block_values[0, 0]).reshape(SLOTS * PACK, LANES)
-    own_swapped = send(tile, core_move)
-    start, own_swapped = lax.optimization_barrier((start, own_swapped))
     start = [start[0]] + [send(start[hop], functools.partial(z_move, hop)) for hop in (1, 2, 3)]
     ahead = send(tile, functools.partial(z_move, 1))
     behind = send(tile, functools.partial(z_move, 3))
     start, ahead, behind = lax.optimization_barrier((start, ahead, behind))
     far = jnp.where(core == 0, ahead, behind)
-    far, start = lax.optimization_barrier((far, start))
+    far, start, near = lax.optimization_barrier((far, start, tile))
     across = send(far, relay_move)
+    own_swapped = send(near, core_move)
     state = jnp.concatenate([piece[:ITEMS] for piece in start])
     tables = jnp.stack([piece[ITEMS : ITEMS + PACK : 16] for piece in start]).astype(jnp.int32)
     tables = tables.transpose(1, 0, 2).reshape(TILES, LANES)
     meta = slot_tables(tables[:, :33], tables[:, 33:113], zl, y, zh, x, core)
     first_parts = [state] + [send(state, functools.partial(gather_ring, hop)) for hop in (1, 2, 3)]
-    first_parts, across, meta = lax.optimization_barrier((first_parts, across, meta))
+    first_parts, across, meta, own_swapped = lax.optimization_barrier((first_parts, across, meta, own_swapped))
     same_core = [tile, ahead, across, behind]
     tiles = same_core + [own_swapped] + [send(piece, core_move) for piece in same_core[1:]]
 

time: 174 us -> 173 us (level)
  waiting for transfers between devices: 49.3 us -> 54.4 us
  starting transfers between devices: 40.5 us -> 38 us
  local copies, waits for them, and re-layouts: 14.8 us -> 12.9 us
    ppermute x33, waiting for transfers between devices: 49.3 us -> 54.4 us  [send(): return lax.ppermute(value, AXES, permutation(move))]
    ppermute x33, starting transfers between devices: 40.5 us -> 38 us  [send(): return lax.ppermute(value, AXES, permutation(move))]
  transfers between devices with their start and end apart: 33 -> 33, of which waited for: 20 -> 19; matrix products, arithmetic and copies ran while one was open for 12% -> 12% of each run, Pallas kernels for 1% -> 1%
where the time goes in v6:
time: 173 us; the launch traced here: 172 us
  waiting for transfers between devices  54.4 us (31%)
  starting transfers between devices  38 us (22%)
  blocking collectives  26.7 us (15%)
  Pallas kernels  23.2 us (13%)
  other arithmetic  13.3 us (8%)
  local copies, waits for them, and re-layouts  12.9 us (7%)
  matrix products  2.68 us (2%)
    ppermute x33, waiting for transfers between devices, send(): return lax.ppermute(value, AXES, permutation(move))  54.4 us
    ppermute x33, starting transfers between devices, send(): return lax.ppermute(value, AXES, permutation(move))  38 us
    pallas_call x3, Pallas kernels, block_product(): pl.pallas_call(product_kernel, out_shape=(piece,) * 4, in_specs=[pl.Block...  19.5 us
    all_to_all x1, blocking collectives, body(): landed = lax.all_to_all(spread, ('zl', 'zh', 'x'), 0, 0)  16 us
    all_to_all x1, blocking collectives, body(): lax.all_to_all(jnp.broadcast_to(mine[None], (8, 128, 128)), LOOP, 0, 0)  10.7 us
  transfers between devices with their start and end apart: 33, of which 19 were waited for; matrix products, arithmetic and copies ran while one was open for 12% of the time, Pallas kernels for 1%

profile of v6, /device:TPU:0, one launch (start us, length us, event | category | flops | bytes accessed | tf_op | source)
XLA Modules:
  0.0 172.4 jit_solution(1746223461651255623)
XLA Ops:
  0.6 1.3 fusion.65
  3.0 4.2 %collective-permute-start.5 = (bf16[2560,128]{1,0:T(8,128)(2,1)S(1)}, bf16[2560,128]{1,0:T(8,128)(2,1)S(1)}, u32[]{:S(2)}, u32[]{:S(2)}) collective-permute-start(bf16[2560,128]{1,0:T(8,128)(2,1)S(1)} %bitcast.57), channel_id=1, source_target_pairs={{0,72},{1,73},{2,74},{3,75},{4,76},{5,77},{6,78},{7,79},{8,64},{9,... | collective-permute-start | bytes 1966088 | tf_op jit(solution)/shard_map/ppermute | solution.py:43
  7.3 1.0 pad_maximum_fusion.1.own
  9.9 1.6 start_pieces.1
  11.5 3.3 %collective-permute-start.3 = (bf16[288,128]{1,0:T(8,128)(2,1)S(1)}, bf16[288,128]{1,0:T(8,128)(2,1)S(1)}, u32[]{:S(2)}, u32[]{:S(2)}) collective-permute-start(bf16[288,128]{1,0:T(8,128)(2,1)S(1)} %get-tuple-element.113), channel_id=1, source_target_pairs={{0,72},{1,73},{2,74},{3,75},{4,76},{5,77},{6,78},{7,79},{8,64},{9,... | collective-permute-start | bytes 221192 | tf_op jit(solution)/shard_map/ppermute | solution.py:43
  14.8 0.9 collective-permute-start.1
  16.3 8.0 %collective-permute-done.3 = bf16[288,128]{1,0:T(8,128)(2,1)S(1)} collective-permute-done((bf16[288,128]{1,0:T(8,128)(2,1)S(1)}, bf16[288,128]{1,0:T(8,128)(2,1)S(1)}, u32[]{:S(2)}, u32[]{:S(2)}) %collective-permute-start.3) | collective-permute-done | bytes 73760 | tf_op jit(solution)/shard_map/ppermute | solution.py:43
  24.3 1.4 collective-permute-done.2
  25.7 2.1 %collective-permute-done.1 = bf16[288,128]{1,0:T(8,128)(2,1)S(1)} collective-permute-done((bf16[288,128]{1,0:T(8,128)(2,1)S(1)}, bf16[288,128]{1,0:T(8,128)(2,1)S(1)}, u32[]{:S(2)}, u32[]{:S(2)}) %collective-permute-start.1) | collective-permute-done | bytes 73760 | tf_op jit(solution)/shard_map/ppermute | solution.py:43
  29.1 2.8 %collective-permute-start.8 = (bf16[1024,128]{1,0:T(8,128)(2,1)S(1)}, bf16[1024,128]{1,0:T(8,128)(2,1)}, u32[]{:S(2)}, u32[]{:S(2)}) collective-permute-start(bf16[1024,128]{1,0:T(8,128)(2,1)S(1)} %pad_maximum_fusion.2.refs_8_), channel_id=1, source_target_pairs={{0,6},{1,49},{2,0},{3,51},{4,2},{5,53},{6,4},{7,55},{8,14},{9,57},... | collective-permute-start | bytes 786440 | tf_op jit(solution)/shard_map/ppermute | solution.py:43
  36.3 1.4 fusion.23
  40.1 2.0 %compare_select_fusion.1 = (s32[1,704]{1,0:T(1,128)S(1)}, s32[1,704]{1,0:T(1,128)S(1)}) fusion(s32[]{:T(128)} %axis_index.52, s32[]{:T(128)} %bitcast.19, s32[]{:T(128)} %bitcast.18, s32[704]{0:T(1024)S(1)} %get-tuple-element.108, s32[704]{0:T(1024)} %get-tuple-element.126), kind=kLoop, calls=%fused_computation.47 | loop fusion | flops 6336 | bytes 11276 | tf_op jit(solution)/shard_map/jit(_where)/select_n | solution.py:256
  43.3 3.8 %collective-permute-done.9.refs_2_ = bf16[2560,128]{1,0:T(8,128)(2,1)S(1)} collective-permute-done((bf16[2560,128]{1,0:T(8,128)(2,1)}, bf16[2560,128]{1,0:T(8,128)(2,1)S(1)}, u32[]{:S(2)}, u32[]{:S(2)}) %collective-permute-start.9) | collective-permute-done | bytes 655392 | tf_op jit(solution)/shard_map/ppermute | solution.py:43
  47.1 2.2 %collective-permute-done.12.refs_6_ = bf16[2560,128]{1,0:T(8,128)(2,1)} collective-permute-done((bf16[2560,128]{1,0:T(8,128)(2,1)S(1)}, bf16[2560,128]{1,0:T(8,128)(2,1)}, u32[]{:S(2)}, u32[]{:S(2)}) %collective-permute-start.12) | collective-permute-done | bytes 655392 | tf_op jit(solution)/shard_map/ppermute | solution.py:43
  50.0 6.7 %block_product.3 = (bf16[1024,128]{1,0:T(8,128)(2,1)S(1)}, bf16[1024,128]{1,0:T(8,128)(2,1)S(1)}, bf16[1024,128]{1,0:T(8,128)(2,1)S(1)}, bf16[1024,128]{1,0:T(8,128)(2,1)S(1)}) custom-call(s32[4,704]{1,0:T(4,128)S(1)} %copy-done.7, bf16[2,32,128]{2,1,0:T(8,128)(2,1)S(1)} %broadcast_in_dim.66.masks, bf16[2560,128]{1,0:T(8,128)(2,1)S(1)} %bitcast.60, ...), custom_call_target="tpu_custom_call" | custom-call | tf_op jit(solution)/shard_map/block_product/pallas_call | solution.py:150
  56.7 1.7 collective-permute-start.14
  58.4 2.9 %collective-permute-start.15 = (bf16[1024,128]{1,0:T(8,128)(2,1)S(1)}, bf16[1024,128]{1,0:T(8,128)(2,1)S(1)}, u32[]{:S(2)}, u32[]{:S(2)}) collective-permute-start(bf16[1024,128]{1,0:T(8,128)(2,1)S(1)} %get-tuple-element.80), channel_id=1, source_target_pairs={{0,32},{1,5},{2,34},{3,7},{4,36},{5,1},{6,38},{7,3},{8,40},{9,13},... | collective-permute-start | bytes 786440 | tf_op jit(solution)/shard_map/ppermute | solution.py:43
  61.8 2.7 %multiply_convert_fusion = (bf16[512,1024]{1,0:T(8,128)(2,1)}, f32[512,1024]{1,0:T(8,128)}) fusion(bf16[512,256]{1,0:T(8,128)(2,1)S(1)} %bitcast.68, bf16[256,1024]{1,0:T(8,128)(2,1)S(1)} %copy-done.5), kind=kOutput, calls=%fused_computation | convolution fusion | flops 273154048 | bytes 3932160 | tf_op jit(solution)/shard_map/dot_general | solution.py:317
  64.5 3.9 %collective-permute-done.15 = bf16[1024,128]{1,0:T(8,128)(2,1)S(1)} collective-permute-done((bf16[1024,128]{1,0:T(8,128)(2,1)S(1)}, bf16[1024,128]{1,0:T(8,128)(2,1)S(1)}, u32[]{:S(2)}, u32[]{:S(2)}) %collective-permute-start.15) | collective-permute-done | bytes 262176 | tf_op jit(solution)/shard_map/ppermute | solution.py:43
  68.6 2.9 %collective-permute-start.19 = (bf16[1024,128]{1,0:T(8,128)(2,1)S(1)}, bf16[1024,128]{1,0:T(8,128)(2,1)S(1)}, u32[]{:S(2)}, u32[]{:S(2)}) collective-permute-start(bf16[1024,128]{1,0:T(8,128)(2,1)S(1)} %fusion.3.refs_8_), channel_id=1, source_target_pairs={{0,6},{1,49},{2,0},{3,51},{4,2},{5,53},{6,4},{7,55},{8,14},{9,57},... | collective-permute-start | bytes 786440 | tf_op jit(solution)/shard_map/ppermute | solution.py:43
  71.8 1.0 collective-permute-start.17
  72.8 5.5 %collective-permute-done.19.refs_11_ = bf16[1024,128]{1,0:T(8,128)(2,1)S(1)} collective-permute-done((bf16[1024,128]{1,0:T(8,128)(2,1)S(1)}, bf16[1024,128]{1,0:T(8,128)(2,1)S(1)}, u32[]{:S(2)}, u32[]{:S(2)}) %collective-permute-start.19) | collective-permute-done | bytes 262176 | tf_op jit(solution)/shard_map/ppermute | solution.py:43
  78.2 1.2 collective-permute-done.18.refs_10_
  79.5 2.7 %collective-permute-done.17.refs_9_ = bf16[1024,128]{1,0:T(8,128)(2,1)S(1)} collective-permute-done((bf16[1024,128]{1,0:T(8,128)(2,1)S(1)}, bf16[1024,128]{1,0:T(8,128)(2,1)S(1)}, u32[]{:S(2)}, u32[]{:S(2)}) %collective-permute-start.17) | collective-permute-done | bytes 262176 | tf_op jit(solution)/shard_map/ppermute | solution.py:43
  82.2 6.8 %block_product.4 = (bf16[1024,128]{1,0:T(8,128)(2,1)S(1)}, bf16[1024,128]{1,0:T(8,128)(2,1)}, bf16[1024,128]{1,0:T(8,128)(2,1)}, bf16[1024,128]{1,0:T(8,128)(2,1)}) custom-call(s32[4,704]{1,0:T(4,128)S(1)} %copy-done.7, bf16[2,32,128]{2,1,0:T(8,128)(2,1)S(1)} %broadcast_in_dim.66.masks, bf16[2560,128]{1,0:T(8,128)(2,1)S(1)} %bitcast.61, ...), custom_call_target="tpu_custom_call" | custom-call | tf_op jit(solution)/shard_map/block_product/pallas_call | solution.py:150
  89.7 1.6 collective-permute-start.20
  91.3 3.0 %collective-permute-start.21 = (bf16[1024,128]{1,0:T(8,128)(2,1)}, bf16[1024,128]{1,0:T(8,128)(2,1)}, u32[]{:S(2)}, u32[]{:S(2)}) collective-permute-start(bf16[1024,128]{1,0:T(8,128)(2,1)} %get-tuple-element.93), channel_id=1, source_target_pairs={{0,32},{1,5},{2,34},{3,7},{4,36},{5,1},{6,38},{7,3},{8,40},{9,13},... | collective-permute-start | bytes 786440 | tf_op jit(solution)/shard_map/ppermute | solution.py:43
  94.3 1.8 %copy.30 = bf16[512,256]{0,1:T(8,128)(2,1)} copy(bf16[512,256]{1,0:T(8,128)(2,1)} %bitcast.69) | data formatting | bytes 524288 | tf_op jit(solution)/shard_map/optimization_barrier | solution.py:321
  96.2 2.3 %copy.31 = bf16[1024,512]{1,0:T(8,128)(2,1)} copy(bf16[1024,512]{0,1:T(8,128)(2,1)} %bitcast.71) | data formatting | bytes 2097152 | tf_op jit(solution)/shard_map/transpose | solution.py:323
  99.4 1.1 constant_dynamic-slice_fusion
  100.5 1.3 collective-permute-done.21
  101.8 1.5 fusion.4.refs_8_
  103.3 1.0 collective-permute-start.25
  104.7 1.2 collective-permute-start.23
  105.9 3.9 %collective-permute-done.25.refs_11_ = bf16[1024,128]{1,0:T(8,128)(2,1)S(1)} collective-permute-done((bf16[1024,128]{1,0:T(8,128)(2,1)S(1)}, bf16[1024,128]{1,0:T(8,128)(2,1)S(1)}, u32[]{:S(2)}, u32[]{:S(2)}) %collective-permute-start.25) | collective-permute-done | bytes 262176 | tf_op jit(solution)/shard_map/ppermute | solution.py:43
  109.7 2.6 %collective-permute-done.24.refs_10_ = bf16[1024,128]{1,0:T(8,128)(2,1)S(1)} collective-permute-done((bf16[1024,128]{1,0:T(8,128)(2,1)S(1)}, bf16[1024,128]{1,0:T(8,128)(2,1)S(1)}, u32[]{:S(2)}, u32[]{:S(2)}) %collective-permute-start.24) | collective-permute-done | bytes 262176 | tf_op jit(solution)/shard_map/ppermute | solution.py:43
  112.3 2.7 %collective-permute-done.23.refs_9_ = bf16[1024,128]{1,0:T(8,128)(2,1)S(1)} collective-permute-done((bf16[1024,128]{1,0:T(8,128)(2,1)S(1)}, bf16[1024,128]{1,0:T(8,128)(2,1)S(1)}, u32[]{:S(2)}, u32[]{:S(2)}) %collective-permute-start.23) | collective-permute-done | bytes 262176 | tf_op jit(solution)/shard_map/ppermute | solution.py:43
  115.0 6.0 %block_product.5 = (bf16[1024,128]{1,0:T(8,128)(2,1)S(1)}, bf16[1024,128]{1,0:T(8,128)(2,1)S(1)}, bf16[1024,128]{1,0:T(8,128)(2,1)S(1)}, bf16[1024,128]{1,0:T(8,128)(2,1)S(1)}) custom-call(s32[4,704]{1,0:T(4,128)S(1)} %copy-done.8, bf16[2,32,128]{2,1,0:T(8,128)(2,1)S(1)} %broadcast_in_dim.66.masks, bf16[2560,128]{1,0:T(8,128)(2,1)S(1)} %bitcast.62, ...), custom_call_target="tpu_custom_call" | custom-call | tf_op jit(solution)/shard_map/block_product/pallas_call | solution.py:150
  121.1 1.2 collective-permute-start.26
  122.2 3.5 %collective-permute-start.27 = (bf16[1024,128]{1,0:T(8,128)(2,1)S(1)}, bf16[1024,128]{1,0:T(8,128)(2,1)S(1)}, u32[]{:S(2)}, u32[]{:S(2)}) collective-permute-start(bf16[1024,128]{1,0:T(8,128)(2,1)S(1)} %get-tuple-element.100), channel_id=1, source_target_pairs={{0,32},{1,5},{2,34},{3,7},{4,36},{5,1},{6,38},{7,3},{8,40},{9,13},... | collective-permute-start | bytes 786440 | tf_op jit(solution)/shard_map/ppermute | solution.py:43
  125.7 3.2 %collective-permute-done.26 = bf16[1024,128]{1,0:T(8,128)(2,1)S(1)} collective-permute-done((bf16[1024,128]{1,0:T(8,128)(2,1)S(1)}, bf16[1024,128]{1,0:T(8,128)(2,1)S(1)}, u32[]{:S(2)}, u32[]{:S(2)}) %collective-permute-start.26) | collective-permute-done | bytes 262176 | tf_op jit(solution)/shard_map/ppermute | solution.py:43
  128.9 3.9 %collective-permute-done.27 = bf16[1024,128]{1,0:T(8,128)(2,1)S(1)} collective-permute-done((bf16[1024,128]{1,0:T(8,128)(2,1)S(1)}, bf16[1024,128]{1,0:T(8,128)(2,1)S(1)}, u32[]{:S(2)}, u32[]{:S(2)}) %collective-permute-start.27) | collective-permute-done | bytes 262176 | tf_op jit(solution)/shard_map/ppermute | solution.py:43
  133.4 2.3 %collective-permute-start.30 = (bf16[256,128]{1,0:T(8,128)(2,1)S(1)}, bf16[256,128]{1,0:T(8,128)(2,1)S(1)}, u32[]{:S(2)}, u32[]{:S(2)}) collective-permute-start(bf16[256,128]{1,0:T(8,128)(2,1)S(1)} %get-tuple-element.119), channel_id=1, source_target_pairs={{0,8},{1,9},{2,10},{3,11},{4,12},{5,13},{6,14},{7,15},{8,0},{9,1},... | collective-permute-start | bytes 196616 | tf_op jit(solution)/shard_map/ppermute | solution.py:43
  136.6 2.9 %collective-permute-done.31 = bf16[256,128]{1,0:T(8,128)(2,1)S(1)} collective-permute-done((bf16[256,128]{1,0:T(8,128)(2,1)S(1)}, bf16[256,128]{1,0:T(8,128)(2,1)S(1)}, u32[]{:S(2)}, u32[]{:S(2)}) %collective-permute-start.31) | collective-permute-done | bytes 65568 | tf_op jit(solution)/shard_map/ppermute | solution.py:43
  140.5 1.5 collective-permute-done.32.other
  142.0 2.1 %finish.1 = (bf16[2048,128]{1,0:T(8,128)(2,1)S(1)}, bf16[256,256]{1,0:T(8,128)(2,1)}) custom-call(s32[2]{0:T(128)S(1)} %copy-done.10, bf16[4,256,128]{2,1,0:T(8,128)(2,1)S(1)} %pad_maximum_fusion.3.own, bf16[4,256,128]{2,1,0:T(8,128)(2,1)S(1)} %collective-permute-done.32.other, bf16[128,512]{1,0:T(8,128)(2,1)S(1)} %bitcast.65, ...), custom_call_target="tpu_custom_call" | custom-call | tf_op jit(solution)/shard_map/finish/pallas_call | solution.py:209
  144.1 16.0 %all_to_all.10 = bf16[16,128,128]{2,1,0:T(8,128)(2,1)S(1)} all-to-all(bf16[16,128,128]{2,1,0:T(8,128)(2,1)S(1)} %bitcast.66), channel_id=1, replica_groups=mesh['zl'=2,'y'=4,'zh'=2,'x'=4,'c'=2] {'zl','zh','x'}, dimensions={0} | all-to-all | bytes 1048576 | tf_op jit(solution)/shard_map/all_to_all | solution.py:341
  160.2 10.7 %all_to_all.11 = bf16[8,128,128]{2,1,0:T(8,128)(2,1)S(1)} all-to-all(bf16[8,128,128]{2,1,0:T(8,128)(2,1)S(1)} %broadcast_in_dim.68), channel_id=1, replica_groups=mesh['zl'=2,'y'=4,'zh'=2,'x'=4,'c'=2] {'zl','y'}, dimensions={0} | all-to-all | bytes 524288 | tf_op jit(solution)/shard_map/all_to_all | solution.py:343
  (140 shorter events, 20.2 us)
Async XLA Ops:
  1.9 8.0 %copy-start.1 = (bf16[1024,256]{1,0:T(8,128)(2,1)S(1)}, bf16[1024,256]{1,0:T(8,128)(2,1)}, u32[]{:S(2)}) copy-start(bf16[1024,256]{1,0:T(8,128)(2,1)} %w_second.3) | copy-start | bytes 1572868
  1.9 7.9 %copy-start.4 = (bf16[256,1024]{1,0:T(8,128)(2,1)S(1)}, bf16[256,1024]{1,0:T(8,128)(2,1)}, u32[]{:S(2)}) copy-start(bf16[256,1024]{1,0:T(8,128)(2,1)} %w_first.1) | copy-start | bytes 1572868
  3.0 24.8 %collective-permute-start.5 = (bf16[2560,128]{1,0:T(8,128)(2,1)S(1)}, bf16[2560,128]{1,0:T(8,128)(2,1)S(1)}, u32[]{:S(2)}, u32[]{:S(2)}) collective-permute-start(bf16[2560,128]{1,0:T(8,128)(2,1)S(1)} %bitcast.57), channel_id=1, source_target_pairs={{0,72},{1,73},{2,74},{3,75},{4,76},{5,77},{6,78},{7,79},{8,64},{9,... | collective-permute-start | bytes 1966088 | tf_op jit(solution)/shard_map/ppermute | solution.py:43
  7.2 20.6 %collective-permute-start.4 = (bf16[2560,128]{1,0:T(8,128)(2,1)S(1)}, bf16[2560,128]{1,0:T(8,128)(2,1)S(1)}, u32[]{:S(2)}, u32[]{:S(2)}) collective-permute-start(bf16[2560,128]{1,0:T(8,128)(2,1)S(1)} %bitcast.58), channel_id=1, source_target_pairs={{0,64},{1,65},{2,66},{3,67},{4,68},{5,69},{6,70},{7,71},{8,72},{9,... | collective-permute-start | bytes 1966088 | tf_op jit(solution)/shard_map/ppermute | solution.py:43
  8.3 1.6 collective-permute-start
  8.4 19.3 %copy-start.9 = (s32[2]{0:T(128)}, s32[2]{0:T(128)S(1)}, u32[]{:S(2)}) copy-start(s32[2]{0:T(128)S(1)} %pad_add_fusion.1.place) | copy-start | bytes 28
  9.9 18.8 %copy-start.3 = (bf16[528,256]{1,0:T(8,128)(2,1)}, bf16[528,256]{1,0:T(8,128)(2,1)S(1)}, u32[]{:S(2)}) copy-start(bf16[528,256]{1,0:T(8,128)(2,1)S(1)} %collective-permute-done.other) | copy-start | bytes 811012
  11.5 12.8 %collective-permute-start.3 = (bf16[288,128]{1,0:T(8,128)(2,1)S(1)}, bf16[288,128]{1,0:T(8,128)(2,1)S(1)}, u32[]{:S(2)}, u32[]{:S(2)}) collective-permute-start(bf16[288,128]{1,0:T(8,128)(2,1)S(1)} %get-tuple-element.113), channel_id=1, source_target_pairs={{0,72},{1,73},{2,74},{3,75},{4,76},{5,77},{6,78},{7,79},{8,64},{9,... | collective-permute-start | bytes 221192 | tf_op jit(solution)/shard_map/ppermute | solution.py:43
  14.8 10.8 %collective-permute-start.2 = (bf16[288,128]{1,0:T(8,128)(2,1)S(1)}, bf16[288,128]{1,0:T(8,128)(2,1)S(1)}, u32[]{:S(2)}, u32[]{:S(2)}) collective-permute-start(bf16[288,128]{1,0:T(8,128)(2,1)S(1)} %get-tuple-element.114), channel_id=1, source_target_pairs={{0,8},{1,9},{2,10},{3,11},{4,12},{5,13},{6,14},{7,15},{8,0},{9,1},... | collective-permute-start | bytes 221192 | tf_op jit(solution)/shard_map/ppermute | solution.py:43
  14.8 12.9 %collective-permute-start.1 = (bf16[288,128]{1,0:T(8,128)(2,1)S(1)}, bf16[288,128]{1,0:T(8,128)(2,1)S(1)}, u32[]{:S(2)}, u32[]{:S(2)}) collective-permute-start(bf16[288,128]{1,0:T(8,128)(2,1)S(1)} %get-tuple-element.115), channel_id=1, source_target_pairs={{0,64},{1,65},{2,66},{3,67},{4,68},{5,69},{6,70},{7,71},{8,72},{9,... | collective-permute-start | bytes 221192 | tf_op jit(solution)/shard_map/ppermute | solution.py:43
  29.1 13.5 %collective-permute-start.8 = (bf16[1024,128]{1,0:T(8,128)(2,1)S(1)}, bf16[1024,128]{1,0:T(8,128)(2,1)}, u32[]{:S(2)}, u32[]{:S(2)}) collective-permute-start(bf16[1024,128]{1,0:T(8,128)(2,1)S(1)} %pad_maximum_fusion.2.refs_8_), channel_id=1, source_target_pairs={{0,6},{1,49},{2,0},{3,51},{4,2},{5,53},{6,4},{7,55},{8,14},{9,57},... | collective-permute-start | bytes 786440 | tf_op jit(solution)/shard_map/ppermute | solution.py:43
  32.0 11.2 %collective-permute-start.7 = (bf16[1024,128]{1,0:T(8,128)(2,1)S(1)}, bf16[1024,128]{1,0:T(8,128)(2,1)}, u32[]{:S(2)}, u32[]{:S(2)}) collective-permute-start(bf16[1024,128]{1,0:T(8,128)(2,1)S(1)} %pad_maximum_fusion.2.refs_8_), channel_id=1, source_target_pairs={{0,4},{1,33},{2,6},{3,35},{4,0},{5,37},{6,2},{7,39},{8,12},{9,41},... | collective-permute-start | bytes 786440 | tf_op jit(solution)/shard_map/ppermute | solution.py:43
  32.8 10.5 %collective-permute-start.6 = (bf16[1024,128]{1,0:T(8,128)(2,1)S(1)}, bf16[1024,128]{1,0:T(8,128)(2,1)}, u32[]{:S(2)}, u32[]{:S(2)}) collective-permute-start(bf16[1024,128]{1,0:T(8,128)(2,1)S(1)} %pad_maximum_fusion.2.refs_8_), channel_id=1, source_target_pairs={{0,2},{1,17},{2,4},{3,19},{4,6},{5,21},{6,0},{7,23},{8,10},{9,25},... | collective-permute-start | bytes 786440 | tf_op jit(solution)/shard_map/ppermute | solution.py:43
  35.0 12.0 %collective-permute-start.9 = (bf16[2560,128]{1,0:T(8,128)(2,1)}, bf16[2560,128]{1,0:T(8,128)(2,1)S(1)}, u32[]{:S(2)}, u32[]{:S(2)}) collective-permute-start(bf16[2560,128]{1,0:T(8,128)(2,1)} %broadcast_select_fusion), channel_id=1, source_target_pairs={{0,64},{1,73},{2,66},{3,75},{4,68},{5,77},{6,70},{7,79},{8,72},{9,... | collective-permute-start | bytes 1966088 | tf_op jit(solution)/shard_map/ppermute | solution.py:43
  35.0 12.0 %collective-permute-start.10 = (bf16[2560,128]{1,0:T(8,128)(2,1)S(1)}, bf16[2560,128]{1,0:T(8,128)(2,1)S(1)}, u32[]{:S(2)}, u32[]{:S(2)}) collective-permute-start(bf16[2560,128]{1,0:T(8,128)(2,1)S(1)} %bitcast.59), channel_id=1, source_target_pairs={{0,1},{1,0},{2,3},{3,2},{4,5},{5,4},{6,7},{7,6},{8,9},{9,8},{10,11... | collective-permute-start | bytes 1966088 | tf_op jit(solution)/shard_map/ppermute | solution.py:43
  42.7 4.4 %collective-permute-start.11 = (bf16[2560,128]{1,0:T(8,128)(2,1)S(1)}, bf16[2560,128]{1,0:T(8,128)(2,1)}, u32[]{:S(2)}, u32[]{:S(2)}) collective-permute-start(bf16[2560,128]{1,0:T(8,128)(2,1)S(1)} %collective-permute-done.4.refs_1_), channel_id=1, source_target_pairs={{0,1},{1,0},{2,3},{3,2},{4,5},{5,4},{6,7},{7,6},{8,9},{9,8},{10,11... | collective-permute-start | bytes 1966088 | tf_op jit(solution)/shard_map/ppermute | solution.py:43
  43.2 3.9 %collective-permute-start.13 = (bf16[2560,128]{1,0:T(8,128)(2,1)S(1)}, bf16[2560,128]{1,0:T(8,128)(2,1)}, u32[]{:S(2)}, u32[]{:S(2)}) collective-permute-start(bf16[2560,128]{1,0:T(8,128)(2,1)S(1)} %collective-permute-done.5.refs_3_), channel_id=1, source_target_pairs={{0,1},{1,0},{2,3},{3,2},{4,5},{5,4},{6,7},{7,6},{8,9},{9,8},{10,11... | collective-permute-start | bytes 1966088 | tf_op jit(solution)/shard_map/ppermute | solution.py:43
  47.0 2.2 %collective-permute-start.12 = (bf16[2560,128]{1,0:T(8,128)(2,1)S(1)}, bf16[2560,128]{1,0:T(8,128)(2,1)}, u32[]{:S(2)}, u32[]{:S(2)}) collective-permute-start(bf16[2560,128]{1,0:T(8,128)(2,1)S(1)} %collective-permute-done.9.refs_2_), channel_id=1, source_target_pairs={{0,1},{1,0},{2,3},{3,2},{4,5},{5,4},{6,7},{7,6},{8,9},{9,8},{10,11... | collective-permute-start | bytes 1966088 | tf_op jit(solution)/shard_map/ppermute | solution.py:43
  50.0 11.7 %slice-start = ((bf16[528,256]{1,0:T(8,128)(2,1)}), bf16[256,256]{1,0:T(8,128)(2,1)S(1)}, s32[]{:S(2)}) async-start(bf16[528,256]{1,0:T(8,128)(2,1)} %copy-done.3), calls=%async_computation.2 | async-start | bytes 262144 | tf_op jit(solution)/shard_map/slice | solution.py:315
  50.0 11.7 %copy-start.24 = (bf16[1,256,256]{2,1,0:T(8,128)(2,1)S(1)}, bf16[1,256,256]{2,1,0:T(8,128)(2,1)}, u32[]{:S(2)}) copy-start(bf16[1,256,256]{2,1,0:T(8,128)(2,1)} %param.7) | copy-start | bytes 393220
  50.0 11.8 %copy-start.5 = (bf16[256,1024]{1,0:T(8,128)(2,1)S(1)}, bf16[256,1024]{1,0:T(8,128)(2,1)}, u32[]{:S(2)}) copy-start(bf16[256,1024]{1,0:T(8,128)(2,1)} %w_first.1) | copy-start | bytes 1572868
  56.7 7.8 %collective-permute-start.14 = (bf16[1024,128]{1,0:T(8,128)(2,1)S(1)}, bf16[1024,128]{1,0:T(8,128)(2,1)S(1)}, u32[]{:S(2)}, u32[]{:S(2)}) collective-permute-start(bf16[1024,128]{1,0:T(8,128)(2,1)S(1)} %get-tuple-element.79), channel_id=1, source_target_pairs={{0,16},{1,3},{2,18},{3,5},{4,20},{5,7},{6,22},{7,1},{8,24},{9,11},... | collective-permute-start | bytes 786440 | tf_op jit(solution)/shard_map/ppermute | solution.py:43
  58.4 10.0 %collective-permute-start.15 = (bf16[1024,128]{1,0:T(8,128)(2,1)S(1)}, bf16[1024,128]{1,0:T(8,128)(2,1)S(1)}, u32[]{:S(2)}, u32[]{:S(2)}) collective-permute-start(bf16[1024,128]{1,0:T(8,128)(2,1)S(1)} %get-tuple-element.80), channel_id=1, source_target_pairs={{0,32},{1,5},{2,34},{3,7},{4,36},{5,1},{6,38},{7,3},{8,40},{9,13},... | collective-permute-start | bytes 786440 | tf_op jit(solution)/shard_map/ppermute | solution.py:43
  61.2 7.2 %collective-permute-start.16 = (bf16[1024,128]{1,0:T(8,128)(2,1)S(1)}, bf16[1024,128]{1,0:T(8,128)(2,1)S(1)}, u32[]{:S(2)}, u32[]{:S(2)}) collective-permute-start(bf16[1024,128]{1,0:T(8,128)(2,1)S(1)} %get-tuple-element.81), channel_id=1, source_target_pairs={{0,48},{1,7},{2,50},{3,1},{4,52},{5,3},{6,54},{7,5},{8,56},{9,15},... | collective-permute-start | bytes 786440 | tf_op jit(solution)/shard_map/ppermute | solution.py:43
  68.6 9.6 %collective-permute-start.19 = (bf16[1024,128]{1,0:T(8,128)(2,1)S(1)}, bf16[1024,128]{1,0:T(8,128)(2,1)S(1)}, u32[]{:S(2)}, u32[]{:S(2)}) collective-permute-start(bf16[1024,128]{1,0:T(8,128)(2,1)S(1)} %fusion.3.refs_8_), channel_id=1, source_target_pairs={{0,6},{1,49},{2,0},{3,51},{4,2},{5,53},{6,4},{7,55},{8,14},{9,57},... | collective-permute-start | bytes 786440 | tf_op jit(solution)/shard_map/ppermute | solution.py:43
  71.5 8.0 %collective-permute-start.18 = (bf16[1024,128]{1,0:T(8,128)(2,1)S(1)}, bf16[1024,128]{1,0:T(8,128)(2,1)S(1)}, u32[]{:S(2)}, u32[]{:S(2)}) collective-permute-start(bf16[1024,128]{1,0:T(8,128)(2,1)S(1)} %fusion.3.refs_8_), channel_id=1, source_target_pairs={{0,4},{1,33},{2,6},{3,35},{4,0},{5,37},{6,2},{7,39},{8,12},{9,41},... | collective-permute-start | bytes 786440 | tf_op jit(solution)/shard_map/ppermute | solution.py:43
  71.8 10.4 %collective-permute-start.17 = (bf16[1024,128]{1,0:T(8,128)(2,1)S(1)}, bf16[1024,128]{1,0:T(8,128)(2,1)S(1)}, u32[]{:S(2)}, u32[]{:S(2)}) collective-permute-start(bf16[1024,128]{1,0:T(8,128)(2,1)S(1)} %fusion.3.refs_8_), channel_id=1, source_target_pairs={{0,2},{1,17},{2,4},{3,19},{4,6},{5,21},{6,0},{7,23},{8,10},{9,25},... | collective-permute-start | bytes 786440 | tf_op jit(solution)/shard_map/ppermute | solution.py:43
  89.7 10.7 %collective-permute-start.20 = (bf16[1024,128]{1,0:T(8,128)(2,1)}, bf16[1024,128]{1,0:T(8,128)(2,1)}, u32[]{:S(2)}, u32[]{:S(2)}) collective-permute-start(bf16[1024,128]{1,0:T(8,128)(2,1)} %get-tuple-element.92), channel_id=1, source_target_pairs={{0,16},{1,3},{2,18},{3,5},{4,20},{5,7},{6,22},{7,1},{8,24},{9,11},... | collective-permute-start | bytes 786440 | tf_op jit(solution)/shard_map/ppermute | solution.py:43
  91.3 10.5 %collective-permute-start.21 = (bf16[1024,128]{1,0:T(8,128)(2,1)}, bf16[1024,128]{1,0:T(8,128)(2,1)}, u32[]{:S(2)}, u32[]{:S(2)}) collective-permute-start(bf16[1024,128]{1,0:T(8,128)(2,1)} %get-tuple-element.93), channel_id=1, source_target_pairs={{0,32},{1,5},{2,34},{3,7},{4,36},{5,1},{6,38},{7,3},{8,40},{9,13},... | collective-permute-start | bytes 786440 | tf_op jit(solution)/shard_map/ppermute | solution.py:43
  94.3 7.5 %collective-permute-start.22 = (bf16[1024,128]{1,0:T(8,128)(2,1)}, bf16[1024,128]{1,0:T(8,128)(2,1)}, u32[]{:S(2)}, u32[]{:S(2)}) collective-permute-start(bf16[1024,128]{1,0:T(8,128)(2,1)} %get-tuple-element.94), channel_id=1, source_target_pairs={{0,48},{1,7},{2,50},{3,1},{4,52},{5,3},{6,54},{7,5},{8,56},{9,15},... | collective-permute-start | bytes 786440 | tf_op jit(solution)/shard_map/ppermute | solution.py:43
  98.4 16.6 %copy-start.8 = (s32[4,704]{1,0:T(4,128)S(1)}, s32[4,704]{1,0:T(4,128)}, u32[]{:S(2)}) copy-start(s32[4,704]{1,0:T(4,128)} %pad_add_fusion.meta) | copy-start | bytes 33796
  103.3 29.6 %copy-start.13 = (bf16[256,128]{1,0:T(8,128)(2,1)S(1)}, bf16[256,128]{1,0:T(8,128)(2,1)}, u32[]{:S(2)}) copy-start(bf16[256,128]{1,0:T(8,128)(2,1)} %copy-done.11) | copy-start | bytes 196612
  103.3 29.6 %copy-start.16 = (bf16[256,128]{1,0:T(8,128)(2,1)S(1)}, bf16[256,128]{1,0:T(8,128)(2,1)}, u32[]{:S(2)}) copy-start(bf16[256,128]{1,0:T(8,128)(2,1)} %copy-done.14) | copy-start | bytes 196612
  103.3 29.6 %copy-start.19 = (bf16[256,128]{1,0:T(8,128)(2,1)S(1)}, bf16[256,128]{1,0:T(8,128)(2,1)}, u32[]{:S(2)}) copy-start(bf16[256,128]{1,0:T(8,128)(2,1)} %copy-done.17) | copy-start | bytes 196612
  103.3 29.6 %copy-start.22 = (bf16[256,128]{1,0:T(8,128)(2,1)S(1)}, bf16[256,128]{1,0:T(8,128)(2,1)}, u32[]{:S(2)}) copy-start(bf16[256,128]{1,0:T(8,128)(2,1)} %copy-done.20) | copy-start | bytes 196612
  103.3 6.4 %collective-permute-start.25 = (bf16[1024,128]{1,0:T(8,128)(2,1)S(1)}, bf16[1024,128]{1,0:T(8,128)(2,1)S(1)}, u32[]{:S(2)}, u32[]{:S(2)}) collective-permute-start(bf16[1024,128]{1,0:T(8,128)(2,1)S(1)} %fusion.4.refs_8_), channel_id=1, source_target_pairs={{0,6},{1,49},{2,0},{3,51},{4,2},{5,53},{6,4},{7,55},{8,14},{9,57},... | collective-permute-start | bytes 786440 | tf_op jit(solution)/shard_map/ppermute | solution.py:43
  104.3 8.0 %collective-permute-start.24 = (bf16[1024,128]{1,0:T(8,128)(2,1)S(1)}, bf16[1024,128]{1,0:T(8,128)(2,1)S(1)}, u32[]{:S(2)}, u32[]{:S(2)}) collective-permute-start(bf16[1024,128]{1,0:T(8,128)(2,1)S(1)} %fusion.4.refs_8_), channel_id=1, source_target_pairs={{0,4},{1,33},{2,6},{3,35},{4,0},{5,37},{6,2},{7,39},{8,12},{9,41},... | collective-permute-start | bytes 786440 | tf_op jit(solution)/shard_map/ppermute | solution.py:43
  104.7 10.4 %collective-permute-start.23 = (bf16[1024,128]{1,0:T(8,128)(2,1)S(1)}, bf16[1024,128]{1,0:T(8,128)(2,1)S(1)}, u32[]{:S(2)}, u32[]{:S(2)}) collective-permute-start(bf16[1024,128]{1,0:T(8,128)(2,1)S(1)} %fusion.4.refs_8_), channel_id=1, source_target_pairs={{0,2},{1,17},{2,4},{3,19},{4,6},{5,21},{6,0},{7,23},{8,10},{9,25},... | collective-permute-start | bytes 786440 | tf_op jit(solution)/shard_map/ppermute | solution.py:43
  121.0 21.0 %copy-start = (f32[512,1024]{1,0:T(8,128)S(1)}, f32[512,1024]{1,0:T(8,128)}, u32[]{:S(2)}) copy-start(f32[512,1024]{1,0:T(8,128)} %get-tuple-element.104.slope) | copy-start | bytes 6291460
  121.0 21.0 %copy-start.2 = (bf16[1024,256]{1,0:T(8,128)(2,1)S(1)}, bf16[1024,256]{1,0:T(8,128)(2,1)}, u32[]{:S(2)}) copy-start(bf16[1024,256]{1,0:T(8,128)(2,1)} %w_second.3) | copy-start | bytes 1572868
  121.0 21.0 %copy-start.10 = (s32[2]{0:T(128)S(1)}, s32[2]{0:T(128)}, u32[]{:S(2)}) copy-start(s32[2]{0:T(128)} %copy-done.9) | copy-start | bytes 28
  121.1 7.9 %collective-permute-start.26 = (bf16[1024,128]{1,0:T(8,128)(2,1)S(1)}, bf16[1024,128]{1,0:T(8,128)(2,1)S(1)}, u32[]{:S(2)}, u32[]{:S(2)}) collective-permute-start(bf16[1024,128]{1,0:T(8,128)(2,1)S(1)} %get-tuple-element.99), channel_id=1, source_target_pairs={{0,16},{1,3},{2,18},{3,5},{4,20},{5,7},{6,22},{7,1},{8,24},{9,11},... | collective-permute-start | bytes 786440 | tf_op jit(solution)/shard_map/ppermute | solution.py:43
  122.2 10.6 %collective-permute-start.27 = (bf16[1024,128]{1,0:T(8,128)(2,1)S(1)}, bf16[1024,128]{1,0:T(8,128)(2,1)S(1)}, u32[]{:S(2)}, u32[]{:S(2)}) collective-permute-start(bf16[1024,128]{1,0:T(8,128)(2,1)S(1)} %get-tuple-element.100), channel_id=1, source_target_pairs={{0,32},{1,5},{2,34},{3,7},{4,36},{5,1},{6,38},{7,3},{8,40},{9,13},... | collective-permute-start | bytes 786440 | tf_op jit(solution)/shard_map/ppermute | solution.py:43
  125.7 7.2 %collective-permute-start.28 = (bf16[1024,128]{1,0:T(8,128)(2,1)S(1)}, bf16[1024,128]{1,0:T(8,128)(2,1)S(1)}, u32[]{:S(2)}, u32[]{:S(2)}) collective-permute-start(bf16[1024,128]{1,0:T(8,128)(2,1)S(1)} %get-tuple-element.101), channel_id=1, source_target_pairs={{0,48},{1,7},{2,50},{3,1},{4,52},{5,3},{6,54},{7,5},{8,56},{9,15},... | collective-permute-start | bytes 786440 | tf_op jit(solution)/shard_map/ppermute | solution.py:43
  133.3 6.2 %collective-permute-start.31 = (bf16[256,128]{1,0:T(8,128)(2,1)S(1)}, bf16[256,128]{1,0:T(8,128)(2,1)S(1)}, u32[]{:S(2)}, u32[]{:S(2)}) collective-permute-start(bf16[256,128]{1,0:T(8,128)(2,1)S(1)} %get-tuple-element.118), channel_id=1, source_target_pairs={{0,64},{1,65},{2,66},{3,67},{4,68},{5,69},{6,70},{7,71},{8,72},{9,... | collective-permute-start | bytes 196616 | tf_op jit(solution)/shard_map/ppermute | solution.py:43
  133.4 6.2 %collective-permute-start.30 = (bf16[256,128]{1,0:T(8,128)(2,1)S(1)}, bf16[256,128]{1,0:T(8,128)(2,1)S(1)}, u32[]{:S(2)}, u32[]{:S(2)}) collective-permute-start(bf16[256,128]{1,0:T(8,128)(2,1)S(1)} %get-tuple-element.119), channel_id=1, source_target_pairs={{0,8},{1,9},{2,10},{3,11},{4,12},{5,13},{6,14},{7,15},{8,0},{9,1},... | collective-permute-start | bytes 196616 | tf_op jit(solution)/shard_map/ppermute | solution.py:43
  135.7 4.7 %collective-permute-start.29 = (bf16[256,128]{1,0:T(8,128)(2,1)S(1)}, bf16[256,128]{1,0:T(8,128)(2,1)S(1)}, u32[]{:S(2)}, u32[]{:S(2)}) collective-permute-start(bf16[256,128]{1,0:T(8,128)(2,1)S(1)} %get-tuple-element.120), channel_id=1, source_target_pairs={{0,72},{1,73},{2,74},{3,75},{4,76},{5,77},{6,78},{7,79},{8,64},{9,... | collective-permute-start | bytes 196616 | tf_op jit(solution)/shard_map/ppermute | solution.py:43
  140.4 1.6 collective-permute-start.32
  (13 other events, 63.7 us)
